TPU v7x, 32 devices: a whole 2x2x4 slice. The times are simulated.
32 devices in a mesh: track: 4 (over y, x), tm: 8 (over z, core).
Axes of the slice: x: 2, y: 2, z: 4, core: 2. Of those that a mesh axis runs over, the one named last changes fastest.
Arguments:
- observations: float32 [1024, 16, 128], P('tm', 'track'), may hold values from -18 to 18
- dynamics: bfloat16 [256, 128, 128], P('track'), may hold values from -1 to 1
- smoother_gain: bfloat16 [256, 128, 128], P('track'), may hold values from -1 to 1
- gains: bfloat16 [256, 128], P('track'), may hold values from 0 to 1
- regime: int32 [256], P('tm'), may hold values from 0 to 255
Outputs:
- smoothed: float32 [1024, 16, 128], P('tm', 'track')
All inputs are finite; a program needn't handle non-finite values.
Results may differ from a plain program's by a relative error of at most 0.0003.
Values may be sent and summed in bfloat16 or wider, within the bound.
No kernel may reach another device: no remote copies, remote signals or barrier semaphores. Data moves between devices by JAX's collectives and lax.ppermute only.
A program may use at most 64 MiB of HBM per device.

v0:
```python
import jax
import jax.numpy as jnp
import numpy as np
from jax import lax
from jax.sharding import PartitionSpec as P


def prefix(shard, axis, combine, identity, reverse):
    peers, position = (lax.axis_size(axis), lax.axis_index(axis))
    everything = jax.tree.map(lambda part: lax.all_gather(part, axis), shard)
    start = jax.tree.map(
        lambda part, zero: jnp.broadcast_to(jnp.asarray(zero, part.dtype), part.shape),
        shard,
        identity,
    )

    def step(k, before):
        at = peers - 1 - k if reverse else k
        reached = at > position if reverse else at < position
        new = combine(before, jax.tree.map(lambda part: part[at], everything))
        return jax.tree.map(lambda a, b: jnp.where(reached, a, b), new, before)

    return lax.fori_loop(0, peers, step, start)


def from_root(shard, axis, root):
    mine = lax.axis_index(axis) == root
    return lax.psum(jnp.where(mine, shard, jnp.zeros_like(shard)), axis)


def shifted(value, axis, steps):
    count = lax.axis_size(axis)
    initial, last = (max(0, -steps), min(count, count - steps))
    return lax.ppermute(value, axis, [(source, source + steps) for source in range(initial, last)])


def matmul(left, right):
    return jnp.dot(left, right, precision=lax.Precision.HIGHEST)


def compose(earlier, later):
    return (matmul(earlier[0], later[0]), matmul(earlier[1], later[0]) + later[1])


def carried_forward(pair):
    width = pair[0].shape[0]
    identity_pair = (jnp.eye(width, dtype=jnp.float32), jnp.zeros_like(pair[1]))
    return prefix(pair, "tm", compose, identity_pair, False)[1]


def carried_backward(pair):
    width = pair[0].shape[0]
    identity_pair = (jnp.eye(width, dtype=jnp.float32), jnp.zeros_like(pair[1]))
    return prefix(pair, "tm", compose, identity_pair, True)[1]


def spread_forward(pair):
    width = pair[0].shape[0]
    identity_pair = (jnp.eye(width, dtype=jnp.float32), jnp.zeros_like(pair[1]))
    within = prefix(pair, "track", compose, identity_pair, False)
    through = compose(within, pair)
    joined = jnp.concatenate([through[0], through[1]], axis=0)
    total = from_root(joined, "track", lax.axis_size("track") - 1)
    earlier = carried_forward((total[:width], total[width:]))
    return matmul(earlier, within[0]) + within[1]


def spread_backward(pair):
    width = pair[0].shape[0]
    identity_pair = (jnp.eye(width, dtype=jnp.float32), jnp.zeros_like(pair[1]))
    within = prefix(pair, "track", compose, identity_pair, True)
    through = compose(within, pair)
    joined = jnp.concatenate([through[0], through[1]], axis=0)
    total = from_root(joined, "track", 0)
    later = carried_backward((total[:width], total[width:]))
    return matmul(later, within[0]) + within[1]


def pick_rows(block_ids, dynamics, smoother_gain, gains):
    owned = dynamics.shape[0]
    width = dynamics.shape[1]
    offset = lax.axis_index("track") * owned
    selector = (block_ids[:, None] - offset == jnp.arange(owned, dtype=jnp.int32)[None, :]).astype(
        jnp.bfloat16
    )
    pick_dyn = jnp.dot(
        selector, dynamics.reshape(owned, width * width), preferred_element_type=jnp.float32
    )
    pick_smooth = jnp.dot(
        selector, smoother_gain.reshape(owned, width * width), preferred_element_type=jnp.float32
    )
    pick_gain = jnp.dot(selector, gains, preferred_element_type=jnp.float32)
    return (pick_dyn, pick_smooth, pick_gain)


def local_map(carry, inputs):
    matrix, vector = inputs
    return ((matmul(carry[0], matrix), matmul(carry[1], matrix) + vector), None)


def propagate(state, inputs):
    matrix, vector = inputs
    state = matmul(state, matrix) + vector
    return (state, state)


def retreat(state, inputs):
    matrix, vector = inputs
    state = vector + matmul(state, matrix)
    return (state, state)


def smooth_span(picked, measured, dwell, finishing, forward_carry, backward_carry):
    pick_dyn, pick_smooth, pick_gain = picked
    length, tracks, width = measured.shape
    count = pick_gain.shape[0]
    step_dyn = jnp.repeat(pick_dyn.reshape(count, width, width), dwell, axis=0)
    step_smooth = jnp.repeat(pick_smooth.reshape(count, width, width), dwell, axis=0)
    step_gain = jnp.repeat(pick_gain, dwell, axis=0)[:length]
    current = step_dyn[:length]
    upcoming = step_dyn[1 : length + 1]
    final_row = jnp.arange(length) == length - 1
    live = jnp.where(jnp.logical_and(finishing, final_row), 0.0, 1.0).astype(jnp.float32)
    next_gain = step_smooth[1 : length + 1] * live[:, None, None]
    closed = jnp.swapaxes(current, 1, 2) * (1.0 - step_gain)[:, None, :]
    driven = step_gain[:, None, :] * measured
    empty_vec = jnp.zeros((tracks, width), jnp.float32)
    unit_mat = jnp.eye(width, dtype=jnp.float32)
    filter_pair, _ = lax.scan(local_map, (unit_mat, empty_vec), (closed, driven))
    before = forward_carry(filter_pair)
    _, filtered = lax.scan(propagate, before, (closed, driven))
    cross = jnp.einsum("tij,tjk->tik", next_gain, upcoming, precision=lax.Precision.HIGHEST)
    innovation = filtered - jnp.einsum(
        "tbj,tij->tbi", filtered, cross, precision=lax.Precision.HIGHEST
    )
    gain_rows = jnp.swapaxes(next_gain, 1, 2)
    smooth_pair, _ = lax.scan(
        local_map, (unit_mat, empty_vec), (gain_rows, innovation), reverse=True
    )
    after = backward_carry(smooth_pair)
    _, smoothed = lax.scan(retreat, after, (gain_rows, innovation), reverse=True)
    return smoothed


def body(observations, dynamics, smoother_gain, gains, regime):
    length = observations.shape[0]
    blocks = regime.shape[0]
    dwell = length // blocks
    following = shifted(regime[:1], "tm", -1)
    block_ids = jnp.concatenate([regime, following])
    on_last = lax.axis_index("tm") == lax.axis_size("tm") - 1
    groups = lax.axis_size("track")
    share = blocks // groups
    place = lax.axis_index("track")
    order = (np.arange(groups)[:, None] * share + np.arange(share + 1)[None, :]).reshape(-1)
    spread_ids = block_ids[order]
    picked = pick_rows(spread_ids, dynamics, smoother_gain, gains)
    picked = (
        lax.psum_scatter(
            picked[0].astype(jnp.bfloat16), "track", scatter_dimension=0, tiled=True
        ).astype(jnp.float32),
        lax.psum_scatter(
            picked[1].astype(jnp.bfloat16), "track", scatter_dimension=0, tiled=True
        ).astype(jnp.float32),
        lax.psum_scatter(
            picked[2].astype(jnp.bfloat16), "track", scatter_dimension=0, tiled=True
        ).astype(jnp.float32),
    )
    measured = lax.all_to_all(observations, "track", split_axis=0, concat_axis=1, tiled=True)
    finishing = jnp.logical_and(on_last, place == groups - 1)
    smoothed = smooth_span(picked, measured, dwell, finishing, spread_forward, spread_backward)
    return lax.all_to_all(smoothed, "track", split_axis=1, concat_axis=0, tiled=True)


def solution(mesh):
    placed = (
        P("tm", "track", None),
        P("track", None, None),
        P("track", None, None),
        P("track", None),
        P("tm"),
    )
    return jax.shard_map(
        body, mesh=mesh, in_specs=placed, out_specs=P("tm", "track", None), check_vma=False
    )
```

profile of v0, /device:TPU:0, one launch (start us, length us, event | category | flops | bytes accessed | tf_op | source)
XLA Modules:
  0.0 525.0 jit_solution(3427825557945967753)
XLA Ops:
  12.0 4.2 convolution_convert_fusion
  16.2 2.6 convolution_convert_fusion.1
  18.9 5.2 all-to-all-start
  25.6 17.5 %all-reduce.2 = bf16[36,128]{1,0:T(8,128)(2,1)S(1)} all-reduce(bf16[36,128]{1,0:T(8,128)(2,1)S(1)} %convolution_convert_fusion.2), channel_id=12, replica_groups=mesh['track'=4,'tm'=8] {'track'}, use_global_device_ids=true, to_apply=%region_2.0.clone | all-reduce | flops 4608 | bytes 18432
  43.2 58.4 %all-reduce.12.cloned.1.call-done = (bf16[36,16384]{1,0:T(8,128)(2,1)}, bf16[36,16384]{1,0:T(8,128)(2,1)}) async-done(((bf16[36,16384]{1,0:T(8,128)(2,1)}, bf16[36,16384]{1,0:T(8,128)(2,1)}), (bf16[36,16384]{1,0:T(8,128)(2,1)}, bf16[36,16384]{1,0:T(8,128)(2,1)})) %all-reduce.12.cloned.1.call-update) | async-done | bytes 2359312
  106.8 70.1 %while.124 = (s32[]{:T(128)}, f32[128,128]{0,1:T(8,128)S(1)}, f32[16,128]{1,0:T(8,128)S(1)}, f32[32,128,128]{2,1,0:T(8,128)}, f32[32,16,128]{2,1,0:T(8,128)S(1)}, /*index=5*/s32[]{:T(128)}, s32[]{:T(128)}) while((s32[]{:T(128)}, f32[128,128]{0,1:T(8,128)S(1)}, f32[16,128]{1,0:T(8,128)S(1)}, f32[32,128,128]{2,1,0:T(8,128)}, ...), condition=%wide.region_4.5_spmd.clone, body=%wide.region_3.4_spmd.clone.sunk | while | flops 28315648 | bytes 435799 | solution.py:129
  177.0 10.0 %all-gather = f32[512,128]{0,1:T(8,128)S(1)} all-gather(f32[128,128]{0,1:T(8,128)S(1)} %get-tuple-element.758), channel_id=2, replica_groups=mesh['track'=4,'tm'=8] {'track'}, dimensions={0}, use_global_device_ids=true | all-gather | bytes 327680 | tf_op jit(solution)/shard_map/all_gather | solution.py:10
  187.1 7.2 %all-gather.1 = f32[64,128]{1,0:T(8,128)S(1)} all-gather(f32[16,128]{1,0:T(8,128)S(1)} %get-tuple-element.759), channel_id=3, replica_groups=mesh['track'=4,'tm'=8] {'track'}, dimensions={0}, use_global_device_ids=true | all-gather | bytes 40960 | tf_op jit(solution)/shard_map/all_gather | solution.py:10
  194.3 2.1 while.125
  199.0 3.6 fusion.78
  204.1 34.3 %all-reduce.8.cloned.1.call-done = f32[144,128]{1,0:T(8,128)} async-done(((f32[144,128]{1,0:T(8,128)}), f32[144,128]{1,0:T(8,128)}) %all-reduce.8.cloned.1.call-update) | async-done | bytes 73744 | tf_op jit(solution)/shard_map/psum | solution.py:28
  239.3 14.7 %all-gather.2 = f32[1024,128]{1,0:T(8,128)S(1)} all-gather(f32[128,128]{1,0:T(8,128)S(1)} %slice.58), channel_id=4, replica_groups=mesh['track'=4,'tm'=8] {'tm'}, dimensions={0}, use_global_device_ids=true | all-gather | bytes 589824 | tf_op jit(solution)/shard_map/all_gather | solution.py:10
  254.7 14.3 %all-gather.3 = f32[128,128]{1,0:T(8,128)S(1)} all-gather(f32[16,128]{1,0:T(8,128)S(1)} %slice.59), channel_id=5, replica_groups=mesh['track'=4,'tm'=8] {'tm'}, dimensions={0}, use_global_device_ids=true | all-gather | bytes 73728 | tf_op jit(solution)/shard_map/all_gather | solution.py:10
  270.7 32.9 %while.122 = (s32[]{:T(128)}, f32[16,128]{1,0:T(8,128)S(1)}, f32[32,16,128]{2,1,0:T(8,128)S(1)}, f32[32,128,128]{2,1,0:T(8,128)}, f32[32,16,128]{2,1,0:T(8,128)}, /*index=5*/s32[]{:T(128)}) while((s32[]{:T(128)}, f32[16,128]{1,0:T(8,128)S(1)}, f32[32,16,128]{2,1,0:T(8,128)S(1)}, f32[32,128,128]{2,1,0:T(8,128)}, f32[32,16,128]{2,1,0:T(8,128)}, ...), condition=%wide.region_11.12_spmd, body=%wide.region_10.11_spmd.sunk | while | flops 3147778 | bytes 115781 | solution.py:131
  303.6 3.4 convolution_subtract_fusion
  307.0 70.2 %while.127 = (s32[]{:T(128)}, f32[128,128]{0,1:T(8,128)S(1)}, f32[16,128]{1,0:T(8,128)S(1)}, f32[32,128,128]{2,1,0:T(8,128)}, f32[32,16,128]{2,1,0:T(8,128)S(1)}, /*index=5*/s32[]{:T(128)}, s32[]{:T(128)}, s32[]{:T(128)}) while((s32[]{:T(128)}, f32[128,128]{0,1:T(8,128)S(1)}, f32[16,128]{1,0:T(8,128)S(1)}, ...), condition=%wide.region_13.14_spmd.clone, body=%wide.region_12.13_spmd.clone.sunk | while | flops 28315652 | bytes 435822 | solution.py:137
  377.2 10.7 %all-gather.4 = f32[512,128]{0,1:T(8,128)S(1)} all-gather(f32[128,128]{0,1:T(8,128)S(1)} %get-tuple-element.764), channel_id=6, replica_groups=mesh['track'=4,'tm'=8] {'track'}, dimensions={0}, use_global_device_ids=true | all-gather | bytes 327680 | tf_op jit(solution)/shard_map/all_gather | solution.py:10
  388.1 8.1 %all-gather.5 = f32[64,128]{1,0:T(8,128)S(1)} all-gather(f32[16,128]{1,0:T(8,128)S(1)} %get-tuple-element.765), channel_id=7, replica_groups=mesh['track'=4,'tm'=8] {'track'}, dimensions={0}, use_global_device_ids=true | all-gather | bytes 40960 | tf_op jit(solution)/shard_map/all_gather | solution.py:10
  396.2 2.1 while.128
  399.5 40.9 %all-reduce.10.cloned.1.call-done = f32[144,128]{1,0:T(8,128)} async-done(((f32[144,128]{1,0:T(8,128)}), f32[144,128]{1,0:T(8,128)}) %all-reduce.10.cloned.1.call-update) | async-done | bytes 73744 | tf_op jit(solution)/shard_map/psum | solution.py:28
  441.3 14.7 %all-gather.6 = f32[1024,128]{1,0:T(8,128)S(1)} all-gather(f32[128,128]{1,0:T(8,128)S(1)} %slice.61), channel_id=8, replica_groups=mesh['track'=4,'tm'=8] {'tm'}, dimensions={0}, use_global_device_ids=true | all-gather | bytes 589824 | tf_op jit(solution)/shard_map/all_gather | solution.py:10
  456.7 14.0 %all-gather.7 = f32[128,128]{1,0:T(8,128)S(1)} all-gather(f32[16,128]{1,0:T(8,128)S(1)} %slice.62), channel_id=9, replica_groups=mesh['track'=4,'tm'=8] {'tm'}, dimensions={0}, use_global_device_ids=true | all-gather | bytes 73728 | tf_op jit(solution)/shard_map/all_gather | solution.py:10
  472.4 35.0 %while.123 = (s32[]{:T(128)}, f32[16,128]{1,0:T(8,128)S(1)}, f32[32,16,128]{2,0,1:T(8,128)S(1)}, f32[32,16,128]{2,1,0:T(8,128)S(1)}, f32[32,128,128]{2,1,0:T(8,128)}, /*index=5*/s32[]{:T(128)}, s32[]{:T(128)}, s32[]{:T(128)}) while((s32[]{:T(128)}, f32[16,128]{1,0:T(8,128)S(1)}, f32[32,16,128]{2,0,1:T(8,128)S(1)}, ...), condition=%wide.region_20.21_spmd, body=%wide.region_19.20_spmd.sunk | while | flops 3147779 | bytes 124005 | solution.py:141
  507.4 10.1 %all_to_all.36 = f32[32,16,128]{2,0,1:T(8,128)S(1)} all-to-all(f32[32,16,128]{2,0,1:T(8,128)S(1)} %get-tuple-element.769), channel_id=1, replica_groups=mesh['track'=4,'tm'=8] {'track'}, dimensions={1} | all-to-all | bytes 524288 | tf_op jit(solution)/shard_map/all_to_all | solution.py:172
  (559 shorter events, 235.4 us)
Async XLA Ops:
  6.5 18.8 %copy-start = (bf16[64,128]{1,0:T(8,128)(2,1)S(1)}, bf16[64,128]{1,0:T(8,128)(2,1)}, u32[]{:S(2)}) copy-start(bf16[64,128]{1,0:T(8,128)(2,1)} %param.26) | copy-start | bytes 49156
  6.5 9.7 %copy-start.6 = (bf16[64,128,128]{2,1,0:T(8,128)(2,1)S(1)}, bf16[64,128,128]{2,1,0:T(8,128)(2,1)}, u32[]{:S(2)}) copy-start(bf16[64,128,128]{2,1,0:T(8,128)(2,1)} %param.25) | copy-start | bytes 6291460
  6.5 95.0 %all-reduce.12.cloned.1.call-start = ((), (), s32[]{:S(2)}) async-start(), calls=%async_computation.4 | async-start | bytes 5242880
  6.5 3.3 collective-permute-start
  18.9 5.3 %copy-start.9 = (u32[32]{0:T(128)S(1)}, u32[32]{0:T(128)}, u32[]{:S(2)}) copy-start(u32[32]{0:T(128)} %constant.255) | copy-start | bytes 388
  18.9 24.2 %all-to-all-start = ((f32[128,4,128]{2,1,0:T(4,128)}), f32[128,4,128]{2,1,0:T(4,128)S(1)}, u32[]{:S(2)}, u32[]{:S(2)}) async-start(f32[128,4,128]{2,1,0:T(4,128)} %param.23), calls=%async_computation | async-start | bytes 524288 | tf_op jit(solution)/shard_map/all_to_all | solution.py:169
  24.1 214.4 %all-reduce.8.cloned.1.call-start = ((), (), s32[]{:S(2)}) async-start(), calls=%async_computation.2 | async-start | bytes 147456 | tf_op jit(solution)/shard_map/psum | solution.py:28
  24.1 79.0 %copy-start.1 = (f32[128,128]{0,1:T(8,128)}, f32[128,128]{0,1:T(8,128)S(1)}, u32[]{:S(2)}) copy-start(f32[128,128]{0,1:T(8,128)S(1)} %fusion.82) | copy-start | bytes 196612
  104.0 2.8 copy-start.3
  106.8 87.5 %copy-start.4 = (f32[128,128]{0,1:T(8,128)S(1)}, f32[128,128]{0,1:T(8,128)}, u32[]{:S(2)}) copy-start(f32[128,128]{0,1:T(8,128)} %copy-done.1) | copy-start | bytes 196612
  176.9 20.7 %copy-start.7 = (f32[32,16,128]{2,1,0:T(8,128)}, f32[32,16,128]{2,1,0:T(8,128)S(1)}, u32[]{:S(2)}) copy-start(f32[32,16,128]{2,1,0:T(8,128)S(1)} %get-tuple-element.1440) | copy-start | bytes 786436
  197.6 242.8 %all-reduce.10.cloned.1.call-start = ((), (), s32[]{:S(2)}) async-start(), calls=%async_computation.3 | async-start | bytes 147456 | tf_op jit(solution)/shard_map/psum | solution.py:28
  202.6 68.1 %copy-start.8 = (f32[32,16,128]{2,1,0:T(8,128)S(1)}, f32[32,16,128]{2,1,0:T(8,128)}, u32[]{:S(2)}) copy-start(f32[32,16,128]{2,1,0:T(8,128)} %custom-call.8) | copy-start | bytes 786436
  254.7 52.2 %copy-start.5 = (f32[128,128]{0,1:T(8,128)S(1)}, f32[128,128]{0,1:T(8,128)}, u32[]{:S(2)}) copy-start(f32[128,128]{0,1:T(8,128)} %copy-done.1) | copy-start | bytes 196612
  307.0 89.2 %copy-start.2 = (f32[128,128]{0,1:T(8,128)S(1)}, f32[128,128]{0,1:T(8,128)}, u32[]{:S(2)}) copy-start(f32[128,128]{0,1:T(8,128)} %copy-done.1) | copy-start | bytes 196612
Sparse Core Ops, SparseCore 0:
  19.0 82.4 all-reduce.11
  197.7 40.6 all-reduce.7
  399.6 40.7 all-reduce.9
where the time goes:
time: 535 us; the launch traced here: 525 us
  matrix products  223 us (42%)
  waiting for transfers between devices  135 us (25%)
  blocking collectives  121 us (23%)
  between operations  14.1 us (3%)
  local copies, waits for them, and re-layouts  12.8 us (2%)
  other arithmetic  8.16 us (2%)
  starting transfers between devices  6.66 us (1%)
    dot_general x230, matrix products, matmul(): return jnp.dot(left, right, precision=lax.Precision.HIGHEST)  208 us
    all_gather x8, blocking collectives, prefix(): everything = jax.tree.map(lambda part: lax.all_gather(part, axis), shard)  93.8 us
    psum x2, waiting for transfers between devices, from_root(): return lax.psum(jnp.where(mine, shard, jnp.zeros_like(shard)), axis)  75.2 us
    unnamed x4, waiting for transfers between devices  58.4 us
    unnamed x1, blocking collectives  17.5 us
  transfers between devices with their start and end apart: 5, of which 4 were waited for; matrix products, arithmetic and copies ran while one was open for 2% of the time, Pallas kernels for 0%

commit v1 on v0

v1 whole, which is shorter than its diff:
```python
import functools

import jax
import jax.numpy as jnp
from jax import lax
from jax.experimental import pallas as pl
from jax.experimental.pallas import tpu as pltpu
from jax.sharding import PartitionSpec as P


F32 = jnp.float32
BF16 = jnp.bfloat16
VMEM = pl.BlockSpec(memory_space=pltpu.VMEM)
SMEM = pl.BlockSpec(memory_space=pltpu.SMEM)
HBM = pl.BlockSpec(memory_space=pltpu.HBM)
STRANDS = 4
GRANT = 16 * 1024 * 1024


def call(kernel, outs, ins, cost, scratch=()):
    return pl.pallas_call(
        kernel,
        out_shape=outs,
        in_specs=ins,
        out_specs=[VMEM] * len(outs),
        scratch_shapes=list(scratch),
        compiler_params=pltpu.CompilerParams(vmem_limit_bytes=GRANT),
        cost_estimate=pl.CostEstimate(flops=cost, bytes_accessed=cost // 64, transcendentals=0),
    )


def shape(dims, dtype=F32):
    return jax.ShapeDtypeStruct(dims, dtype)


def split(value):
    high = value.astype(BF16)
    low = (value - high.astype(F32)).astype(BF16)
    return high, low


def times_rows(value, doubled):
    pieces = jnp.concatenate(split(value), axis=1)
    return lax.dot_general(
        pieces, doubled, (((1,), (1,)), ((), ())), preferred_element_type=F32
    )


def times(value, matrix):
    high, low = split(value)
    upper, lower = split(matrix)
    left = jnp.concatenate([high, low, high], axis=1)
    right = jnp.concatenate([upper, upper, lower], axis=0)
    return jnp.dot(left, right, preferred_element_type=F32)


def compose(first, second):
    width = first.shape[1]
    product = times(first, second[:width])
    return jnp.concatenate([product[:width], product[width:] + second[width:]], axis=0)


def apply(state, chart):
    width = chart.shape[1]
    return times(state, chart[:width]) + chart[width:]


def unit_chart(width, rows):
    unit = (
        lax.broadcasted_iota(jnp.int32, (width, width), 0)
        == lax.broadcasted_iota(jnp.int32, (width, width), 1)
    ).astype(F32)
    return jnp.concatenate([unit, jnp.zeros((rows, width), F32)], axis=0)


def choose(index, options):
    value = options[0]
    for j in range(1, len(options)):
        value = jnp.where(index == j, options[j], value)
    return value


def swapped(rows, mask, groups):
    block = rows.shape[0] // groups
    return jnp.concatenate(
        [rows[(j ^ mask) * block : ((j ^ mask) + 1) * block] for j in range(groups)], axis=0
    )


def doubled(matrix):
    return jnp.concatenate([matrix, matrix], axis=1)


def step_rows(parts, t):
    return jnp.concatenate([part[t] for part in parts], axis=0)


class Plan:
    def __init__(self, groups, share, dwell, owned, tracks, width):
        self.groups, self.share, self.dwell = groups, share, dwell
        self.owned, self.tracks, self.width = owned, tracks, width
        self.span, self.rows = share * dwell, groups * tracks
        self.extra = -(-share // tracks)
        self.per = share // STRANDS
        self.length = self.per * dwell

    def here(self, regime_ref, peer, b):
        local = regime_ref[peer * self.share + b] - lax.axis_index("track") * self.owned
        return jnp.clip(local, 0, self.owned - 1)

    def source(self, regime_ref, b):
        me = lax.axis_index("track")
        return (regime_ref[me * self.share + b] // self.owned) ^ me

    def gain_row(self, regime_ref, meas, b):
        step, row = self.span + b // self.tracks, b % self.tracks
        return choose(
            self.source(regime_ref, b), [part[step][row : row + 1] for part in meas]
        )

    def forward_steps(self):
        for i in range(self.length):
            for s in range(STRANDS):
                b = s * self.per + i // self.dwell
                yield i, s, b, b * self.dwell + i % self.dwell

    def backward_steps(self):
        for i in range(self.length):
            for s in range(STRANDS):
                b = s * self.per + self.per - 1 - i // self.dwell
                yield i, s, b, b * self.dwell + self.dwell - 1 - i % self.dwell


def gather_rows(plan, regime_ref, table_ref, outs, sems):
    for j in range(plan.groups):
        peer = lax.axis_index("track") ^ j
        for b in range(plan.share):
            at = plan.here(regime_ref, peer, b)
            pltpu.make_async_copy(table_ref.at[at], outs[j].at[b], sems.at[j]).start()


def gather_wait(plan, table_ref, outs, sems):
    for j in range(plan.groups):
        rows = table_ref.at[pl.ds(0, plan.share)]
        pltpu.make_async_copy(rows, outs[j], sems.at[j]).wait()


def gather_kernel(plan, regime_ref, table_ref, *refs):
    outs, sems = (refs[: plan.groups], refs[plan.groups])
    gather_rows(plan, regime_ref, table_ref, outs, sems)
    gather_wait(plan, table_ref, outs, sems)


def second_gather_kernel(plan, regime_ref, table_ref, gains_ref, obs_ref, *refs):
    groups, tracks = (plan.groups, plan.tracks)
    mats, meas = (refs[:groups], refs[groups : 2 * groups])
    gain_ref, sems = refs[2 * groups :]
    gather_rows(plan, regime_ref, table_ref, mats, sems)
    gain_ref[...] = gains_ref[...].astype(F32)
    for j in range(groups):
        peer = lax.axis_index("track") ^ j
        first = pl.multiple_of(peer * plan.span, plan.span)
        meas[j][0 : plan.span] = obs_ref[pl.ds(first, plan.span)]
        for e in range(plan.extra):
            blocks = [min(e * tracks + i, plan.share - 1) for i in range(tracks)]
            meas[j][plan.span + e] = jnp.concatenate(
                [gain_ref[pl.ds(plan.here(regime_ref, peer, b), 1), :] for b in blocks], axis=0
            )
    gather_wait(plan, table_ref, mats, sems)


def picked_weights(plan, regime_ref, mats, picked_ref):
    weights = []
    for b in range(plan.share):
        picked = choose(plan.source(regime_ref, b), [part[b] for part in mats])
        picked_ref[b] = picked
        weights.append(doubled(picked))
    return weights


def forward_kernel(plan, regime_ref, *refs):
    groups, width = (plan.groups, plan.width)
    mats, meas = (refs[:groups], refs[groups : 2 * groups])
    total_ref, strand_ref, picked_ref = refs[2 * groups :]
    weights = picked_weights(plan, regime_ref, mats, picked_ref)
    gains = [plan.gain_row(regime_ref, meas, b) for b in range(plan.share)]
    states = [unit_chart(width, plan.rows)] * STRANDS
    for i, s, b, t in plan.forward_steps():
        kept = times_rows(states[s], weights[b]) * (1.0 - gains[b])
        driven = gains[b] * step_rows(meas, t)
        states[s] = jnp.concatenate([kept[:width], kept[width:] + driven], axis=0)
    for s in range(STRANDS):
        strand_ref[s] = states[s]
    while len(states) > 1:
        states = [compose(states[i], states[i + 1]) for i in range(0, len(states), 2)]
    total_ref[...] = states[0]


def backward_kernel(plan, regime_ref, *refs):
    groups, width = (plan.groups, plan.width)
    mats, pushed_ref = (refs[:groups], refs[groups])
    total_ref, strand_ref, picked_ref = refs[groups + 1 :]
    weights = picked_weights(plan, regime_ref, mats, picked_ref)
    states = [unit_chart(width, plan.rows)] * STRANDS
    for i, s, b, t in plan.backward_steps():
        state = states[s]
        state = jnp.concatenate([state[:width], state[width:] + pushed_ref[t]], axis=0)
        states[s] = times_rows(state, weights[b])
    for s in range(STRANDS):
        strand_ref[s] = states[s]
    while len(states) > 1:
        states = [compose(states[i + 1], states[i]) for i in range(0, len(states), 2)]
    total_ref[...] = states[0]


def group_kernel(plan, reverse, *refs):
    groups, width = (plan.groups, plan.width)
    parts, (total_ref, before_ref) = (refs[:groups], refs[groups:])
    fixed = []
    for j in range(groups):
        part = parts[j][...]
        fixed.append(jnp.concatenate([part[:width], swapped(part[width:], j, groups)], axis=0))
    me = lax.axis_index("track")
    order = list(range(groups))[::-1] if reverse else list(range(groups))
    charts = [choose(me ^ q, fixed) for q in order]
    place = groups - 1 - me if reverse else me
    befores = [unit_chart(width, plan.rows), charts[0]]
    while len(befores) < groups:
        befores.append(compose(befores[-1], charts[len(befores) - 1]))
    before_ref[...] = choose(place, befores)
    while len(charts) > 1:
        odd = charts[len(charts) // 2 * 2 :]
        charts = [compose(charts[i], charts[i + 1]) for i in range(0, len(charts) - 1, 2)] + odd
    total_ref[...] = charts[0]


def is_second(mask, reverse):
    second = (lax.axis_index("tm") & mask) != 0
    return jnp.logical_not(second) if reverse else second


def pair_kernel(mask, reverse, last, own_ref, other_ref, before_ref, joined_ref, after_ref):
    width = own_ref.shape[1]
    own, other, before = (own_ref[...], other_ref[...], before_ref[...])
    second = is_second(mask, reverse)
    earlier, later = (jnp.where(second, other, own), jnp.where(second, own, other))
    if last:
        joined_ref[...] = apply(earlier[width:], later)
    else:
        joined_ref[...] = compose(earlier, later)
    after_ref[...] = jnp.where(second, compose(other, before), before)


def entering(far_ref, before_ref, reverse):
    far = far_ref[...]
    return apply(jnp.where(is_second(lax.axis_size("tm") // 2, reverse), far, jnp.zeros_like(far)), before_ref[...])


def filter_kernel(plan, regime_ref, before_ref, far_ref, strand_ref, picked_ref, *refs):
    meas, (filtered_ref, pushed_ref) = (refs[: plan.groups], refs[plan.groups :])
    states = [entering(far_ref, before_ref, False)]
    for s in range(STRANDS - 1):
        states.append(apply(states[-1], strand_ref[s]))
    gains = [plan.gain_row(regime_ref, meas, b) for b in range(plan.share)]
    weights = [doubled(picked_ref[b]) for b in range(plan.share)]
    for i, s, b, t in plan.forward_steps():
        ahead = times_rows(states[s], weights[b])
        pushed = gains[b] * (step_rows(meas, t) - ahead)
        states[s] = ahead + pushed
        filtered_ref[t] = states[s]
        pushed_ref[t] = pushed


def smooth_kernel(
    plan, before_ref, far_ref, strand_ref, picked_ref, filtered_ref, pushed_ref, *outs
):
    tracks = plan.tracks
    states = [entering(far_ref, before_ref, True)]
    for s in range(STRANDS - 1, 0, -1):
        states.append(apply(states[-1], strand_ref[s]))
    states = states[::-1]
    weights = [doubled(picked_ref[b]) for b in range(plan.share)]
    for i, s, b, t in plan.backward_steps():
        value = filtered_ref[t] + states[s]
        for j in range(plan.groups):
            outs[j][t] = value[j * tracks : (j + 1) * tracks]
        if i < plan.length - 1:
            states[s] = times_rows(states[s] + pushed_ref[t], weights[b])


def collect_kernel(plan, *refs):
    parts, out_ref = (refs[: plan.groups], refs[plan.groups])
    for j in range(plan.groups):
        first = pl.multiple_of((lax.axis_index("track") ^ j) * plan.span, plan.span)
        out_ref[pl.ds(first, plan.span)] = parts[j][...]


def body(observations, dynamics, smoother_gain, gains, regime):
    length, tracks, width = observations.shape
    blocks = regime.shape[0]
    groups, spans = (lax.axis_size("track"), lax.axis_size("tm"))
    owned = dynamics.shape[0]
    plan = Plan(groups, blocks // groups, length // blocks, owned, tracks, width)
    chart = shape((width + plan.rows, width))
    offset = shape((plan.rows, width))
    strands = shape((STRANDS,) + chart.shape)
    mats = [shape((plan.share, width, width), BF16)] * groups
    unit = width * width * width
    regime, observations, dynamics, smoother_gain, gains = [
        pltpu.with_memory_space_constraint(value, pltpu.HBM)
        for value in (regime, observations, dynamics, smoother_gain, gains)
    ]

    def swap(value, mask, axis):
        pairs = [(source, source ^ mask) for source in range(lax.axis_size(axis))]
        return lax.ppermute(value, axis, pairs)

    def exchange(values):
        return [values[0]] + [swap(values[j], j, "track") for j in range(1, groups)]

    sems = pltpu.SemaphoreType.DMA((groups,))
    trans = call(
        functools.partial(gather_kernel, plan), mats, [SMEM, HBM], unit, [sems]
    )(regime, dynamics)
    trans = exchange(trans)
    gathered = call(
        functools.partial(second_gather_kernel, plan),
        mats + [shape((plan.span + plan.extra, tracks, width))] * groups,
        [SMEM, HBM, VMEM, VMEM],
        unit,
        [pltpu.VMEM((owned, width), F32), sems],
    )(regime, smoother_gain, gains, observations)
    meas = exchange(gathered[groups:])

    total, fstrand, fpick = call(
        functools.partial(forward_kernel, plan),
        [chart, strands, shape((plan.share, width, width), BF16)],
        [SMEM] + [VMEM] * (2 * groups),
        400 * unit,
    )(regime, *trans, *meas)

    smooth, total = lax.optimization_barrier((gathered[:groups], total))

    def spread(total):
        return exchange([total] * groups)

    def across(total, reverse):
        total, before = call(
            functools.partial(group_kernel, plan, reverse),
            [chart, chart],
            [VMEM] * groups,
            20 * unit,
        )(*spread(total))
        stride = 1
        while 2 * stride < spans:
            last = 4 * stride >= spans
            total, before = call(
                functools.partial(pair_kernel, stride, reverse, last),
                [offset if last else chart, chart],
                [VMEM] * 3,
                20 * unit,
            )(total, swap(total, stride, "tm"), before)
            stride *= 2
        total = total[-plan.rows :] if stride == 1 else total
        return before, swap(total, stride, "tm")

    entry = across(total, False)
    filtered, pushed = call(
        functools.partial(filter_kernel, plan),
        [shape((plan.span, plan.rows, width))] * 2,
        [SMEM] + [VMEM] * (4 + groups),
        100 * unit,
    )(regime, *entry, fstrand, fpick, *meas)

    smooth = exchange(smooth)
    total, bstrand, bpick = call(
        functools.partial(backward_kernel, plan),
        [chart, strands, shape((plan.share, width, width), BF16)],
        [SMEM] + [VMEM] * (groups + 1),
        400 * unit,
    )(regime, *smooth, pushed)

    entry = across(total, True)
    outs = call(
        functools.partial(smooth_kernel, plan),
        [shape((plan.span, tracks, width))] * groups,
        [VMEM] * 6,
        50 * unit,
    )(*entry, bstrand, bpick, filtered, pushed)
    return call(
        functools.partial(collect_kernel, plan),
        [shape((length, tracks, width))],
        [VMEM] * groups,
        unit,
    )(*exchange(outs))[0]


def solution(mesh):
    placed = (
        P("tm", "track", None),
        P("track", None, None),
        P("track", None, None),
        P("track", None),
        P("tm"),
    )

    return jax.shard_map(
        body, mesh=mesh, in_specs=placed, out_specs=P("tm", "track", None), check_vma=False
    )
```

time: 535 us -> 86.8 us (0.16); the launches traced: 525 us -> 86.3 us
  matrix products: 223 us -> 0 us
  blocking collectives: 121 us -> 0 us
  waiting for transfers between devices: 135 us -> 35.7 us
  starting transfers between devices: 6.66 us -> 33.8 us
  Pallas kernels: 0 us -> 16.6 us
  between operations: 14.1 us -> 0.13 us
  local copies, waits for them, and re-layouts: 12.8 us -> 0 us
  other arithmetic: 8.16 us -> 0 us
    dot_general x235 -> x0, matrix products: 223 us -> none  [the longest x230 208 us: matmul(): return jnp.dot(left, right, precision=lax.Precision.HIGHEST)]
    all_gather x8 -> x0, blocking collectives: 93.8 us -> none  [prefix(): everything = jax.tree.map(lambda part: lax.all_gather(part, axis), shard)]
    psum x2 -> x0, waiting for transfers between devices: 75.2 us -> none  [from_root(): return lax.psum(jnp.where(mine, shard, jnp.zeros_like(shard)), axis)]
    unnamed x4 -> x0, waiting for transfers between devices: 58.4 us -> none
    ppermute x1 -> x24, waiting for transfers between devices: 1.2 us -> 35.7 us  [swap(): return lax.ppermute(value, axis, pairs)]
    ppermute x1 -> x24, starting transfers between devices: 1.41 us -> 33.8 us  [swap(): return lax.ppermute(value, axis, pairs)]
    unnamed x1 -> x0, blocking collectives: 17.5 us -> none
    pallas_call x0 -> x13, Pallas kernels: none -> 16.6 us  [the longest x1 3.69 us: body(): call(functools.partial(second_gather_kernel, plan), mats + [shape((plan.s...]
  transfers between devices with their start and end apart: 5 -> 24, of which waited for: 4 -> 15; matrix products, arithmetic and copies ran while one was open for 2% -> 0% of each run, Pallas kernels for 0% -> 8%
where the time goes in v1:
time: 86.8 us; the launch traced here: 86.3 us
  waiting for transfers between devices  35.7 us (41%)
  starting transfers between devices  33.8 us (39%)
  Pallas kernels  16.6 us (19%)
    ppermute x24, waiting for transfers between devices, swap(): return lax.ppermute(value, axis, pairs)  35.7 us
    ppermute x24, starting transfers between devices, swap(): return lax.ppermute(value, axis, pairs)  33.8 us
    pallas_call x1, Pallas kernels, body(): call(functools.partial(second_gather_kernel, plan), mats + [shape((plan.s...  3.69 us
    pallas_call x1, Pallas kernels, body(): call(functools.partial(gather_kernel, plan), mats, [SMEM, HBM], unit, [se...  2.48 us
    pallas_call x1, Pallas kernels, body(): call(functools.partial(forward_kernel, plan), [chart, strands, shape((pla...  2.15 us
    pallas_call x1, Pallas kernels, body(): call(functools.partial(backward_kernel, plan), [chart, strands, shape((pl...  2.14 us
    pallas_call x1, Pallas kernels, body(): call(functools.partial(filter_kernel, plan), [shape((plan.span, plan.rows...  2.13 us
  transfers between devices with their start and end apart: 24, of which 15 were waited for; matrix products, arithmetic and copies ran while one was open for 0% of the time, Pallas kernels for 8%

profile of v1, /device:TPU:0, one launch (start us, length us, event | category | flops | bytes accessed | tf_op | source)
XLA Modules:
  0.0 86.3 jit_solution(4868097002738505394)
XLA Ops:
  0.0 2.5 %shard_map.56 = (bf16[8,128,128]{2,1,0:T(8,128)(2,1)S(1)}, bf16[8,128,128]{2,1,0:T(8,128)(2,1)S(1)}, bf16[8,128,128]{2,1,0:T(8,128)(2,1)S(1)}, bf16[8,128,128]{2,1,0:T(8,128)(2,1)S(1)}) custom-call(s32[32]{0:T(128)} %regime_ref.9, bf16[64,128,128]{2,1,0:T(8,128)(2,1)} %table_ref.3), custom_call_target="tpu_custom_call" | custom-call | flops 2097152 | bytes 32768 | tf_op jit(solution)/shard_map/pallas_call | solution.py:322
  2.5 2.9 %collective-permute-start = (bf16[8,128,128]{2,1,0:T(8,128)(2,1)S(1)}, bf16[8,128,128]{2,1,0:T(8,128)(2,1)S(1)}, u32[]{:S(2)}, u32[]{:S(2)}) collective-permute-start(bf16[8,128,128]{2,1,0:T(8,128)(2,1)S(1)} %get-tuple-element.51), channel_id=1, source_target_pairs={{0,8},{8,0},{16,24},{24,16},{1,9},{9,1},{17,25},{25,17},{2,10},{10... | collective-permute-start | bytes 786440 | tf_op jit(solution)/shard_map/ppermute | solution.py:316
  7.0 3.7 %shard_map.55 = (bf16[8,128,128]{2,1,0:T(8,128)(2,1)S(1)}, bf16[8,128,128]{2,1,0:T(8,128)(2,1)S(1)}, bf16[8,128,128]{2,1,0:T(8,128)(2,1)S(1)}, bf16[8,128,128]{2...) custom-call(s32[32]{0:T(128)} %regime_ref.9, ...), custom_call_target="tpu_custom_call" | custom-call | flops 2097152 | bytes 32768 | tf_op jit(solution)/shard_map/pallas_call | solution.py:326
  10.7 1.8 %collective-permute-start.3 = (f32[34,4,128]{2,1,0:T(4,128)S(1)}, f32[34,4,128]{2,1,0:T(4,128)S(1)}, u32[]{:S(2)}, u32[]{:S(2)}) collective-permute-start(f32[34,4,128]{2,1,0:T(4,128)S(1)} %get-tuple-element.55), channel_id=1, source_target_pairs={{0,8},{8,0},{16,24},{24,16},{1,9},{9,1},{17,25},{25,17},{2,10},{10... | collective-permute-start | bytes 208904 | tf_op jit(solution)/shard_map/ppermute | solution.py:316
  13.9 4.8 %collective-permute-done.3.refs_5_.refs_1_ = f32[34,4,128]{2,1,0:T(4,128)S(1)} collective-permute-done((f32[34,4,128]{2,1,0:T(4,128)S(1)}, f32[34,4,128]{2,1,0:T(4,128)S(1)}, u32[]{:S(2)}, u32[]{:S(2)}) %collective-permute-start.3) | collective-permute-done | bytes 69664 | tf_op jit(solution)/shard_map/ppermute | solution.py:316
  18.7 2.8 %collective-permute-start.5 = (f32[34,4,128]{2,1,0:T(4,128)S(1)}, f32[34,4,128]{2,1,0:T(4,128)S(1)}, u32[]{:S(2)}, u32[]{:S(2)}) collective-permute-start(f32[34,4,128]{2,1,0:T(4,128)S(1)} %get-tuple-element.57), channel_id=1, source_target_pairs={{0,24},{8,16},{16,8},{24,0},{1,25},{9,17},{17,9},{25,1},{2,26},{10... | collective-permute-start | bytes 208904 | tf_op jit(solution)/shard_map/ppermute | solution.py:316
  21.6 2.4 %collective-permute-done.5.refs_7_.refs_3_ = f32[34,4,128]{2,1,0:T(4,128)S(1)} collective-permute-done((f32[34,4,128]{2,1,0:T(4,128)S(1)}, f32[34,4,128]{2,1,0:T(4,128)S(1)}, u32[]{:S(2)}, u32[]{:S(2)}) %collective-permute-start.5) | collective-permute-done | bytes 69664 | tf_op jit(solution)/shard_map/ppermute | solution.py:316
  23.9 2.2 %shard_map.57 = (f32[144,128]{1,0:T(8,128)S(1)}, f32[4,144,128]{2,1,0:T(8,128)S(1)}, bf16[8,128,128]{2,1,0:T(8,128)(2,1)S(1)}) custom-call(s32[32]{0:T(128)} %regime_ref.9, bf16[8,128,128]{2,1,0:T(8,128)(2,1)S(1)} %get-tuple-element.50.refs_0_, bf16[8,128,128]{2,1,0:T(8,128)(2,1)S(1)} %collective-permute-done.refs_1_, ...), custom_call_target="tpu_custom_call" | custom-call | flops 838860800 | bytes 13107200 | tf_op jit(solution)/shard_map/pallas_call | solution.py:335
  26.1 2.9 %collective-permute-start.11 = (f32[144,128]{1,0:T(8,128)S(1)}, f32[144,128]{1,0:T(8,128)S(1)}, u32[]{:S(2)}, u32[]{:S(2)}) collective-permute-start(f32[144,128]{1,0:T(8,128)S(1)} %get-tuple-element.63.refs_0_), channel_id=1, source_target_pairs={{0,24},{8,16},{16,8},{24,0},{1,25},{9,17},{17,9},{25,1},{2,26},{10... | collective-permute-start | bytes 221192 | tf_op jit(solution)/shard_map/ppermute | solution.py:316
  29.7 2.8 %collective-permute-start.8 = (bf16[8,128,128]{2,1,0:T(8,128)(2,1)S(1)}, bf16[8,128,128]{2,1,0:T(8,128)(2,1)S(1)}, u32[]{:S(2)}, u32[]{:S(2)}) collective-permute-start(bf16[8,128,128]{2,1,0:T(8,128)(2,1)S(1)} %get-tuple-element.62), channel_id=1, source_target_pairs={{0,24},{8,16},{16,8},{24,0},{1,25},{9,17},{17,9},{25,1},{2,26},{10... | collective-permute-start | bytes 786440 | tf_op jit(solution)/shard_map/ppermute | solution.py:316
  34.1 9.2 %collective-permute-done.10.refs_2_ = f32[144,128]{1,0:T(8,128)S(1)} collective-permute-done((f32[144,128]{1,0:T(8,128)S(1)}, f32[144,128]{1,0:T(8,128)S(1)}, u32[]{:S(2)}, u32[]{:S(2)}) %collective-permute-start.10) | collective-permute-done | bytes 73760 | tf_op jit(solution)/shard_map/ppermute | solution.py:316
  46.7 3.1 %collective-permute-done.13.other_ref = f32[144,128]{1,0:T(8,128)S(1)} collective-permute-done((f32[144,128]{1,0:T(8,128)S(1)}, f32[144,128]{1,0:T(8,128)S(1)}, u32[]{:S(2)}, u32[]{:S(2)}) %collective-permute-start.13) | collective-permute-done | bytes 73760 | tf_op jit(solution)/shard_map/ppermute | solution.py:316
  50.1 2.5 %collective-permute-start.14 = (f32[16,128]{1,0:T(8,128)S(1)}, f32[16,128]{1,0:T(8,128)S(1)}, u32[]{:S(2)}, u32[]{:S(2)}) collective-permute-start(f32[16,128]{1,0:T(8,128)S(1)} %get-tuple-element.69), channel_id=1, source_target_pairs={{0,4},{1,5},{2,6},{3,7},{4,0},{5,1},{6,2},{7,3},{8,12},{9,13},{10,... | collective-permute-start | bytes 24584 | tf_op jit(solution)/shard_map/ppermute | solution.py:316
  52.5 2.1 %collective-permute-done.14.far_ref = f32[16,128]{1,0:T(8,128)S(1)} collective-permute-done((f32[16,128]{1,0:T(8,128)S(1)}, f32[16,128]{1,0:T(8,128)S(1)}, u32[]{:S(2)}, u32[]{:S(2)}) %collective-permute-start.14) | collective-permute-done | bytes 8224 | tf_op jit(solution)/shard_map/ppermute | solution.py:316
  54.7 2.1 %shard_map.61 = (f32[32,16,128]{2,1,0:T(8,128)S(1)}, f32[32,16,128]{2,1,0:T(8,128)S(1)}) custom-call(s32[32]{0:T(128)} %regime_ref.9, f32[144,128]{1,0:T(8,128)S(1)} %get-tuple-element.68.before_ref, f32[16,128]{1,0:T(8,128)S(1)} %collective-permute-done.14.far_ref, f32[4,144,128]{2,1,0:T(8,128)S(1)} %get-tuple-element.70.strand_ref, ...), custom_call_target="tpu_custom_call" | custom-call | flops 209715200 | bytes 3276800 | tf_op jit(solution)/shard_map/pallas_call | solution.py:368
  56.8 2.1 %shard_map.62 = (f32[144,128]{1,0:T(8,128)S(1)}, f32[4,144,128]{2,1,0:T(8,128)S(1)}, bf16[8,128,128]{2,1,0:T(8,128)(2,1)S(1)}) custom-call(s32[32]{0:T(128)} %regime_ref.9, bf16[8,128,128]{2,1,0:T(8,128)(2,1)S(1)} %get-tuple-element.59.refs_0_, bf16[8,128,128]{2,1,0:T(8,128)(2,1)S(1)} %collective-permute-done.6.refs_1_, ...), custom_call_target="tpu_custom_call" | custom-call | flops 838860800 | bytes 13107200 | tf_op jit(solution)/shard_map/pallas_call | solution.py:376
  59.0 1.5 %collective-permute-start.17 = (f32[144,128]{1,0:T(8,128)S(1)}, f32[144,128]{1,0:T(8,128)S(1)}, u32[]{:S(2)}, u32[]{:S(2)}) collective-permute-start(f32[144,128]{1,0:T(8,128)S(1)} %get-tuple-element.73.refs_0_), channel_id=1, source_target_pairs={{0,24},{8,16},{16,8},{24,0},{1,25},{9,17},{17,9},{25,1},{2,26},{10... | collective-permute-start | bytes 221192 | tf_op jit(solution)/shard_map/ppermute | solution.py:316
  62.5 1.8 %collective-permute-done.17.refs_3_ = f32[144,128]{1,0:T(8,128)S(1)} collective-permute-done((f32[144,128]{1,0:T(8,128)S(1)}, f32[144,128]{1,0:T(8,128)S(1)}, u32[]{:S(2)}, u32[]{:S(2)}) %collective-permute-start.17) | collective-permute-done | bytes 73760 | tf_op jit(solution)/shard_map/ppermute | solution.py:316
  68.2 1.6 %collective-permute-start.19 = (f32[144,128]{1,0:T(8,128)S(1)}, f32[144,128]{1,0:T(8,128)S(1)}, u32[]{:S(2)}, u32[]{:S(2)}) collective-permute-start(f32[144,128]{1,0:T(8,128)S(1)} %get-tuple-element.76.own_ref), channel_id=1, source_target_pairs={{0,2},{1,3},{2,0},{3,1},{4,6},{5,7},{6,4},{7,5},{8,10},{9,11},{10,... | collective-permute-start | bytes 221192 | tf_op jit(solution)/shard_map/ppermute | solution.py:316
  69.8 2.8 %collective-permute-done.19.other_ref = f32[144,128]{1,0:T(8,128)S(1)} collective-permute-done((f32[144,128]{1,0:T(8,128)S(1)}, f32[144,128]{1,0:T(8,128)S(1)}, u32[]{:S(2)}, u32[]{:S(2)}) %collective-permute-start.19) | collective-permute-done | bytes 73760 | tf_op jit(solution)/shard_map/ppermute | solution.py:316
  72.8 2.7 %collective-permute-start.20 = (f32[16,128]{1,0:T(8,128)S(1)}, f32[16,128]{1,0:T(8,128)S(1)}, u32[]{:S(2)}, u32[]{:S(2)}) collective-permute-start(f32[16,128]{1,0:T(8,128)S(1)} %get-tuple-element.79), channel_id=1, source_target_pairs={{0,4},{1,5},{2,6},{3,7},{4,0},{5,1},{6,2},{7,3},{8,12},{9,13},{10,... | collective-permute-start | bytes 24584 | tf_op jit(solution)/shard_map/ppermute | solution.py:316
  75.6 1.9 %collective-permute-done.20.far_ref = f32[16,128]{1,0:T(8,128)S(1)} collective-permute-done((f32[16,128]{1,0:T(8,128)S(1)}, f32[16,128]{1,0:T(8,128)S(1)}, u32[]{:S(2)}, u32[]{:S(2)}) %collective-permute-start.20) | collective-permute-done | bytes 8224 | tf_op jit(solution)/shard_map/ppermute | solution.py:316
  80.4 1.9 %collective-permute-start.23 = (f32[32,4,128]{2,1,0:T(4,128)S(1)}, f32[32,4,128]{2,1,0:T(4,128)S(1)}, u32[]{:S(2)}, u32[]{:S(2)}) collective-permute-start(f32[32,4,128]{2,1,0:T(4,128)S(1)} %get-tuple-element.86), channel_id=1, source_target_pairs={{0,24},{8,16},{16,8},{24,0},{1,25},{9,17},{17,9},{25,1},{2,26},{10... | collective-permute-start | bytes 196616 | tf_op jit(solution)/shard_map/ppermute | solution.py:316
  83.9 1.7 %collective-permute-done.23.refs_3_ = f32[32,4,128]{2,1,0:T(4,128)S(1)} collective-permute-done((f32[32,4,128]{2,1,0:T(4,128)S(1)}, f32[32,4,128]{2,1,0:T(4,128)S(1)}, u32[]{:S(2)}, u32[]{:S(2)}) %collective-permute-start.23) | collective-permute-done | bytes 65568 | tf_op jit(solution)/shard_map/ppermute | solution.py:316
  (37 shorter events, 20.1 us)
Async XLA Ops:
  2.5 21.5 %collective-permute-start = (bf16[8,128,128]{2,1,0:T(8,128)(2,1)S(1)}, bf16[8,128,128]{2,1,0:T(8,128)(2,1)S(1)}, u32[]{:S(2)}, u32[]{:S(2)}) collective-permute-start(bf16[8,128,128]{2,1,0:T(8,128)(2,1)S(1)} %get-tuple-element.51), channel_id=1, source_target_pairs={{0,8},{8,0},{16,24},{24,16},{1,9},{9,1},{17,25},{25,17},{2,10},{10... | collective-permute-start | bytes 786440 | tf_op jit(solution)/shard_map/ppermute | solution.py:316
  5.4 18.5 %collective-permute-start.1 = (bf16[8,128,128]{2,1,0:T(8,128)(2,1)S(1)}, bf16[8,128,128]{2,1,0:T(8,128)(2,1)S(1)}, u32[]{:S(2)}, u32[]{:S(2)}) collective-permute-start(bf16[8,128,128]{2,1,0:T(8,128)(2,1)S(1)} %get-tuple-element.52), channel_id=1, source_target_pairs={{0,16},{8,24},{16,0},{24,8},{1,17},{9,25},{17,1},{25,9},{2,18},{10... | collective-permute-start | bytes 786440 | tf_op jit(solution)/shard_map/ppermute | solution.py:316
  6.9 17.0 %collective-permute-start.2 = (bf16[8,128,128]{2,1,0:T(8,128)(2,1)S(1)}, bf16[8,128,128]{2,1,0:T(8,128)(2,1)S(1)}, u32[]{:S(2)}, u32[]{:S(2)}) collective-permute-start(bf16[8,128,128]{2,1,0:T(8,128)(2,1)S(1)} %get-tuple-element.53), channel_id=1, source_target_pairs={{0,24},{8,16},{16,8},{24,0},{1,25},{9,17},{17,9},{25,1},{2,26},{10... | collective-permute-start | bytes 786440 | tf_op jit(solution)/shard_map/ppermute | solution.py:316
  10.7 8.1 %collective-permute-start.3 = (f32[34,4,128]{2,1,0:T(4,128)S(1)}, f32[34,4,128]{2,1,0:T(4,128)S(1)}, u32[]{:S(2)}, u32[]{:S(2)}) collective-permute-start(f32[34,4,128]{2,1,0:T(4,128)S(1)} %get-tuple-element.55), channel_id=1, source_target_pairs={{0,8},{8,0},{16,24},{24,16},{1,9},{9,1},{17,25},{25,17},{2,10},{10... | collective-permute-start | bytes 208904 | tf_op jit(solution)/shard_map/ppermute | solution.py:316
  12.4 9.2 %collective-permute-start.4 = (f32[34,4,128]{2,1,0:T(4,128)S(1)}, f32[34,4,128]{2,1,0:T(4,128)S(1)}, u32[]{:S(2)}, u32[]{:S(2)}) collective-permute-start(f32[34,4,128]{2,1,0:T(4,128)S(1)} %get-tuple-element.56), channel_id=1, source_target_pairs={{0,16},{8,24},{16,0},{24,8},{1,17},{9,25},{17,1},{25,9},{2,18},{10... | collective-permute-start | bytes 208904 | tf_op jit(solution)/shard_map/ppermute | solution.py:316
  18.7 5.2 %collective-permute-start.5 = (f32[34,4,128]{2,1,0:T(4,128)S(1)}, f32[34,4,128]{2,1,0:T(4,128)S(1)}, u32[]{:S(2)}, u32[]{:S(2)}) collective-permute-start(f32[34,4,128]{2,1,0:T(4,128)S(1)} %get-tuple-element.57), channel_id=1, source_target_pairs={{0,24},{8,16},{16,8},{24,0},{1,25},{9,17},{17,9},{25,1},{2,26},{10... | collective-permute-start | bytes 208904 | tf_op jit(solution)/shard_map/ppermute | solution.py:316
  26.1 6.8 %collective-permute-start.11 = (f32[144,128]{1,0:T(8,128)S(1)}, f32[144,128]{1,0:T(8,128)S(1)}, u32[]{:S(2)}, u32[]{:S(2)}) collective-permute-start(f32[144,128]{1,0:T(8,128)S(1)} %get-tuple-element.63.refs_0_), channel_id=1, source_target_pairs={{0,24},{8,16},{16,8},{24,0},{1,25},{9,17},{17,9},{25,1},{2,26},{10... | collective-permute-start | bytes 221192 | tf_op jit(solution)/shard_map/ppermute | solution.py:316
  29.0 27.8 %collective-permute-start.6 = (bf16[8,128,128]{2,1,0:T(8,128)(2,1)S(1)}, bf16[8,128,128]{2,1,0:T(8,128)(2,1)S(1)}, u32[]{:S(2)}, u32[]{:S(2)}) collective-permute-start(bf16[8,128,128]{2,1,0:T(8,128)(2,1)S(1)} %get-tuple-element.60), channel_id=1, source_target_pairs={{0,8},{8,0},{16,24},{24,16},{1,9},{9,1},{17,25},{25,17},{2,10},{10... | collective-permute-start | bytes 786440 | tf_op jit(solution)/shard_map/ppermute | solution.py:316
  29.6 27.2 %collective-permute-start.7 = (bf16[8,128,128]{2,1,0:T(8,128)(2,1)S(1)}, bf16[8,128,128]{2,1,0:T(8,128)(2,1)S(1)}, u32[]{:S(2)}, u32[]{:S(2)}) collective-permute-start(bf16[8,128,128]{2,1,0:T(8,128)(2,1)S(1)} %get-tuple-element.61), channel_id=1, source_target_pairs={{0,16},{8,24},{16,0},{24,8},{1,17},{9,25},{17,1},{25,9},{2,18},{10... | collective-permute-start | bytes 786440 | tf_op jit(solution)/shard_map/ppermute | solution.py:316
  29.7 27.1 %collective-permute-start.8 = (bf16[8,128,128]{2,1,0:T(8,128)(2,1)S(1)}, bf16[8,128,128]{2,1,0:T(8,128)(2,1)S(1)}, u32[]{:S(2)}, u32[]{:S(2)}) collective-permute-start(bf16[8,128,128]{2,1,0:T(8,128)(2,1)S(1)} %get-tuple-element.62), channel_id=1, source_target_pairs={{0,24},{8,16},{16,8},{24,0},{1,25},{9,17},{17,9},{25,1},{2,26},{10... | collective-permute-start | bytes 786440 | tf_op jit(solution)/shard_map/ppermute | solution.py:316
  32.5 10.8 %collective-permute-start.10 = (f32[144,128]{1,0:T(8,128)S(1)}, f32[144,128]{1,0:T(8,128)S(1)}, u32[]{:S(2)}, u32[]{:S(2)}) collective-permute-start(f32[144,128]{1,0:T(8,128)S(1)} %get-tuple-element.63.refs_0_), channel_id=1, source_target_pairs={{0,16},{8,24},{16,0},{24,8},{1,17},{9,25},{17,1},{25,9},{2,18},{10... | collective-permute-start | bytes 221192 | tf_op jit(solution)/shard_map/ppermute | solution.py:316
  32.9 10.4 %collective-permute-start.9 = (f32[144,128]{1,0:T(8,128)S(1)}, f32[144,128]{1,0:T(8,128)S(1)}, u32[]{:S(2)}, u32[]{:S(2)}) collective-permute-start(f32[144,128]{1,0:T(8,128)S(1)} %get-tuple-element.63.refs_0_), channel_id=1, source_target_pairs={{0,8},{8,0},{16,24},{24,16},{1,9},{9,1},{17,25},{25,17},{2,10},{10... | collective-permute-start | bytes 221192 | tf_op jit(solution)/shard_map/ppermute | solution.py:316
  43.9 1.3 %collective-permute-start.12 = (f32[144,128]{1,0:T(8,128)S(1)}, f32[144,128]{1,0:T(8,128)S(1)}, u32[]{:S(2)}, u32[]{:S(2)}) collective-permute-start(f32[144,128]{1,0:T(8,128)S(1)} %get-tuple-element.64.own_ref), channel_id=1, source_target_pairs={{0,1},{1,0},{2,3},{3,2},{4,5},{5,4},{6,7},{7,6},{8,9},{9,8},{10,11... | collective-permute-start | bytes 221192 | tf_op jit(solution)/shard_map/ppermute | solution.py:316
  45.4 4.4 %collective-permute-start.13 = (f32[144,128]{1,0:T(8,128)S(1)}, f32[144,128]{1,0:T(8,128)S(1)}, u32[]{:S(2)}, u32[]{:S(2)}) collective-permute-start(f32[144,128]{1,0:T(8,128)S(1)} %get-tuple-element.66.own_ref), channel_id=1, source_target_pairs={{0,2},{1,3},{2,0},{3,1},{4,6},{5,7},{6,4},{7,5},{8,10},{9,11},{10,... | collective-permute-start | bytes 221192 | tf_op jit(solution)/shard_map/ppermute | solution.py:316
  50.1 4.6 %collective-permute-start.14 = (f32[16,128]{1,0:T(8,128)S(1)}, f32[16,128]{1,0:T(8,128)S(1)}, u32[]{:S(2)}, u32[]{:S(2)}) collective-permute-start(f32[16,128]{1,0:T(8,128)S(1)} %get-tuple-element.69), channel_id=1, source_target_pairs={{0,4},{1,5},{2,6},{3,7},{4,0},{5,1},{6,2},{7,3},{8,12},{9,13},{10,... | collective-permute-start | bytes 24584 | tf_op jit(solution)/shard_map/ppermute | solution.py:316
  59.0 5.3 %collective-permute-start.17 = (f32[144,128]{1,0:T(8,128)S(1)}, f32[144,128]{1,0:T(8,128)S(1)}, u32[]{:S(2)}, u32[]{:S(2)}) collective-permute-start(f32[144,128]{1,0:T(8,128)S(1)} %get-tuple-element.73.refs_0_), channel_id=1, source_target_pairs={{0,24},{8,16},{16,8},{24,0},{1,25},{9,17},{17,9},{25,1},{2,26},{10... | collective-permute-start | bytes 221192 | tf_op jit(solution)/shard_map/ppermute | solution.py:316
  60.5 4.6 %collective-permute-start.16 = (f32[144,128]{1,0:T(8,128)S(1)}, f32[144,128]{1,0:T(8,128)S(1)}, u32[]{:S(2)}, u32[]{:S(2)}) collective-permute-start(f32[144,128]{1,0:T(8,128)S(1)} %get-tuple-element.73.refs_0_), channel_id=1, source_target_pairs={{0,16},{8,24},{16,0},{24,8},{1,17},{9,25},{17,1},{25,9},{2,18},{10... | collective-permute-start | bytes 221192 | tf_op jit(solution)/shard_map/ppermute | solution.py:316
  61.7 4.4 %collective-permute-start.15 = (f32[144,128]{1,0:T(8,128)S(1)}, f32[144,128]{1,0:T(8,128)S(1)}, u32[]{:S(2)}, u32[]{:S(2)}) collective-permute-start(f32[144,128]{1,0:T(8,128)S(1)} %get-tuple-element.73.refs_0_), channel_id=1, source_target_pairs={{0,8},{8,0},{16,24},{24,16},{1,9},{9,1},{17,25},{25,17},{2,10},{10... | collective-permute-start | bytes 221192 | tf_op jit(solution)/shard_map/ppermute | solution.py:316
  66.6 1.3 %collective-permute-start.18 = (f32[144,128]{1,0:T(8,128)S(1)}, f32[144,128]{1,0:T(8,128)S(1)}, u32[]{:S(2)}, u32[]{:S(2)}) collective-permute-start(f32[144,128]{1,0:T(8,128)S(1)} %get-tuple-element.74.own_ref), channel_id=1, source_target_pairs={{0,1},{1,0},{2,3},{3,2},{4,5},{5,4},{6,7},{7,6},{8,9},{9,8},{10,11... | collective-permute-start | bytes 221192 | tf_op jit(solution)/shard_map/ppermute | solution.py:316
  68.2 4.4 %collective-permute-start.19 = (f32[144,128]{1,0:T(8,128)S(1)}, f32[144,128]{1,0:T(8,128)S(1)}, u32[]{:S(2)}, u32[]{:S(2)}) collective-permute-start(f32[144,128]{1,0:T(8,128)S(1)} %get-tuple-element.76.own_ref), channel_id=1, source_target_pairs={{0,2},{1,3},{2,0},{3,1},{4,6},{5,7},{6,4},{7,5},{8,10},{9,11},{10,... | collective-permute-start | bytes 221192 | tf_op jit(solution)/shard_map/ppermute | solution.py:316
  72.8 4.6 %collective-permute-start.20 = (f32[16,128]{1,0:T(8,128)S(1)}, f32[16,128]{1,0:T(8,128)S(1)}, u32[]{:S(2)}, u32[]{:S(2)}) collective-permute-start(f32[16,128]{1,0:T(8,128)S(1)} %get-tuple-element.79), channel_id=1, source_target_pairs={{0,4},{1,5},{2,6},{3,7},{4,0},{5,1},{6,2},{7,3},{8,12},{9,13},{10,... | collective-permute-start | bytes 24584 | tf_op jit(solution)/shard_map/ppermute | solution.py:316
  78.8 4.3 %collective-permute-start.21 = (f32[32,4,128]{2,1,0:T(4,128)S(1)}, f32[32,4,128]{2,1,0:T(4,128)S(1)}, u32[]{:S(2)}, u32[]{:S(2)}) collective-permute-start(f32[32,4,128]{2,1,0:T(4,128)S(1)} %get-tuple-element.84), channel_id=1, source_target_pairs={{0,8},{8,0},{16,24},{24,16},{1,9},{9,1},{17,25},{25,17},{2,10},{10... | collective-permute-start | bytes 196616 | tf_op jit(solution)/shard_map/ppermute | solution.py:316
  79.6 4.3 %collective-permute-start.22 = (f32[32,4,128]{2,1,0:T(4,128)S(1)}, f32[32,4,128]{2,1,0:T(4,128)S(1)}, u32[]{:S(2)}, u32[]{:S(2)}) collective-permute-start(f32[32,4,128]{2,1,0:T(4,128)S(1)} %get-tuple-element.85), channel_id=1, source_target_pairs={{0,16},{8,24},{16,0},{24,8},{1,17},{9,25},{17,1},{25,9},{2,18},{10... | collective-permute-start | bytes 196616 | tf_op jit(solution)/shard_map/ppermute | solution.py:316
  80.4 5.2 %collective-permute-start.23 = (f32[32,4,128]{2,1,0:T(4,128)S(1)}, f32[32,4,128]{2,1,0:T(4,128)S(1)}, u32[]{:S(2)}, u32[]{:S(2)}) collective-permute-start(f32[32,4,128]{2,1,0:T(4,128)S(1)} %get-tuple-element.86), channel_id=1, source_target_pairs={{0,24},{8,16},{16,8},{24,0},{1,25},{9,17},{17,9},{25,1},{2,26},{10... | collective-permute-start | bytes 196616 | tf_op jit(solution)/shard_map/ppermute | solution.py:316

commit v2 on v1

v2 whole, which is shorter than its diff:
```python
import functools

import jax
import jax.numpy as jnp
from jax import lax
from jax.experimental import pallas as pl
from jax.experimental.pallas import tpu as pltpu
from jax.sharding import PartitionSpec as P


F32 = jnp.float32
BF16 = jnp.bfloat16
VMEM = pl.BlockSpec(memory_space=pltpu.VMEM)
SMEM = pl.BlockSpec(memory_space=pltpu.SMEM)
HBM = pl.BlockSpec(memory_space=pltpu.HBM)
GRANT = 16 * 1024 * 1024


def call(kernel, outs, ins, cost, scratch=()):
    return pl.pallas_call(
        kernel,
        out_shape=outs,
        in_specs=ins,
        out_specs=[VMEM] * len(outs),
        scratch_shapes=list(scratch),
        compiler_params=pltpu.CompilerParams(vmem_limit_bytes=GRANT),
        cost_estimate=pl.CostEstimate(flops=cost, bytes_accessed=cost // 64, transcendentals=0),
    )


def shape(dims, dtype=F32):
    return jax.ShapeDtypeStruct(dims, dtype)


def split(value):
    high = value.astype(BF16)
    low = (value - high.astype(F32)).astype(BF16)
    return high, low


def times_rows(value, doubled):
    pieces = jnp.concatenate(split(value), axis=1)
    return lax.dot_general(
        pieces, doubled, (((1,), (1,)), ((), ())), preferred_element_type=F32
    )


def times(value, matrix):
    high, low = split(value)
    upper, lower = split(matrix)
    left = jnp.concatenate([high, low, high], axis=1)
    right = jnp.concatenate([upper, upper, lower], axis=0)
    return jnp.dot(left, right, preferred_element_type=F32)


def compose(first, second):
    width = first.shape[1]
    product = times(first, second[:width])
    return jnp.concatenate([product[:width], product[width:] + second[width:]], axis=0)


def apply(state, chart):
    width = chart.shape[1]
    return times(state, chart[:width]) + chart[width:]


def unit_matrix(width):
    rows = lax.broadcasted_iota(jnp.int32, (width, width), 0)
    return (rows == lax.broadcasted_iota(jnp.int32, (width, width), 1)).astype(F32)


def unit_chart(width, rows):
    return jnp.concatenate([unit_matrix(width), jnp.zeros((rows, width), F32)], axis=0)


def choose(index, options):
    value = options[0]
    for j in range(1, len(options)):
        value = jnp.where(index == j, options[j], value)
    return value


def swapped(rows, mask, groups):
    block = rows.shape[0] // groups
    return jnp.concatenate(
        [rows[(j ^ mask) * block : ((j ^ mask) + 1) * block] for j in range(groups)], axis=0
    )


def doubled(matrix):
    return jnp.concatenate([matrix, matrix], axis=1)


def step_rows(parts, t):
    return jnp.concatenate([part[t] for part in parts], axis=0)


class Plan:
    def __init__(self, groups, share, dwell, owned, tracks, width):
        self.groups, self.share, self.dwell = groups, share, dwell
        self.owned, self.tracks, self.width = owned, tracks, width
        self.span, self.rows = share * dwell, groups * tracks
        self.extra = -(-share // tracks)

    def local(self, regime_ref, peer, b):
        return regime_ref[peer * self.share + b] - lax.axis_index("track") * self.owned

    def here(self, regime_ref, peer, b):
        return jnp.clip(self.local(regime_ref, peer, b), 0, self.owned - 1)

    def source(self, regime_ref, b):
        me = lax.axis_index("track")
        return (regime_ref[me * self.share + b] // self.owned) ^ me

    def gain_row(self, regime_ref, meas, b):
        step, row = self.span + b // self.tracks, b % self.tracks
        return choose(
            self.source(regime_ref, b), [part[step][row : row + 1] for part in meas]
        )

    def forward_steps(self, first, last):
        return [(b, b * self.dwell + i) for i in range(self.dwell) for b in range(first, last)]

    def backward_steps(self, first, last):
        turn = self.dwell - 1
        return [(b, t + turn - 2 * (t % self.dwell)) for b, t in self.forward_steps(first, last)]


def piece_of(pieces, b):
    for piece in pieces:
        if b < piece.shape[0]:
            return piece.at[b]
        b -= piece.shape[0]


def each_row(plan, regime_ref, table_ref, targets, sem, act):
    for j, pieces in targets:
        peer = lax.axis_index("track") ^ j
        for b in range(plan.share):
            at = plan.local(regime_ref, peer, b)

            @pl.when(jnp.logical_and(at >= 0, at < plan.owned))
            def _():
                copy = pltpu.make_async_copy(table_ref.at[at], piece_of(pieces, b), sem)
                copy.start() if act else copy.wait()


def split_up(refs, layout):
    refs, found = (list(refs), [])
    for pieces in layout:
        found.append([refs.pop(0) for _ in pieces])
    return found


def gather_kernel(plan, layout, regime_ref, table_ref, *refs):
    outs, sem = (split_up(refs[:-1], layout), refs[-1])
    targets = [(j + 1, pieces) for j, pieces in enumerate(outs)]
    each_row(plan, regime_ref, table_ref, targets, sem, True)
    each_row(plan, regime_ref, table_ref, targets, sem, False)


def second_gather_kernel(plan, layout, regime_ref, first_ref, second_ref, *refs):
    own_ref, outs, sem = (refs[0], split_up(refs[1:-1], layout), refs[-1])
    targets = list(enumerate(outs))
    for act in (True, False):
        each_row(plan, regime_ref, first_ref, [(0, [own_ref])], sem, act)
        each_row(plan, regime_ref, second_ref, targets, sem, act)


def measured_kernel(plan, regime_ref, gains_ref, obs_ref, *refs):
    meas, gain_ref = (refs[:-1], refs[-1])
    gain_ref[...] = gains_ref[...].astype(F32)
    for j in range(plan.groups):
        peer = lax.axis_index("track") ^ j
        first = pl.multiple_of(peer * plan.span, plan.span)
        meas[j][0 : plan.span] = obs_ref[pl.ds(first, plan.span)]
        for e in range(plan.extra):
            blocks = [min(e * plan.tracks + i, plan.share - 1) for i in range(plan.tracks)]
            meas[j][plan.span + e] = jnp.concatenate(
                [gain_ref[pl.ds(plan.here(regime_ref, peer, b), 1), :] for b in blocks], axis=0
            )


def picked_weight(plan, regime_ref, mats, b):
    return choose(plan.source(regime_ref, b), [piece_of(pieces, b)[...] for pieces in mats])


def joined(charts):
    while len(charts) > 1:
        odd = charts[len(charts) // 2 * 2 :]
        charts = [compose(charts[i], charts[i + 1]) for i in range(0, len(charts) - 1, 2)] + odd
    return charts[0]


def running(charts):
    if len(charts) == 1:
        return charts
    pairs = running([compose(charts[i], charts[i + 1]) for i in range(0, len(charts) - 1, 2)])
    found = [charts[0]]
    for i in range(1, len(charts)):
        found.append(pairs[i // 2] if i % 2 else compose(pairs[i // 2 - 1], charts[i]))
    return found


def forward_kernel(plan, first, last, layout, regime_ref, *refs):
    count = sum(len(pieces) for pieces in layout)
    mats, refs = (split_up(refs[:count], layout), refs[count:])
    meas, refs = (refs[: plan.groups], refs[plan.groups :])
    earlier_ref, refs = (refs[0], refs[1:]) if first else (None, refs)
    strand_ref, picked_ref, total_ref = refs
    weights, gains, states = ({}, {}, {})
    for b in range(first, last):
        picked = choose(
            plan.source(regime_ref, b),
            [piece_of(mats[0], b)[...]]
            + [piece_of(pieces, b - first)[...] for pieces in mats[1:]],
        )
        picked_ref[b - first] = picked
        weights[b] = doubled(picked)
        gains[b] = plan.gain_row(regime_ref, meas, b)
        states[b] = unit_chart(plan.width, plan.rows)
    for b, t in plan.forward_steps(first, last):
        kept = times_rows(states[b], weights[b]) * (1.0 - gains[b])
        driven = gains[b] * step_rows(meas, t)
        states[b] = jnp.concatenate(
            [kept[: plan.width], kept[plan.width :] + driven], axis=0
        )
    for b in range(first, last):
        strand_ref[b - first] = states[b]
    total = joined(list(states.values()))
    total_ref[...] = compose(earlier_ref[...], total) if first else total


def gain_levels(charts):
    found = [charts]
    while len(charts) > 1:
        charts = [times(charts[i], charts[i + 1]) for i in range(0, len(charts), 2)]
        found.append(charts)
    return found


def backward_kernel(plan, layout, regime_ref, *refs):
    mats, (level_ref, picked_ref) = (split_up(refs[:-2], layout), refs[-2:])
    weights = []
    for b in range(plan.share):
        picked = picked_weight(plan, regime_ref, mats, b)
        picked_ref[b] = picked
        weights.append(doubled(picked))
    states = [unit_matrix(plan.width)] * plan.share
    for b, t in plan.backward_steps(0, plan.share):
        states[b] = times_rows(states[b], weights[b])
    at = 0
    for level in gain_levels(states[::-1]):
        for chart in level:
            level_ref[at] = chart
            at += 1


def forward_running_kernel(first_ref, second_ref, running_ref):
    charts = [first_ref[s] for s in range(first_ref.shape[0])]
    charts += [second_ref[s] for s in range(second_ref.shape[0] - 1)]
    for s, chart in enumerate(running(charts)):
        running_ref[s] = chart


def backward_running_kernel(level_ref, offset_ref, running_ref):
    charts = [
        jnp.concatenate([level_ref[s], offset_ref[s]], axis=0)
        for s in range(offset_ref.shape[0] - 1)
    ]
    for s, chart in enumerate(running(charts)):
        running_ref[s] = chart


def group_kernel(plan, reverse, *refs):
    groups, width = (plan.groups, plan.width)
    parts, (total_ref, before_ref) = (refs[:groups], refs[groups:])
    fixed = []
    for j in range(groups):
        part = parts[j][...]
        fixed.append(jnp.concatenate([part[:width], swapped(part[width:], j, groups)], axis=0))
    me = lax.axis_index("track")
    order = list(range(groups))[::-1] if reverse else list(range(groups))
    charts = [choose(me ^ q, fixed) for q in order]
    place = groups - 1 - me if reverse else me
    befores = [unit_chart(width, plan.rows), charts[0]]
    while len(befores) < groups:
        befores.append(compose(befores[-1], charts[len(befores) - 1]))
    before_ref[...] = choose(place, befores)
    total_ref[...] = joined(charts)


def is_second(mask, reverse):
    second = (lax.axis_index("tm") & mask) != 0
    return jnp.logical_not(second) if reverse else second


def pair_kernel(mask, reverse, last, own_ref, other_ref, before_ref, joined_ref, after_ref):
    width = own_ref.shape[1]
    own, other, before = (own_ref[...], other_ref[...], before_ref[...])
    second = is_second(mask, reverse)
    earlier, later = (jnp.where(second, other, own), jnp.where(second, own, other))
    if last:
        joined_ref[...] = apply(earlier[width:], later)
    else:
        joined_ref[...] = compose(earlier, later)
    after_ref[...] = jnp.where(second, compose(other, before), before)


def entering(far_ref, before_ref, running_ref, reverse):
    far = far_ref[...]
    second = is_second(lax.axis_size("tm") // 2, reverse)
    state = apply(jnp.where(second, far, jnp.zeros_like(far)), before_ref[...])
    return [state] + [apply(state, running_ref[s]) for s in range(running_ref.shape[0])]


def filter_kernel(plan, regime_ref, before_ref, far_ref, running_ref, fpick1_ref, fpick2_ref, *refs):
    meas, refs = (refs[: plan.groups], refs[plan.groups :])
    level_ref, bpick_ref, filtered_ref, pushed_ref, offset_ref, total_ref = refs
    states = entering(far_ref, before_ref, running_ref, False)
    gains = [plan.gain_row(regime_ref, meas, b) for b in range(plan.share)]
    weights = [
        doubled(piece_of([fpick1_ref, fpick2_ref], b)[...]) for b in range(plan.share)
    ]
    pushes = {}
    for b, t in plan.forward_steps(0, plan.share):
        ahead = times_rows(states[b], weights[b])
        pushes[t] = gains[b] * (step_rows(meas, t) - ahead)
        states[b] = ahead + pushes[t]
        filtered_ref[t] = states[b]
        pushed_ref[t] = pushes[t]
    weights = [doubled(bpick_ref[b]) for b in range(plan.share)]
    states = [None] * plan.share
    for b, t in plan.backward_steps(0, plan.share):
        state = pushes[t] if states[b] is None else states[b] + pushes[t]
        states[b] = times_rows(state, weights[b])
    states = states[::-1]
    for b in range(plan.share):
        offset_ref[b] = states[b]
    at = 0
    while len(states) > 1:
        count = len(states)
        states = [
            times(states[i], level_ref[at + i + 1]) + states[i + 1] for i in range(0, count, 2)
        ]
        at += count
    total_ref[0 : plan.width] = level_ref[at]
    total_ref[plan.width :] = states[0]


def smooth_kernel(
    plan, before_ref, far_ref, running_ref, picked_ref, filtered_ref, pushed_ref, *outs
):
    tracks = plan.tracks
    states = entering(far_ref, before_ref, running_ref, True)[::-1]
    weights = [doubled(picked_ref[b]) for b in range(plan.share)]
    for b, t in plan.backward_steps(0, plan.share):
        value = filtered_ref[t] + states[b]
        for j in range(plan.groups):
            outs[j][t] = value[j * tracks : (j + 1) * tracks]
        if t % plan.dwell > 0:
            states[b] = times_rows(states[b] + pushed_ref[t], weights[b])


def collect_kernel(plan, *refs):
    parts, out_ref = (refs[: plan.groups], refs[plan.groups])
    for j in range(plan.groups):
        first = pl.multiple_of((lax.axis_index("track") ^ j) * plan.span, plan.span)
        out_ref[pl.ds(first, plan.span)] = parts[j][...]


def body(observations, dynamics, smoother_gain, gains, regime):
    length, tracks, width = observations.shape
    blocks = regime.shape[0]
    groups, spans = (lax.axis_size("track"), lax.axis_size("tm"))
    owned = dynamics.shape[0]
    plan = Plan(groups, blocks // groups, length // blocks, owned, tracks, width)
    chart = shape((width + plan.rows, width))
    offset = shape((plan.rows, width))
    share, half = (plan.share, plan.share // 2)
    block_mats = lambda count: shape((count, width, width), BF16)
    unit = width * width * width
    regime, observations, dynamics, smoother_gain, gains = [
        pltpu.with_memory_space_constraint(value, pltpu.HBM)
        for value in (regime, observations, dynamics, smoother_gain, gains)
    ]

    def swap(value, mask, axis):
        pairs = [(source, source ^ mask) for source in range(lax.axis_size(axis))]
        return lax.ppermute(value, axis, pairs)

    def exchange(values):
        return [values[0]] + [swap(values[j], j, "track") for j in range(1, groups)]

    sem = pltpu.SemaphoreType.DMA
    halves = [[half, share - half]] * (groups - 1)
    parts = split_up(
        call(
            functools.partial(gather_kernel, plan, halves),
            [block_mats(count) for pieces in halves for count in pieces],
            [SMEM, HBM],
            unit,
            [sem],
        )(regime, dynamics),
        halves,
    )
    first = [swap(pieces[0], j + 1, "track") for j, pieces in enumerate(parts)]
    meas = call(
        functools.partial(measured_kernel, plan),
        [shape((plan.span + plan.extra, tracks, width))] * groups,
        [SMEM, VMEM, VMEM],
        unit,
        [pltpu.VMEM((owned, width), F32)],
    )(regime, gains, observations)
    meas = exchange(meas)
    second = [swap(pieces[1], j + 1, "track") for j, pieces in enumerate(parts)]
    layout = [[share]] * groups
    own, *smooth = call(
        functools.partial(second_gather_kernel, plan, layout),
        [block_mats(share)] + [block_mats(count) for pieces in layout for count in pieces],
        [SMEM, HBM, HBM],
        unit,
        [sem],
    )(regime, dynamics, smoother_gain)
    smooth = split_up(smooth, layout)
    pick = lambda begin, end, mats, more: call(
        functools.partial(forward_kernel, plan, begin, end, [[share]] + [[end - begin]] * (groups - 1)),
        [shape((end - begin,) + chart.shape), block_mats(end - begin), chart],
        [SMEM] + [VMEM] * (2 * groups + len(more)),
        200 * unit,
    )(regime, own, *mats, *meas, *more)
    fstrand1, fpick1, total = pick(0, half, first, [])
    fstrand2, fpick2, total = pick(half, share, second, [total])

    late, total = lax.optimization_barrier(([smooth[j][-1] for j in range(1, groups)], total))

    def spread(total):
        return exchange([total] * groups)

    def across(total, reverse):
        maps = spread(total)
        total, before = call(
            functools.partial(group_kernel, plan, reverse),
            [chart, chart],
            [VMEM] * groups,
            20 * unit,
        )(*maps)
        stride = 1
        while 2 * stride < spans:
            last = 4 * stride >= spans
            total, before = call(
                functools.partial(pair_kernel, stride, reverse, last),
                [offset if last else chart, chart],
                [VMEM] * 3,
                20 * unit,
            )(total, swap(total, stride, "tm"), before)
            stride *= 2
        total = total[-plan.rows :] if stride == 1 else total
        return before, swap(total, stride, "tm")

    late = [swap(value, j + 1, "track") for j, value in enumerate(late)]
    smooth = [smooth[0]] + [[value] for value in late]
    levels = 2 * share - 1
    level, bpick = call(
        functools.partial(backward_kernel, plan, layout),
        [shape((levels, width, width)), block_mats(share)],
        [SMEM] + [VMEM] * sum(len(pieces) for pieces in layout),
        300 * unit,
    )(regime, *[value for pieces in smooth for value in pieces])

    before, far = across(total, False)
    runs = [shape((share - 1,) + chart.shape)]
    (frun,) = call(forward_running_kernel, runs, [VMEM] * 2, 60 * unit)(fstrand1, fstrand2)
    filtered, pushed, offsets, total = call(
        functools.partial(filter_kernel, plan),
        [shape((plan.span, plan.rows, width))] * 2 + [shape((share,) + offset.shape), chart],
        [SMEM] + [VMEM] * (7 + groups),
        100 * unit,
    )(regime, before, far, frun, fpick1, fpick2, *meas, level, bpick)

    before, far = across(total, True)
    (brun,) = call(backward_running_kernel, runs, [VMEM] * 2, 60 * unit)(level, offsets)
    outs = call(
        functools.partial(smooth_kernel, plan),
        [shape((plan.span, tracks, width))] * groups,
        [VMEM] * 6,
        50 * unit,
    )(before, far, brun, bpick, filtered, pushed)
    return call(
        functools.partial(collect_kernel, plan),
        [shape((length, tracks, width))],
        [VMEM] * groups,
        unit,
    )(*exchange(outs))[0]


def solution(mesh):
    placed = (
        P("tm", "track", None),
        P("track", None, None),
        P("track", None, None),
        P("track", None),
        P("tm"),
    )

    return jax.shard_map(
        body, mesh=mesh, in_specs=placed, out_specs=P("tm", "track", None), check_vma=False
    )
```

time: 86.8 us -> 84.1 us (0.969)
  waiting for transfers between devices: 35.7 us -> 28.9 us
  starting transfers between devices: 33.8 us -> 37.7 us
    ppermute x24 -> x27, waiting for transfers between devices: 35.7 us -> 28.9 us  [swap(): return lax.ppermute(value, axis, pairs)]
    ppermute x24 -> x27, starting transfers between devices: 33.8 us -> 37.7 us  [swap(): return lax.ppermute(value, axis, pairs)]
    pallas_call x4 -> x8, Pallas kernels: 10.5 us -> 10.9 us  [the longest x2 3.43 us: body(): call(functools.partial(forward_kernel, plan, begin, end, [[share]] + [[en...]
  transfers between devices with their start and end apart: 24 -> 27, of which waited for: 15 -> 14; matrix products, arithmetic and copies ran while one was open for 0% -> 0% of each run, Pallas kernels for 8% -> 10%
where the time goes in v2:
time: 84.1 us; the launch traced here: 83.7 us
  starting transfers between devices  37.7 us (45%)
  waiting for transfers between devices  28.9 us (34%)
  Pallas kernels  17 us (20%)
    ppermute x27, starting transfers between devices, swap(): return lax.ppermute(value, axis, pairs)  37.7 us
    ppermute x27, waiting for transfers between devices, swap(): return lax.ppermute(value, axis, pairs)  28.9 us
    pallas_call x2, Pallas kernels, body(): call(functools.partial(forward_kernel, plan, begin, end, [[share]] + [[en...  3.43 us
    pallas_call x1, Pallas kernels, body(): call(functools.partial(filter_kernel, plan), [shape((plan.span, plan.rows...  2.59 us
    pallas_call x1, Pallas kernels, body(): call(functools.partial(backward_kernel, plan, layout), [shape((levels, wi...  2.01 us
  transfers between devices with their start and end apart: 27, of which 14 were waited for; matrix products, arithmetic and copies ran while one was open for 0% of the time, Pallas kernels for 10%

profile of v2, /device:TPU:0, one launch (start us, length us, event | category | flops | bytes accessed | tf_op | source)
XLA Modules:
  0.0 83.7 jit_solution(7476282207449963829)
XLA Ops:
  0.0 1.5 %shard_map.56 = (bf16[4,128,128]{2,1,0:T(8,128)(2,1)S(1)}, bf16[4,128,128]{2,1,0:T(8,128)(2,1)S(1)}, bf16[4,128,128]{2,1,0:T(8,128)(2,1)S(1)}, bf16[4,128,128]{2...) custom-call(s32[32]{0:T(128)} %regime_ref.13, bf16[64,128,128]{2,1,0:T(8,128)(2,1)} %table_ref.1), custom_call_target="tpu_custom_call" | custom-call | flops 2097152 | bytes 32768 | tf_op jit(solution)/shard_map/pallas_call | solution.py:398
  1.5 3.0 %collective-permute-start.6 = (bf16[4,128,128]{2,1,0:T(8,128)(2,1)S(1)}, bf16[4,128,128]{2,1,0:T(8,128)(2,1)S(1)}, u32[]{:S(2)}, u32[]{:S(2)}) collective-permute-start(bf16[4,128,128]{2,1,0:T(8,128)(2,1)S(1)} %get-tuple-element.63), channel_id=1, source_target_pairs={{0,8},{8,0},{16,24},{24,16},{1,9},{9,1},{17,25},{25,17},{2,10},{10... | collective-permute-start | bytes 393224 | tf_op jit(solution)/shard_map/ppermute | solution.py:390
  5.7 2.1 %collective-permute-start.4 = (f32[34,4,128]{2,1,0:T(4,128)S(1)}, f32[34,4,128]{2,1,0:T(4,128)S(1)}, u32[]{:S(2)}, u32[]{:S(2)}) collective-permute-start(f32[34,4,128]{2,1,0:T(4,128)S(1)} %get-tuple-element.61), channel_id=1, source_target_pairs={{0,16},{8,24},{16,0},{24,8},{1,17},{9,25},{17,1},{25,9},{2,18},{10... | collective-permute-start | bytes 208904 | tf_op jit(solution)/shard_map/ppermute | solution.py:390
  9.2 1.5 %collective-permute-start.7 = (bf16[4,128,128]{2,1,0:T(8,128)(2,1)S(1)}, bf16[4,128,128]{2,1,0:T(8,128)(2,1)S(1)}, u32[]{:S(2)}, u32[]{:S(2)}) collective-permute-start(bf16[4,128,128]{2,1,0:T(8,128)(2,1)S(1)} %get-tuple-element.64), channel_id=1, source_target_pairs={{0,16},{8,24},{16,0},{24,8},{1,17},{9,25},{17,1},{25,9},{2,18},{10... | collective-permute-start | bytes 393224 | tf_op jit(solution)/shard_map/ppermute | solution.py:390
  10.7 2.0 %collective-permute-start.8 = (bf16[4,128,128]{2,1,0:T(8,128)(2,1)S(1)}, bf16[4,128,128]{2,1,0:T(8,128)(2,1)S(1)}, u32[]{:S(2)}, u32[]{:S(2)}) collective-permute-start(bf16[4,128,128]{2,1,0:T(8,128)(2,1)S(1)} %get-tuple-element.65), channel_id=1, source_target_pairs={{0,24},{8,16},{16,8},{24,0},{1,25},{9,17},{17,9},{25,1},{2,26},{10... | collective-permute-start | bytes 393224 | tf_op jit(solution)/shard_map/ppermute | solution.py:390
  13.7 3.2 %collective-permute-start.1 = (bf16[4,128,128]{2,1,0:T(8,128)(2,1)S(1)}, bf16[4,128,128]{2,1,0:T(8,128)(2,1)S(1)}, u32[]{:S(2)}, u32[]{:S(2)}) collective-permute-start(bf16[4,128,128]{2,1,0:T(8,128)(2,1)S(1)} %get-tuple-element.57), channel_id=1, source_target_pairs={{0,16},{8,24},{16,0},{24,8},{1,17},{9,25},{17,1},{25,9},{2,18},{10... | collective-permute-start | bytes 393224 | tf_op jit(solution)/shard_map/ppermute | solution.py:390
  17.0 1.6 %shard_map.55 = (bf16[8,128,128]{2,1,0:T(8,128)(2,1)S(1)}, bf16[8,128,128]{2,1,0:T(8,128)(2,1)S(1)}, bf16[8,128,128]{2,1,0:T(8,128)(2,1)S(1)}, bf16[8,128,128]{2,1,0:T(8,128)(2,1)S(1)}, bf16[8,128,128]{2,1,0:T(8,128)(2,1)S(1)}) custom-call(s32[32]{0:T(128)} %regime_ref.13, bf16[64,128,128]{2,1,0:T(8,128)(2,1)} %table_ref.1, bf16[64,128,128]{2,1,0:T(8,128)(2,1)} %second_ref.1), custom_call_target="tpu_custom_call" | custom-call | flops 2097152 | bytes 32768 | tf_op jit(solution)/shard_map/pallas_call | solution.py:418
  18.6 1.6 %collective-permute-done.7.refs_2_ = bf16[4,128,128]{2,1,0:T(8,128)(2,1)S(1)} collective-permute-done((bf16[4,128,128]{2,1,0:T(8,128)(2,1)S(1)}, bf16[4,128,128]{2,1,0:T(8,128)(2,1)S(1)}, u32[]{:S(2)}, u32[]{:S(2)}) %collective-permute-start.7) | collective-permute-done | bytes 131104 | tf_op jit(solution)/shard_map/ppermute | solution.py:390
  20.2 1.6 %shard_map.58 = (f32[4,144,128]{2,1,0:T(8,128)S(1)}, bf16[4,128,128]{2,1,0:T(8,128)(2,1)S(1)}, f32[144,128]{1,0:T(8,128)S(1)}) custom-call(s32[32]{0:T(128)} %regime_ref.13, bf16[8,128,128]{2,1,0:T(8,128)(2,1)S(1)} %get-tuple-element.55.refs_0_, bf16[4,128,128]{2,1,0:T(8,128)(2,1)S(1)} %collective-permute-done.6.refs_1_, ...), custom_call_target="tpu_custom_call" | custom-call | flops 419430400 | bytes 6553600 | tf_op jit(solution)/shard_map/pallas_call | solution.py:426
  23.2 1.8 %shard_map.59 = (f32[4,144,128]{2,1,0:T(8,128)S(1)}, bf16[4,128,128]{2,1,0:T(8,128)(2,1)S(1)}, f32[144,128]{1,0:T(8,128)S(1)}) custom-call(s32[32]{0:T(128)} %regime_ref.13, bf16[8,128,128]{2,1,0:T(8,128)(2,1)S(1)} %get-tuple-element.55.refs_0_, bf16[4,128,128]{2,1,0:T(8,128)(2,1)S(1)} %collective-permute-done.refs_1_, ...), custom_call_target="tpu_custom_call" | custom-call | flops 419430400 | bytes 6553600 | tf_op jit(solution)/shard_map/pallas_call | solution.py:426
  25.0 2.3 %collective-permute-start.11 = (f32[144,128]{1,0:T(8,128)S(1)}, f32[144,128]{1,0:T(8,128)S(1)}, u32[]{:S(2)}, u32[]{:S(2)}) collective-permute-start(f32[144,128]{1,0:T(8,128)S(1)} %get-tuple-element.68.refs_0_), channel_id=1, source_target_pairs={{0,24},{8,16},{16,8},{24,0},{1,25},{9,17},{17,9},{25,1},{2,26},{10... | collective-permute-start | bytes 221192 | tf_op jit(solution)/shard_map/ppermute | solution.py:390
  28.5 2.2 %collective-permute-start.17 = (bf16[8,128,128]{2,1,0:T(8,128)(2,1)S(1)}, bf16[8,128,128]{2,1,0:T(8,128)(2,1)S(1)}, u32[]{:S(2)}, u32[]{:S(2)}) collective-permute-start(bf16[8,128,128]{2,1,0:T(8,128)(2,1)S(1)} %get-tuple-element.82), channel_id=1, source_target_pairs={{0,24},{8,16},{16,8},{24,0},{1,25},{9,17},{17,9},{25,1},{2,26},{10... | collective-permute-start | bytes 786440 | tf_op jit(solution)/shard_map/ppermute | solution.py:390
  32.3 10.4 %collective-permute-done.10.refs_2_ = f32[144,128]{1,0:T(8,128)S(1)} collective-permute-done((f32[144,128]{1,0:T(8,128)S(1)}, f32[144,128]{1,0:T(8,128)S(1)}, u32[]{:S(2)}, u32[]{:S(2)}) %collective-permute-start.10) | collective-permute-done | bytes 73760 | tf_op jit(solution)/shard_map/ppermute | solution.py:390
  44.9 1.7 %collective-permute-start.13 = (f32[144,128]{1,0:T(8,128)S(1)}, f32[144,128]{1,0:T(8,128)S(1)}, u32[]{:S(2)}, u32[]{:S(2)}) collective-permute-start(f32[144,128]{1,0:T(8,128)S(1)} %get-tuple-element.71.own_ref), channel_id=1, source_target_pairs={{0,2},{1,3},{2,0},{3,1},{4,6},{5,7},{6,4},{7,5},{8,10},{9,11},{10,... | collective-permute-start | bytes 221192 | tf_op jit(solution)/shard_map/ppermute | solution.py:390
  47.3 2.1 %collective-permute-done.13.other_ref = f32[144,128]{1,0:T(8,128)S(1)} collective-permute-done((f32[144,128]{1,0:T(8,128)S(1)}, f32[144,128]{1,0:T(8,128)S(1)}, u32[]{:S(2)}, u32[]{:S(2)}) %collective-permute-start.13) | collective-permute-done | bytes 73760 | tf_op jit(solution)/shard_map/ppermute | solution.py:390
  49.5 2.8 %collective-permute-start.14 = (f32[16,128]{1,0:T(8,128)S(1)}, f32[16,128]{1,0:T(8,128)S(1)}, u32[]{:S(2)}, u32[]{:S(2)}) collective-permute-start(f32[16,128]{1,0:T(8,128)S(1)} %get-tuple-element.74), channel_id=1, source_target_pairs={{0,4},{1,5},{2,6},{3,7},{4,0},{5,1},{6,2},{7,3},{8,12},{9,13},{10,... | collective-permute-start | bytes 24584 | tf_op jit(solution)/shard_map/ppermute | solution.py:390
  52.4 2.0 %shard_map.64 = (f32[15,128,128]{2,1,0:T(8,128)S(1)}, bf16[8,128,128]{2,1,0:T(8,128)(2,1)S(1)}) custom-call(s32[32]{0:T(128)} %regime_ref.13, bf16[8,128,128]{2,1,0:T(8,128)(2,1)S(1)} %get-tuple-element.79.refs_0_, bf16[8,128,128]{2,1,0:T(8,128)(2,1)S(1)} %collective-permute-done.15.refs_1_, bf16[8,128,128]{2,1,0:T(8,128)(2,1)S(1)} %collective-permute-done.16.refs_2_, ...), custom_call_target="tpu_custom_call" | custom-call | flops 629145600 | bytes 9830400 | tf_op jit(solution)/shard_map/pallas_call | solution.py:464
  54.4 2.6 %shard_map.65 = (f32[32,16,128]{2,1,0:T(8,128)S(1)}, f32[32,16,128]{2,1,0:T(8,128)S(1)}, f32[8,16,128]{2,1,0:T(8,128)S(1)}, f32[144,128]{1,0:T(8,128)S(1)}) custom-call(s32[32]{0:T(128)} %regime_ref.13, f32[144,128]{1,0:T(8,128)S(1)} %get-tuple-element.73.before_ref, f32[16,128]{1,0:T(8,128)S(1)} %collective-permute-done.14.far_ref, ...), custom_call_target="tpu_custom_call" | custom-call | flops 209715200 | bytes 3276800 | tf_op jit(solution)/shard_map/pallas_call | solution.py:474
  60.5 1.8 %collective-permute-done.20.refs_3_ = f32[144,128]{1,0:T(8,128)S(1)} collective-permute-done((f32[144,128]{1,0:T(8,128)S(1)}, f32[144,128]{1,0:T(8,128)S(1)}, u32[]{:S(2)}, u32[]{:S(2)}) %collective-permute-start.20) | collective-permute-done | bytes 73760 | tf_op jit(solution)/shard_map/ppermute | solution.py:390
  66.0 1.7 %collective-permute-start.22 = (f32[144,128]{1,0:T(8,128)S(1)}, f32[144,128]{1,0:T(8,128)S(1)}, u32[]{:S(2)}, u32[]{:S(2)}) collective-permute-start(f32[144,128]{1,0:T(8,128)S(1)} %get-tuple-element.88.own_ref), channel_id=1, source_target_pairs={{0,2},{1,3},{2,0},{3,1},{4,6},{5,7},{6,4},{7,5},{8,10},{9,11},{10,... | collective-permute-start | bytes 221192 | tf_op jit(solution)/shard_map/ppermute | solution.py:390
  67.8 2.7 %collective-permute-done.22.other_ref = f32[144,128]{1,0:T(8,128)S(1)} collective-permute-done((f32[144,128]{1,0:T(8,128)S(1)}, f32[144,128]{1,0:T(8,128)S(1)}, u32[]{:S(2)}, u32[]{:S(2)}) %collective-permute-start.22) | collective-permute-done | bytes 73760 | tf_op jit(solution)/shard_map/ppermute | solution.py:390
  70.7 2.6 %collective-permute-start.23 = (f32[16,128]{1,0:T(8,128)S(1)}, f32[16,128]{1,0:T(8,128)S(1)}, u32[]{:S(2)}, u32[]{:S(2)}) collective-permute-start(f32[16,128]{1,0:T(8,128)S(1)} %get-tuple-element.91), channel_id=1, source_target_pairs={{0,4},{1,5},{2,6},{3,7},{4,0},{5,1},{6,2},{7,3},{8,12},{9,13},{10,... | collective-permute-start | bytes 24584 | tf_op jit(solution)/shard_map/ppermute | solution.py:390
  77.8 1.8 %collective-permute-start.26 = (f32[32,4,128]{2,1,0:T(4,128)S(1)}, f32[32,4,128]{2,1,0:T(4,128)S(1)}, u32[]{:S(2)}, u32[]{:S(2)}) collective-permute-start(f32[32,4,128]{2,1,0:T(4,128)S(1)} %get-tuple-element.98), channel_id=1, source_target_pairs={{0,24},{8,16},{16,8},{24,0},{1,25},{9,17},{17,9},{25,1},{2,26},{10... | collective-permute-start | bytes 196616 | tf_op jit(solution)/shard_map/ppermute | solution.py:390
  81.3 1.7 %collective-permute-done.26.refs_3_ = f32[32,4,128]{2,1,0:T(4,128)S(1)} collective-permute-done((f32[32,4,128]{2,1,0:T(4,128)S(1)}, f32[32,4,128]{2,1,0:T(4,128)S(1)}, u32[]{:S(2)}, u32[]{:S(2)}) %collective-permute-start.26) | collective-permute-done | bytes 65568 | tf_op jit(solution)/shard_map/ppermute | solution.py:390
  (47 shorter events, 25.2 us)
Async XLA Ops:
  1.5 15.4 %collective-permute-start.6 = (bf16[4,128,128]{2,1,0:T(8,128)(2,1)S(1)}, bf16[4,128,128]{2,1,0:T(8,128)(2,1)S(1)}, u32[]{:S(2)}, u32[]{:S(2)}) collective-permute-start(bf16[4,128,128]{2,1,0:T(8,128)(2,1)S(1)} %get-tuple-element.63), channel_id=1, source_target_pairs={{0,8},{8,0},{16,24},{24,16},{1,9},{9,1},{17,25},{25,17},{2,10},{10... | collective-permute-start | bytes 393224 | tf_op jit(solution)/shard_map/ppermute | solution.py:390
  5.6 5.1 %collective-permute-start.3 = (f32[34,4,128]{2,1,0:T(4,128)S(1)}, f32[34,4,128]{2,1,0:T(4,128)S(1)}, u32[]{:S(2)}, u32[]{:S(2)}) collective-permute-start(f32[34,4,128]{2,1,0:T(4,128)S(1)} %get-tuple-element.60), channel_id=1, source_target_pairs={{0,8},{8,0},{16,24},{24,16},{1,9},{9,1},{17,25},{25,17},{2,10},{10... | collective-permute-start | bytes 208904 | tf_op jit(solution)/shard_map/ppermute | solution.py:390
  5.7 7.0 %collective-permute-start.4 = (f32[34,4,128]{2,1,0:T(4,128)S(1)}, f32[34,4,128]{2,1,0:T(4,128)S(1)}, u32[]{:S(2)}, u32[]{:S(2)}) collective-permute-start(f32[34,4,128]{2,1,0:T(4,128)S(1)} %get-tuple-element.61), channel_id=1, source_target_pairs={{0,16},{8,24},{16,0},{24,8},{1,17},{9,25},{17,1},{25,9},{2,18},{10... | collective-permute-start | bytes 208904 | tf_op jit(solution)/shard_map/ppermute | solution.py:390
  7.8 5.9 %collective-permute-start.5 = (f32[34,4,128]{2,1,0:T(4,128)S(1)}, f32[34,4,128]{2,1,0:T(4,128)S(1)}, u32[]{:S(2)}, u32[]{:S(2)}) collective-permute-start(f32[34,4,128]{2,1,0:T(4,128)S(1)} %get-tuple-element.62), channel_id=1, source_target_pairs={{0,24},{8,16},{16,8},{24,0},{1,25},{9,17},{17,9},{25,1},{2,26},{10... | collective-permute-start | bytes 208904 | tf_op jit(solution)/shard_map/ppermute | solution.py:390
  9.2 11.0 %collective-permute-start.7 = (bf16[4,128,128]{2,1,0:T(8,128)(2,1)S(1)}, bf16[4,128,128]{2,1,0:T(8,128)(2,1)S(1)}, u32[]{:S(2)}, u32[]{:S(2)}) collective-permute-start(bf16[4,128,128]{2,1,0:T(8,128)(2,1)S(1)} %get-tuple-element.64), channel_id=1, source_target_pairs={{0,16},{8,24},{16,0},{24,8},{1,17},{9,25},{17,1},{25,9},{2,18},{10... | collective-permute-start | bytes 393224 | tf_op jit(solution)/shard_map/ppermute | solution.py:390
  10.7 9.4 %collective-permute-start.8 = (bf16[4,128,128]{2,1,0:T(8,128)(2,1)S(1)}, bf16[4,128,128]{2,1,0:T(8,128)(2,1)S(1)}, u32[]{:S(2)}, u32[]{:S(2)}) collective-permute-start(bf16[4,128,128]{2,1,0:T(8,128)(2,1)S(1)} %get-tuple-element.65), channel_id=1, source_target_pairs={{0,24},{8,16},{16,8},{24,0},{1,25},{9,17},{17,9},{25,1},{2,26},{10... | collective-permute-start | bytes 393224 | tf_op jit(solution)/shard_map/ppermute | solution.py:390
  12.7 9.1 %collective-permute-start = (bf16[4,128,128]{2,1,0:T(8,128)(2,1)S(1)}, bf16[4,128,128]{2,1,0:T(8,128)(2,1)S(1)}, u32[]{:S(2)}, u32[]{:S(2)}) collective-permute-start(bf16[4,128,128]{2,1,0:T(8,128)(2,1)S(1)} %get-tuple-element.56), channel_id=1, source_target_pairs={{0,8},{8,0},{16,24},{24,16},{1,9},{9,1},{17,25},{25,17},{2,10},{10... | collective-permute-start | bytes 393224 | tf_op jit(solution)/shard_map/ppermute | solution.py:390
  13.7 9.4 %collective-permute-start.1 = (bf16[4,128,128]{2,1,0:T(8,128)(2,1)S(1)}, bf16[4,128,128]{2,1,0:T(8,128)(2,1)S(1)}, u32[]{:S(2)}, u32[]{:S(2)}) collective-permute-start(bf16[4,128,128]{2,1,0:T(8,128)(2,1)S(1)} %get-tuple-element.57), channel_id=1, source_target_pairs={{0,16},{8,24},{16,0},{24,8},{1,17},{9,25},{17,1},{25,9},{2,18},{10... | collective-permute-start | bytes 393224 | tf_op jit(solution)/shard_map/ppermute | solution.py:390
  17.0 6.2 %collective-permute-start.2 = (bf16[4,128,128]{2,1,0:T(8,128)(2,1)S(1)}, bf16[4,128,128]{2,1,0:T(8,128)(2,1)S(1)}, u32[]{:S(2)}, u32[]{:S(2)}) collective-permute-start(bf16[4,128,128]{2,1,0:T(8,128)(2,1)S(1)} %get-tuple-element.58), channel_id=1, source_target_pairs={{0,24},{8,16},{16,8},{24,0},{1,25},{9,17},{17,9},{25,1},{2,26},{10... | collective-permute-start | bytes 393224 | tf_op jit(solution)/shard_map/ppermute | solution.py:390
  25.0 6.3 %collective-permute-start.11 = (f32[144,128]{1,0:T(8,128)S(1)}, f32[144,128]{1,0:T(8,128)S(1)}, u32[]{:S(2)}, u32[]{:S(2)}) collective-permute-start(f32[144,128]{1,0:T(8,128)S(1)} %get-tuple-element.68.refs_0_), channel_id=1, source_target_pairs={{0,24},{8,16},{16,8},{24,0},{1,25},{9,17},{17,9},{25,1},{2,26},{10... | collective-permute-start | bytes 221192 | tf_op jit(solution)/shard_map/ppermute | solution.py:390
  27.2 25.1 %collective-permute-start.15 = (bf16[8,128,128]{2,1,0:T(8,128)(2,1)S(1)}, bf16[8,128,128]{2,1,0:T(8,128)(2,1)S(1)}, u32[]{:S(2)}, u32[]{:S(2)}) collective-permute-start(bf16[8,128,128]{2,1,0:T(8,128)(2,1)S(1)} %get-tuple-element.80), channel_id=1, source_target_pairs={{0,8},{8,0},{16,24},{24,16},{1,9},{9,1},{17,25},{25,17},{2,10},{10... | collective-permute-start | bytes 786440 | tf_op jit(solution)/shard_map/ppermute | solution.py:390
  27.8 24.5 %collective-permute-start.16 = (bf16[8,128,128]{2,1,0:T(8,128)(2,1)S(1)}, bf16[8,128,128]{2,1,0:T(8,128)(2,1)S(1)}, u32[]{:S(2)}, u32[]{:S(2)}) collective-permute-start(bf16[8,128,128]{2,1,0:T(8,128)(2,1)S(1)} %get-tuple-element.81), channel_id=1, source_target_pairs={{0,16},{8,24},{16,0},{24,8},{1,17},{9,25},{17,1},{25,9},{2,18},{10... | collective-permute-start | bytes 786440 | tf_op jit(solution)/shard_map/ppermute | solution.py:390
  28.5 23.8 %collective-permute-start.17 = (bf16[8,128,128]{2,1,0:T(8,128)(2,1)S(1)}, bf16[8,128,128]{2,1,0:T(8,128)(2,1)S(1)}, u32[]{:S(2)}, u32[]{:S(2)}) collective-permute-start(bf16[8,128,128]{2,1,0:T(8,128)(2,1)S(1)} %get-tuple-element.82), channel_id=1, source_target_pairs={{0,24},{8,16},{16,8},{24,0},{1,25},{9,17},{17,9},{25,1},{2,26},{10... | collective-permute-start | bytes 786440 | tf_op jit(solution)/shard_map/ppermute | solution.py:390
  30.7 12.1 %collective-permute-start.10 = (f32[144,128]{1,0:T(8,128)S(1)}, f32[144,128]{1,0:T(8,128)S(1)}, u32[]{:S(2)}, u32[]{:S(2)}) collective-permute-start(f32[144,128]{1,0:T(8,128)S(1)} %get-tuple-element.68.refs_0_), channel_id=1, source_target_pairs={{0,16},{8,24},{16,0},{24,8},{1,17},{9,25},{17,1},{25,9},{2,18},{10... | collective-permute-start | bytes 221192 | tf_op jit(solution)/shard_map/ppermute | solution.py:390
  31.2 11.5 %collective-permute-start.9 = (f32[144,128]{1,0:T(8,128)S(1)}, f32[144,128]{1,0:T(8,128)S(1)}, u32[]{:S(2)}, u32[]{:S(2)}) collective-permute-start(f32[144,128]{1,0:T(8,128)S(1)} %get-tuple-element.68.refs_0_), channel_id=1, source_target_pairs={{0,8},{8,0},{16,24},{24,16},{1,9},{9,1},{17,25},{25,17},{2,10},{10... | collective-permute-start | bytes 221192 | tf_op jit(solution)/shard_map/ppermute | solution.py:390
  44.9 4.4 %collective-permute-start.13 = (f32[144,128]{1,0:T(8,128)S(1)}, f32[144,128]{1,0:T(8,128)S(1)}, u32[]{:S(2)}, u32[]{:S(2)}) collective-permute-start(f32[144,128]{1,0:T(8,128)S(1)} %get-tuple-element.71.own_ref), channel_id=1, source_target_pairs={{0,2},{1,3},{2,0},{3,1},{4,6},{5,7},{6,4},{7,5},{8,10},{9,11},{10,... | collective-permute-start | bytes 221192 | tf_op jit(solution)/shard_map/ppermute | solution.py:390
  49.5 4.8 %collective-permute-start.14 = (f32[16,128]{1,0:T(8,128)S(1)}, f32[16,128]{1,0:T(8,128)S(1)}, u32[]{:S(2)}, u32[]{:S(2)}) collective-permute-start(f32[16,128]{1,0:T(8,128)S(1)} %get-tuple-element.74), channel_id=1, source_target_pairs={{0,4},{1,5},{2,6},{3,7},{4,0},{5,1},{6,2},{7,3},{8,12},{9,13},{10,... | collective-permute-start | bytes 24584 | tf_op jit(solution)/shard_map/ppermute | solution.py:390
  57.0 5.3 %collective-permute-start.20 = (f32[144,128]{1,0:T(8,128)S(1)}, f32[144,128]{1,0:T(8,128)S(1)}, u32[]{:S(2)}, u32[]{:S(2)}) collective-permute-start(f32[144,128]{1,0:T(8,128)S(1)} %get-tuple-element.85.refs_0_), channel_id=1, source_target_pairs={{0,24},{8,16},{16,8},{24,0},{1,25},{9,17},{17,9},{25,1},{2,26},{10... | collective-permute-start | bytes 221192 | tf_op jit(solution)/shard_map/ppermute | solution.py:390
  58.4 4.7 %collective-permute-start.19 = (f32[144,128]{1,0:T(8,128)S(1)}, f32[144,128]{1,0:T(8,128)S(1)}, u32[]{:S(2)}, u32[]{:S(2)}) collective-permute-start(f32[144,128]{1,0:T(8,128)S(1)} %get-tuple-element.85.refs_0_), channel_id=1, source_target_pairs={{0,16},{8,24},{16,0},{24,8},{1,17},{9,25},{17,1},{25,9},{2,18},{10... | collective-permute-start | bytes 221192 | tf_op jit(solution)/shard_map/ppermute | solution.py:390
  59.6 4.4 %collective-permute-start.18 = (f32[144,128]{1,0:T(8,128)S(1)}, f32[144,128]{1,0:T(8,128)S(1)}, u32[]{:S(2)}, u32[]{:S(2)}) collective-permute-start(f32[144,128]{1,0:T(8,128)S(1)} %get-tuple-element.85.refs_0_), channel_id=1, source_target_pairs={{0,8},{8,0},{16,24},{24,16},{1,9},{9,1},{17,25},{25,17},{2,10},{10... | collective-permute-start | bytes 221192 | tf_op jit(solution)/shard_map/ppermute | solution.py:390
  66.0 4.4 %collective-permute-start.22 = (f32[144,128]{1,0:T(8,128)S(1)}, f32[144,128]{1,0:T(8,128)S(1)}, u32[]{:S(2)}, u32[]{:S(2)}) collective-permute-start(f32[144,128]{1,0:T(8,128)S(1)} %get-tuple-element.88.own_ref), channel_id=1, source_target_pairs={{0,2},{1,3},{2,0},{3,1},{4,6},{5,7},{6,4},{7,5},{8,10},{9,11},{10,... | collective-permute-start | bytes 221192 | tf_op jit(solution)/shard_map/ppermute | solution.py:390
  70.7 4.6 %collective-permute-start.23 = (f32[16,128]{1,0:T(8,128)S(1)}, f32[16,128]{1,0:T(8,128)S(1)}, u32[]{:S(2)}, u32[]{:S(2)}) collective-permute-start(f32[16,128]{1,0:T(8,128)S(1)} %get-tuple-element.91), channel_id=1, source_target_pairs={{0,4},{1,5},{2,6},{3,7},{4,0},{5,1},{6,2},{7,3},{8,12},{9,13},{10,... | collective-permute-start | bytes 24584 | tf_op jit(solution)/shard_map/ppermute | solution.py:390
  76.1 4.3 %collective-permute-start.24 = (f32[32,4,128]{2,1,0:T(4,128)S(1)}, f32[32,4,128]{2,1,0:T(4,128)S(1)}, u32[]{:S(2)}, u32[]{:S(2)}) collective-permute-start(f32[32,4,128]{2,1,0:T(4,128)S(1)} %get-tuple-element.96), channel_id=1, source_target_pairs={{0,8},{8,0},{16,24},{24,16},{1,9},{9,1},{17,25},{25,17},{2,10},{10... | collective-permute-start | bytes 196616 | tf_op jit(solution)/shard_map/ppermute | solution.py:390
  77.8 5.2 %collective-permute-start.26 = (f32[32,4,128]{2,1,0:T(4,128)S(1)}, f32[32,4,128]{2,1,0:T(4,128)S(1)}, u32[]{:S(2)}, u32[]{:S(2)}) collective-permute-start(f32[32,4,128]{2,1,0:T(4,128)S(1)} %get-tuple-element.98), channel_id=1, source_target_pairs={{0,24},{8,16},{16,8},{24,0},{1,25},{9,17},{17,9},{25,1},{2,26},{10... | collective-permute-start | bytes 196616 | tf_op jit(solution)/shard_map/ppermute | solution.py:390
  (3 other events, 6.9 us)

commit v3 on v2

--- a/solution.py
+++ b/solution.py
@@ -16,12 +16,12 @@
 GRANT = 16 * 1024 * 1024
 
 
-def call(kernel, outs, ins, cost, scratch=()):
+def call(kernel, outs, ins, cost, scratch=(), places=None):
     return pl.pallas_call(
         kernel,
         out_shape=outs,
         in_specs=ins,
-        out_specs=[VMEM] * len(outs),
+        out_specs=places or [VMEM] * len(outs),
         scratch_shapes=list(scratch),
         compiler_params=pltpu.CompilerParams(vmem_limit_bytes=GRANT),
         cost_estimate=pl.CostEstimate(flops=cost, bytes_accessed=cost // 64, transcendentals=0),
@@ -101,6 +101,8 @@
         self.owned, self.tracks, self.width = owned, tracks, width
         self.span, self.rows = share * dwell, groups * tracks
         self.extra = -(-share // tracks)
+        self.spare = share // 4
+        self.fast = share - self.spare
 
     def local(self, regime_ref, peer, b):
         return regime_ref[peer * self.share + b] - lax.axis_index("track") * self.owned
@@ -118,57 +120,75 @@
             self.source(regime_ref, b), [part[step][row : row + 1] for part in meas]
         )
 
-    def forward_steps(self, first, last):
-        return [(b, b * self.dwell + i) for i in range(self.dwell) for b in range(first, last)]
-
-    def backward_steps(self, first, last):
+    def forward_steps(self):
+        return [(b, b * self.dwell + i) for i in range(self.dwell) for b in range(self.share)]
+
+    def backward_steps(self):
         turn = self.dwell - 1
-        return [(b, t + turn - 2 * (t % self.dwell)) for b, t in self.forward_steps(first, last)]
-
-
-def piece_of(pieces, b):
-    for piece in pieces:
-        if b < piece.shape[0]:
-            return piece.at[b]
-        b -= piece.shape[0]
+        return [(b, t + turn - 2 * (t % self.dwell)) for b, t in self.forward_steps()]
 
 
 def each_row(plan, regime_ref, table_ref, targets, sem, act):
-    for j, pieces in targets:
+    def row(held, at, target):
+        @pl.when(held)
+        def _():
+            copy = pltpu.make_async_copy(table_ref.at[at], target, sem)
+            copy.start() if act else copy.wait()
+
+    for j, main, more in targets:
         peer = lax.axis_index("track") ^ j
+        slot = jnp.int32(0)
         for b in range(plan.share):
             at = plan.local(regime_ref, peer, b)
-
-            @pl.when(jnp.logical_and(at >= 0, at < plan.owned))
-            def _():
-                copy = pltpu.make_async_copy(table_ref.at[at], piece_of(pieces, b), sem)
-                copy.start() if act else copy.wait()
-
-
-def split_up(refs, layout):
-    refs, found = (list(refs), [])
-    for pieces in layout:
-        found.append([refs.pop(0) for _ in pieces])
-    return found
-
-
-def gather_kernel(plan, layout, regime_ref, table_ref, *refs):
-    outs, sem = (split_up(refs[:-1], layout), refs[-1])
-    targets = [(j + 1, pieces) for j, pieces in enumerate(outs)]
-    each_row(plan, regime_ref, table_ref, targets, sem, True)
-    each_row(plan, regime_ref, table_ref, targets, sem, False)
-
-
-def second_gather_kernel(plan, layout, regime_ref, first_ref, second_ref, *refs):
-    own_ref, outs, sem = (refs[0], split_up(refs[1:-1], layout), refs[-1])
-    targets = list(enumerate(outs))
+            held = jnp.logical_and(at >= 0, at < plan.owned)
+            if j == 0:
+                row(held, at, main.at[b])
+                continue
+            if b < plan.fast:
+                row(held, at, main.at[slot])
+            else:
+                fits = slot < plan.fast
+                row(jnp.logical_and(held, fits), at, main.at[jnp.minimum(slot, plan.fast - 1)])
+                late = jnp.clip(slot - plan.fast, 0, plan.spare - 1)
+                row(jnp.logical_and(held, jnp.logical_not(fits)), at, more.at[late])
+            slot = slot + held.astype(jnp.int32)
+
+
+def remote_targets(plan, refs):
+    peers = plan.groups - 1
+    return [(j + 1, refs[j], refs[peers + j]) for j in range(peers)]
+
+
+def gather_kernel(plan, regime_ref, table_ref, *refs):
     for act in (True, False):
-        each_row(plan, regime_ref, first_ref, [(0, [own_ref])], sem, act)
+        each_row(plan, regime_ref, table_ref, remote_targets(plan, refs[:-1]), refs[-1], act)
+
+
+def second_gather_kernel(plan, regime_ref, first_ref, second_ref, *refs):
+    own_first, own_second, refs, sem = (refs[0], refs[1], refs[2:-1], refs[-1])
+    targets = [(0, own_second, None)] + remote_targets(plan, refs)
+    for act in (True, False):
+        each_row(plan, regime_ref, first_ref, [(0, own_first, None)], sem, act)
         each_row(plan, regime_ref, second_ref, targets, sem, act)
 
 
+def picked_matrix(plan, regime_ref, refs, b):
+    peers = plan.groups - 1
+    own, main, more = (refs[0], refs[1 : peers + 1], refs[peers + 1 :])
+    me = lax.axis_index("track")
+    holder = [lax.div(regime_ref[me * plan.share + i], plan.owned) for i in range(b + 1)]
+    slot = sum((holder[i] == holder[b]).astype(jnp.int32) for i in range(b)) if b else 0
+    source = holder[b] ^ me
+    if b < plan.fast:
+        return choose(source, [own[b]] + [part[slot] for part in main])
+    found = choose(source, [own[b]] + [part[jnp.minimum(slot, plan.fast - 1)] for part in main])
+    late = jnp.clip(slot - plan.fast, 0, plan.spare - 1)
+    rest = choose(source, [own[b]] + [part[late] for part in more])
+    return jnp.where(slot < plan.fast, found, rest)
+
+
 def measured_kernel(plan, regime_ref, gains_ref, obs_ref, *refs):
-    meas, gain_ref = (refs[:-1], refs[-1])
+    meas, over_ref, gain_ref = (refs[:-2], refs[-2], refs[-1])
     gain_ref[...] = gains_ref[...].astype(F32)
     for j in range(plan.groups):
         peer = lax.axis_index("track") ^ j
@@ -179,10 +199,13 @@
             meas[j][plan.span + e] = jnp.concatenate(
                 [gain_ref[pl.ds(plan.here(regime_ref, peer, b), 1), :] for b in blocks], axis=0
             )
-
-
-def picked_weight(plan, regime_ref, mats, b):
-    return choose(plan.source(regime_ref, b), [piece_of(pieces, b)[...] for pieces in mats])
+    most = jnp.int32(0)
+    for peer in range(plan.groups):
+        holder = [lax.div(regime_ref[peer * plan.share + b], plan.owned) for b in range(plan.share)]
+        for q in range(plan.groups):
+            if q != peer:
+                most = jnp.maximum(most, sum((at == q).astype(jnp.int32) for at in holder))
+    over_ref[0] = most
 
 
 def joined(charts):
@@ -202,33 +225,30 @@
     return found
 
 
-def forward_kernel(plan, first, last, layout, regime_ref, *refs):
-    count = sum(len(pieces) for pieces in layout)
-    mats, refs = (split_up(refs[:count], layout), refs[count:])
-    meas, refs = (refs[: plan.groups], refs[plan.groups :])
-    earlier_ref, refs = (refs[0], refs[1:]) if first else (None, refs)
-    strand_ref, picked_ref, total_ref = refs
-    weights, gains, states = ({}, {}, {})
-    for b in range(first, last):
-        picked = choose(
-            plan.source(regime_ref, b),
-            [piece_of(mats[0], b)[...]]
-            + [piece_of(pieces, b - first)[...] for pieces in mats[1:]],
-        )
-        picked_ref[b - first] = picked
-        weights[b] = doubled(picked)
-        gains[b] = plan.gain_row(regime_ref, meas, b)
-        states[b] = unit_chart(plan.width, plan.rows)
-    for b, t in plan.forward_steps(first, last):
+def forward_kernel(plan, regime_ref, *refs):
+    count = 2 * plan.groups - 1
+    mats, meas = (refs[:count], refs[count : count + plan.groups])
+    total_ref, strand_ref, picked_ref = refs[count + plan.groups :]
+    weights, gains, states = ([], [], [])
+    for b in range(plan.share):
+        picked = picked_matrix(plan, regime_ref, mats, b)
+        picked_ref[b] = picked
+        weights.append(doubled(picked))
+        gains.append(plan.gain_row(regime_ref, meas, b))
+        driven = gains[b] * step_rows(meas, b * plan.dwell)
+        kept = picked.astype(F32).T * (1.0 - gains[b])
+        states.append(jnp.concatenate([kept, driven], axis=0))
+    for b, t in plan.forward_steps():
+        if t % plan.dwell == 0:
+            continue
         kept = times_rows(states[b], weights[b]) * (1.0 - gains[b])
         driven = gains[b] * step_rows(meas, t)
         states[b] = jnp.concatenate(
             [kept[: plan.width], kept[plan.width :] + driven], axis=0
         )
-    for b in range(first, last):
-        strand_ref[b - first] = states[b]
-    total = joined(list(states.values()))
-    total_ref[...] = compose(earlier_ref[...], total) if first else total
+    for b in range(plan.share):
+        strand_ref[b] = states[b]
+    total_ref[...] = joined(states)
 
 
 def gain_levels(charts):
@@ -239,16 +259,17 @@
     return found
 
 
-def backward_kernel(plan, layout, regime_ref, *refs):
-    mats, (level_ref, picked_ref) = (split_up(refs[:-2], layout), refs[-2:])
-    weights = []
+def backward_kernel(plan, regime_ref, *refs):
+    mats, (level_ref, picked_ref) = (refs[:-2], refs[-2:])
+    weights, states = ([], [])
     for b in range(plan.share):
-        picked = picked_weight(plan, regime_ref, mats, b)
+        picked = picked_matrix(plan, regime_ref, mats, b)
         picked_ref[b] = picked
         weights.append(doubled(picked))
-    states = [unit_matrix(plan.width)] * plan.share
-    for b, t in plan.backward_steps(0, plan.share):
-        states[b] = times_rows(states[b], weights[b])
+        states.append(picked.astype(F32).T)
+    for b, t in plan.backward_steps():
+        if t % plan.dwell < plan.dwell - 1:
+            states[b] = times_rows(states[b], weights[b])
     at = 0
     for level in gain_levels(states[::-1]):
         for chart in level:
@@ -256,9 +277,8 @@
             at += 1
 
 
-def forward_running_kernel(first_ref, second_ref, running_ref):
-    charts = [first_ref[s] for s in range(first_ref.shape[0])]
-    charts += [second_ref[s] for s in range(second_ref.shape[0] - 1)]
+def forward_running_kernel(strand_ref, running_ref):
+    charts = [strand_ref[s] for s in range(strand_ref.shape[0] - 1)]
     for s, chart in enumerate(running(charts)):
         running_ref[s] = chart
 
@@ -314,16 +334,14 @@
     return [state] + [apply(state, running_ref[s]) for s in range(running_ref.shape[0])]
 
 
-def filter_kernel(plan, regime_ref, before_ref, far_ref, running_ref, fpick1_ref, fpick2_ref, *refs):
+def filter_kernel(plan, regime_ref, before_ref, far_ref, running_ref, fpick_ref, *refs):
     meas, refs = (refs[: plan.groups], refs[plan.groups :])
     level_ref, bpick_ref, filtered_ref, pushed_ref, offset_ref, total_ref = refs
     states = entering(far_ref, before_ref, running_ref, False)
     gains = [plan.gain_row(regime_ref, meas, b) for b in range(plan.share)]
-    weights = [
-        doubled(piece_of([fpick1_ref, fpick2_ref], b)[...]) for b in range(plan.share)
-    ]
+    weights = [doubled(fpick_ref[b]) for b in range(plan.share)]
     pushes = {}
-    for b, t in plan.forward_steps(0, plan.share):
+    for b, t in plan.forward_steps():
         ahead = times_rows(states[b], weights[b])
         pushes[t] = gains[b] * (step_rows(meas, t) - ahead)
         states[b] = ahead + pushes[t]
@@ -331,7 +349,7 @@
         pushed_ref[t] = pushes[t]
     weights = [doubled(bpick_ref[b]) for b in range(plan.share)]
     states = [None] * plan.share
-    for b, t in plan.backward_steps(0, plan.share):
+    for b, t in plan.backward_steps():
         state = pushes[t] if states[b] is None else states[b] + pushes[t]
         states[b] = times_rows(state, weights[b])
     states = states[::-1]
@@ -354,7 +372,7 @@
     tracks = plan.tracks
     states = entering(far_ref, before_ref, running_ref, True)[::-1]
     weights = [doubled(picked_ref[b]) for b in range(plan.share)]
-    for b, t in plan.backward_steps(0, plan.share):
+    for b, t in plan.backward_steps():
         value = filtered_ref[t] + states[b]
         for j in range(plan.groups):
             outs[j][t] = value[j * tracks : (j + 1) * tracks]
@@ -377,7 +395,7 @@
     plan = Plan(groups, blocks // groups, length // blocks, owned, tracks, width)
     chart = shape((width + plan.rows, width))
     offset = shape((plan.rows, width))
-    share, half = (plan.share, plan.share // 2)
+    share = plan.share
     block_mats = lambda count: shape((count, width, width), BF16)
     unit = width * width * width
     regime, observations, dynamics, smoother_gain, gains = [
@@ -393,46 +411,43 @@
         return [values[0]] + [swap(values[j], j, "track") for j in range(1, groups)]
 
     sem = pltpu.SemaphoreType.DMA
-    halves = [[half, share - half]] * (groups - 1)
-    parts = split_up(
-        call(
-            functools.partial(gather_kernel, plan, halves),
-            [block_mats(count) for pieces in halves for count in pieces],
-            [SMEM, HBM],
-            unit,
-            [sem],
-        )(regime, dynamics),
-        halves,
-    )
-    first = [swap(pieces[0], j + 1, "track") for j, pieces in enumerate(parts)]
-    meas = call(
+    peers = groups - 1
+    slots = [block_mats(plan.fast)] * peers + [block_mats(plan.spare)] * peers
+    trans = call(
+        functools.partial(gather_kernel, plan), slots, [SMEM, HBM], unit, [sem]
+    )(regime, dynamics)
+    atrans = [swap(value, j + 1, "track") for j, value in enumerate(trans[:peers])]
+    *meas, over = call(
         functools.partial(measured_kernel, plan),
-        [shape((plan.span + plan.extra, tracks, width))] * groups,
+        [shape((plan.span + plan.extra, tracks, width))] * groups + [shape((1,), jnp.int32)],
         [SMEM, VMEM, VMEM],
         unit,
         [pltpu.VMEM((owned, width), F32)],
+        [VMEM] * groups + [SMEM],
     )(regime, gains, observations)
     meas = exchange(meas)
-    second = [swap(pieces[1], j + 1, "track") for j, pieces in enumerate(parts)]
-    layout = [[share]] * groups
-    own, *smooth = call(
-        functools.partial(second_gather_kernel, plan, layout),
-        [block_mats(share)] + [block_mats(count) for pieces in layout for count in pieces],
+    own, gown, *smooth = call(
+        functools.partial(second_gather_kernel, plan),
+        [block_mats(share)] * 2 + slots,
         [SMEM, HBM, HBM],
         unit,
         [sem],
     )(regime, dynamics, smoother_gain)
-    smooth = split_up(smooth, layout)
-    pick = lambda begin, end, mats, more: call(
-        functools.partial(forward_kernel, plan, begin, end, [[share]] + [[end - begin]] * (groups - 1)),
-        [shape((end - begin,) + chart.shape), block_mats(end - begin), chart],
-        [SMEM] + [VMEM] * (2 * groups + len(more)),
-        200 * unit,
-    )(regime, own, *mats, *meas, *more)
-    fstrand1, fpick1, total = pick(0, half, first, [])
-    fstrand2, fpick2, total = pick(half, share, second, [total])
-
-    late, total = lax.optimization_barrier(([smooth[j][-1] for j in range(1, groups)], total))
+
+    def all_further(values):
+        return [swap(value, j % peers + 1, "track") for j, value in enumerate(values)]
+
+    further = lax.cond(
+        over[0] > plan.fast, all_further, lambda values: values, [*trans[peers:], *smooth[peers:]]
+    )
+    total, fstrand, fpick = call(
+        functools.partial(forward_kernel, plan),
+        [chart, shape((share,) + chart.shape), block_mats(share)],
+        [SMEM] + [VMEM] * (3 * groups - 1),
+        400 * unit,
+    )(regime, own, *atrans, *further[:peers], *meas)
+
+    late, total = lax.optimization_barrier((smooth[:peers], total))
 
     def spread(total):
         return exchange([total] * groups)
@@ -459,24 +474,23 @@
         return before, swap(total, stride, "tm")
 
     late = [swap(value, j + 1, "track") for j, value in enumerate(late)]
-    smooth = [smooth[0]] + [[value] for value in late]
     levels = 2 * share - 1
     level, bpick = call(
-        functools.partial(backward_kernel, plan, layout),
+        functools.partial(backward_kernel, plan),
         [shape((levels, width, width)), block_mats(share)],
-        [SMEM] + [VMEM] * sum(len(pieces) for pieces in layout),
+        [SMEM] + [VMEM] * (2 * groups - 1),
         300 * unit,
-    )(regime, *[value for pieces in smooth for value in pieces])
+    )(regime, gown, *late, *further[peers:])
 
     before, far = across(total, False)
     runs = [shape((share - 1,) + chart.shape)]
-    (frun,) = call(forward_running_kernel, runs, [VMEM] * 2, 60 * unit)(fstrand1, fstrand2)
+    (frun,) = call(forward_running_kernel, runs, [VMEM], 60 * unit)(fstrand)
     filtered, pushed, offsets, total = call(
         functools.partial(filter_kernel, plan),
         [shape((plan.span, plan.rows, width))] * 2 + [shape((share,) + offset.shape), chart],
-        [SMEM] + [VMEM] * (7 + groups),
+        [SMEM] + [VMEM] * (6 + groups),
         100 * unit,
-    )(regime, before, far, frun, fpick1, fpick2, *meas, level, bpick)
+    )(regime, before, far, frun, fpick, *meas, level, bpick)
 
     before, far = across(total, True)
     (brun,) = call(backward_running_kernel, runs, [VMEM] * 2, 60 * unit)(level, offsets)

time: 84.1 us -> 80.6 us (0.958)
  starting transfers between devices: 37.7 us -> 31.5 us
  waiting for transfers between devices: 28.9 us -> 31.7 us
    ppermute x27 -> x24, starting transfers between devices: 37.7 us -> 31.5 us  [swap(): return lax.ppermute(value, axis, pairs)]
    ppermute x27 -> x24, waiting for transfers between devices: 28.9 us -> 31.7 us  [swap(): return lax.ppermute(value, axis, pairs)]
    pallas_call x6 -> x5, Pallas kernels: 9.19 us -> 7.8 us  [the longest x1 2 us: body(): call(functools.partial(forward_kernel, plan), [chart, shape((share,) + ch...]
  transfers between devices with their start and end apart: 27 -> 24, of which waited for: 14 -> 15; matrix products, arithmetic and copies ran while one was open for 0% -> 0% of each run, Pallas kernels for 10% -> 5%
where the time goes in v3:
time: 80.6 us; the launch traced here: 80.3 us
  waiting for transfers between devices  31.7 us (39%)
  starting transfers between devices  31.5 us (39%)
  Pallas kernels  16.3 us (20%)
  between operations  0.83 us (1%)
    ppermute x24, waiting for transfers between devices, swap(): return lax.ppermute(value, axis, pairs)  31.7 us
    ppermute x24, starting transfers between devices, swap(): return lax.ppermute(value, axis, pairs)  31.5 us
    pallas_call x1, Pallas kernels, body(): call(functools.partial(filter_kernel, plan), [shape((plan.span, plan.rows...  2.58 us
    pallas_call x1, Pallas kernels, body(): call(functools.partial(forward_kernel, plan), [chart, shape((share,) + ch...  2 us
    pallas_call x1, Pallas kernels, body(): call(functools.partial(backward_kernel, plan), [shape((levels, width, wid...  1.97 us
    pallas_call x1, Pallas kernels, body(): call(functools.partial(measured_kernel, plan), [shape((plan.span + plan.e...  1.74 us
    pallas_call x1, Pallas kernels, body(): call(functools.partial(second_gather_kernel, plan), [block_mats(share)] *...  1.62 us
  transfers between devices with their start and end apart: 24, of which 15 were waited for; matrix products, arithmetic and copies ran while one was open for 0% of the time, Pallas kernels for 5%

profile of v3, /device:TPU:0, one launch (start us, length us, event | category | flops | bytes accessed | tf_op | source)
XLA Modules:
  0.0 80.3 jit_solution(11441353056383747684)
XLA Ops:
  0.0 1.6 %shard_map.56 = (bf16[6,128,128]{2,1,0:T(8,128)(2,1)S(1)}, bf16[6,128,128]{2,1,0:T(8,128)(2,1)S(1)}, bf16[6,128,128]{2,1,0:T(8,128)(2,1)S(1)}, bf16[2,128,128]{2...) custom-call(s32[32]{0:T(128)} %regime_ref.11, bf16[64,128,128]{2,1,0:T(8,128)(2,1)} %table_ref.1), custom_call_target="tpu_custom_call" | custom-call | flops 2097152 | bytes 32768 | tf_op jit(solution)/shard_map/pallas_call | solution.py:416
  1.6 1.6 %shard_map.55 = (bf16[8,128,128]{2,1,0:T(8,128)(2,1)S(1)}, bf16[8,128,128]{2,1,0:T(8,128)(2,1)S(1)}, bf16[6,128,128]{2,1,0:T(8,128)(2,1)S(1)}, bf16[6,128,128]{2...) custom-call(s32[32]{0:T(128)} %regime_ref.11, ...), custom_call_target="tpu_custom_call" | custom-call | flops 2097152 | bytes 32768 | tf_op jit(solution)/shard_map/pallas_call | solution.py:429
  3.2 1.7 %shard_map.57 = (f32[34,4,128]{2,1,0:T(4,128)S(1)}, f32[34,4,128]{2,1,0:T(4,128)S(1)}, f32[34,4,128]{2,1,0:T(4,128)S(1)}, f32[34,4,128]{2,1,0:T(4,128)S(1)}, s32[1]{0:T(128)}) custom-call(s32[32]{0:T(128)} %regime_ref.11, bf16[64,128]{1,0:T(8,128)(2,1)} %gains_ref.1, f32[128,4,128]{2,1,0:T(4,128)} %obs_ref.1), custom_call_target="tpu_custom_call" | custom-call | flops 2097152 | bytes 32768 | tf_op jit(solution)/shard_map/pallas_call | solution.py:420
  5.6 3.0 %collective-permute-start.6 = (bf16[6,128,128]{2,1,0:T(8,128)(2,1)S(1)}, bf16[6,128,128]{2,1,0:T(8,128)(2,1)S(1)}, u32[]{:S(2)}, u32[]{:S(2)}) collective-permute-start(bf16[6,128,128]{2,1,0:T(8,128)(2,1)S(1)} %get-tuple-element.93), channel_id=1, source_target_pairs={{0,8},{8,0},{16,24},{24,16},{1,9},{9,1},{17,25},{25,17},{2,10},{10... | collective-permute-start | bytes 589832 | tf_op jit(solution)/shard_map/ppermute | solution.py:408
  8.6 1.6 %collective-permute-start.7 = (bf16[6,128,128]{2,1,0:T(8,128)(2,1)S(1)}, bf16[6,128,128]{2,1,0:T(8,128)(2,1)S(1)}, u32[]{:S(2)}, u32[]{:S(2)}) collective-permute-start(bf16[6,128,128]{2,1,0:T(8,128)(2,1)S(1)} %get-tuple-element.94), channel_id=1, source_target_pairs={{0,16},{8,24},{16,0},{24,8},{1,17},{9,25},{17,1},{25,9},{2,18},{10... | collective-permute-start | bytes 589832 | tf_op jit(solution)/shard_map/ppermute | solution.py:408
  10.3 1.8 %collective-permute-start.9 = (f32[34,4,128]{2,1,0:T(4,128)S(1)}, f32[34,4,128]{2,1,0:T(4,128)S(1)}, u32[]{:S(2)}, u32[]{:S(2)}) collective-permute-start(f32[34,4,128]{2,1,0:T(4,128)S(1)} %get-tuple-element.107), channel_id=1, source_target_pairs={{0,8},{8,0},{16,24},{24,16},{1,9},{9,1},{17,25},{25,17},{2,10},{10... | collective-permute-start | bytes 208904 | tf_op jit(solution)/shard_map/ppermute | solution.py:408
  12.1 1.6 %collective-permute-start.10 = (f32[34,4,128]{2,1,0:T(4,128)S(1)}, f32[34,4,128]{2,1,0:T(4,128)S(1)}, u32[]{:S(2)}, u32[]{:S(2)}) collective-permute-start(f32[34,4,128]{2,1,0:T(4,128)S(1)} %get-tuple-element.108), channel_id=1, source_target_pairs={{0,16},{8,24},{16,0},{24,8},{1,17},{9,25},{17,1},{25,9},{2,18},{10... | collective-permute-start | bytes 208904 | tf_op jit(solution)/shard_map/ppermute | solution.py:408
  13.7 3.6 %collective-permute-done.9.refs_8_.refs_1_ = f32[34,4,128]{2,1,0:T(4,128)S(1)} collective-permute-done((f32[34,4,128]{2,1,0:T(4,128)S(1)}, f32[34,4,128]{2,1,0:T(4,128)S(1)}, u32[]{:S(2)}, u32[]{:S(2)}) %collective-permute-start.9) | collective-permute-done | bytes 69664 | tf_op jit(solution)/shard_map/ppermute | solution.py:408
  17.3 3.0 %collective-permute-start.11 = (f32[34,4,128]{2,1,0:T(4,128)S(1)}, f32[34,4,128]{2,1,0:T(4,128)S(1)}, u32[]{:S(2)}, u32[]{:S(2)}) collective-permute-start(f32[34,4,128]{2,1,0:T(4,128)S(1)} %get-tuple-element.109), channel_id=1, source_target_pairs={{0,24},{8,16},{16,8},{24,0},{1,25},{9,17},{17,9},{25,1},{2,26},{10... | collective-permute-start | bytes 208904 | tf_op jit(solution)/shard_map/ppermute | solution.py:408
  20.3 3.0 %collective-permute-done.11.refs_10_.refs_3_ = f32[34,4,128]{2,1,0:T(4,128)S(1)} collective-permute-done((f32[34,4,128]{2,1,0:T(4,128)S(1)}, f32[34,4,128]{2,1,0:T(4,128)S(1)}, u32[]{:S(2)}, u32[]{:S(2)}) %collective-permute-start.11) | collective-permute-done | bytes 69664 | tf_op jit(solution)/shard_map/ppermute | solution.py:408
  23.3 2.0 %shard_map.58 = (f32[144,128]{1,0:T(8,128)S(1)}, f32[8,144,128]{2,1,0:T(8,128)S(1)}, bf16[8,128,128]{2,1,0:T(8,128)(2,1)S(1)}) custom-call(s32[32]{0:T(128)} %regime_ref.11, bf16[8,128,128]{2,1,0:T(8,128)(2,1)S(1)} %get-tuple-element.92.refs_0_, bf16[6,128,128]{2,1,0:T(8,128)(2,1)S(1)} %collective-permute-done.6.refs_1_, ...), custom_call_target="tpu_custom_call" | custom-call | flops 838860800 | bytes 13107200 | tf_op jit(solution)/shard_map/pallas_call | solution.py:443
  25.3 1.6 %collective-permute-start.12 = (f32[144,128]{1,0:T(8,128)S(1)}, f32[144,128]{1,0:T(8,128)S(1)}, u32[]{:S(2)}, u32[]{:S(2)}) collective-permute-start(f32[144,128]{1,0:T(8,128)S(1)} %get-tuple-element.111.refs_0_), channel_id=1, source_target_pairs={{0,8},{8,0},{16,24},{24,16},{1,9},{9,1},{17,25},{25,17},{2,10},{10... | collective-permute-start | bytes 221192 | tf_op jit(solution)/shard_map/ppermute | solution.py:408
  26.9 2.1 %collective-permute-start.13 = (f32[144,128]{1,0:T(8,128)S(1)}, f32[144,128]{1,0:T(8,128)S(1)}, u32[]{:S(2)}, u32[]{:S(2)}) collective-permute-start(f32[144,128]{1,0:T(8,128)S(1)} %get-tuple-element.111.refs_0_), channel_id=1, source_target_pairs={{0,16},{8,24},{16,0},{24,8},{1,17},{9,25},{17,1},{25,9},{2,18},{10... | collective-permute-start | bytes 221192 | tf_op jit(solution)/shard_map/ppermute | solution.py:408
  30.4 2.0 %collective-permute-start.19 = (bf16[6,128,128]{2,1,0:T(8,128)(2,1)S(1)}, bf16[6,128,128]{2,1,0:T(8,128)(2,1)S(1)}, u32[]{:S(2)}, u32[]{:S(2)}) collective-permute-start(bf16[6,128,128]{2,1,0:T(8,128)(2,1)S(1)} %get-tuple-element.122), channel_id=1, source_target_pairs={{0,16},{8,24},{16,0},{24,8},{1,17},{9,25},{17,1},{25,9},{2,18},{10... | collective-permute-start | bytes 589832 | tf_op jit(solution)/shard_map/ppermute | solution.py:408
  34.8 4.8 %collective-permute-start.15 = (f32[144,128]{1,0:T(8,128)S(1)}, f32[144,128]{1,0:T(8,128)S(1)}, u32[]{:S(2)}, u32[]{:S(2)}) collective-permute-start(f32[144,128]{1,0:T(8,128)S(1)} %get-tuple-element.112.own_ref), channel_id=1, source_target_pairs={{0,1},{1,0},{2,3},{3,2},{4,5},{5,4},{6,7},{7,6},{8,9},{9,8},{10,11... | collective-permute-start | bytes 221192 | tf_op jit(solution)/shard_map/ppermute | solution.py:408
  41.5 3.8 %collective-permute-done.16.other_ref = f32[144,128]{1,0:T(8,128)S(1)} collective-permute-done((f32[144,128]{1,0:T(8,128)S(1)}, f32[144,128]{1,0:T(8,128)S(1)}, u32[]{:S(2)}, u32[]{:S(2)}) %collective-permute-start.16) | collective-permute-done | bytes 73760 | tf_op jit(solution)/shard_map/ppermute | solution.py:408
  45.7 2.0 %shard_map.63 = (f32[15,128,128]{2,1,0:T(8,128)S(1)}, bf16[8,128,128]{2,1,0:T(8,128)(2,1)S(1)}) custom-call(s32[32]{0:T(128)} %regime_ref.11, bf16[8,128,128]{2,1,0:T(8,128)(2,1)S(1)} %get-tuple-element.120.refs_0_, bf16[6,128,128]{2,1,0:T(8,128)(2,1)S(1)} %collective-permute-done.18.refs_1_, bf16[6,128,128]{2,1,0:T(8,128)(2,1)S(1)} %collective-permute-done.19.refs_2_, ...), custom_call_target="tpu_custom_call" | custom-call | flops 629145600 | bytes 9830400 | tf_op jit(solution)/shard_map/pallas_call | solution.py:478
  47.7 2.5 %collective-permute-done.17.far_ref = f32[16,128]{1,0:T(8,128)S(1)} collective-permute-done((f32[16,128]{1,0:T(8,128)S(1)}, f32[16,128]{1,0:T(8,128)S(1)}, u32[]{:S(2)}, u32[]{:S(2)}) %collective-permute-start.17) | collective-permute-done | bytes 8224 | tf_op jit(solution)/shard_map/ppermute | solution.py:408
  50.2 2.6 %shard_map.64 = (f32[32,16,128]{2,1,0:T(8,128)S(1)}, f32[32,16,128]{2,1,0:T(8,128)S(1)}, f32[8,16,128]{2,1,0:T(8,128)S(1)}, f32[144,128]{1,0:T(8,128)S(1)}) custom-call(s32[32]{0:T(128)} %regime_ref.11, f32[144,128]{1,0:T(8,128)S(1)} %get-tuple-element.116.before_ref, f32[16,128]{1,0:T(8,128)S(1)} %collective-permute-done.17.far_ref, ...), custom_call_target="tpu_custom_call" | custom-call | flops 209715200 | bytes 3276800 | tf_op jit(solution)/shard_map/pallas_call | solution.py:488
  54.3 2.0 %collective-permute-start.22 = (f32[144,128]{1,0:T(8,128)S(1)}, f32[144,128]{1,0:T(8,128)S(1)}, u32[]{:S(2)}, u32[]{:S(2)}) collective-permute-start(f32[144,128]{1,0:T(8,128)S(1)} %get-tuple-element.129.refs_0_), channel_id=1, source_target_pairs={{0,16},{8,24},{16,0},{24,8},{1,17},{9,25},{17,1},{25,9},{2,18},{10... | collective-permute-start | bytes 221192 | tf_op jit(solution)/shard_map/ppermute | solution.py:408
  59.1 2.4 %collective-permute-done.23.refs_3_ = f32[144,128]{1,0:T(8,128)S(1)} collective-permute-done((f32[144,128]{1,0:T(8,128)S(1)}, f32[144,128]{1,0:T(8,128)S(1)}, u32[]{:S(2)}, u32[]{:S(2)}) %collective-permute-start.23) | collective-permute-done | bytes 73760 | tf_op jit(solution)/shard_map/ppermute | solution.py:408
  64.0 4.1 %collective-permute-done.25.other_ref = f32[144,128]{1,0:T(8,128)S(1)} collective-permute-done((f32[144,128]{1,0:T(8,128)S(1)}, f32[144,128]{1,0:T(8,128)S(1)}, u32[]{:S(2)}, u32[]{:S(2)}) %collective-permute-start.25) | collective-permute-done | bytes 73760 | tf_op jit(solution)/shard_map/ppermute | solution.py:408
  69.3 3.5 %collective-permute-done.26.far_ref = f32[16,128]{1,0:T(8,128)S(1)} collective-permute-done((f32[16,128]{1,0:T(8,128)S(1)}, f32[16,128]{1,0:T(8,128)S(1)}, u32[]{:S(2)}, u32[]{:S(2)}) %collective-permute-start.26) | collective-permute-done | bytes 8224 | tf_op jit(solution)/shard_map/ppermute | solution.py:408
  74.4 2.8 %collective-permute-start.29 = (f32[32,4,128]{2,1,0:T(4,128)S(1)}, f32[32,4,128]{2,1,0:T(4,128)S(1)}, u32[]{:S(2)}, u32[]{:S(2)}) collective-permute-start(f32[32,4,128]{2,1,0:T(4,128)S(1)} %get-tuple-element.142), channel_id=1, source_target_pairs={{0,24},{8,16},{16,8},{24,0},{1,25},{9,17},{17,9},{25,1},{2,26},{10... | collective-permute-start | bytes 196616 | tf_op jit(solution)/shard_map/ppermute | solution.py:408
  (41 shorter events, 18.8 us)
Async XLA Ops:
  5.6 17.7 %collective-permute-start.6 = (bf16[6,128,128]{2,1,0:T(8,128)(2,1)S(1)}, bf16[6,128,128]{2,1,0:T(8,128)(2,1)S(1)}, u32[]{:S(2)}, u32[]{:S(2)}) collective-permute-start(bf16[6,128,128]{2,1,0:T(8,128)(2,1)S(1)} %get-tuple-element.93), channel_id=1, source_target_pairs={{0,8},{8,0},{16,24},{24,16},{1,9},{9,1},{17,25},{25,17},{2,10},{10... | collective-permute-start | bytes 589832 | tf_op jit(solution)/shard_map/ppermute | solution.py:408
  8.6 14.7 %collective-permute-start.7 = (bf16[6,128,128]{2,1,0:T(8,128)(2,1)S(1)}, bf16[6,128,128]{2,1,0:T(8,128)(2,1)S(1)}, u32[]{:S(2)}, u32[]{:S(2)}) collective-permute-start(bf16[6,128,128]{2,1,0:T(8,128)(2,1)S(1)} %get-tuple-element.94), channel_id=1, source_target_pairs={{0,16},{8,24},{16,0},{24,8},{1,17},{9,25},{17,1},{25,9},{2,18},{10... | collective-permute-start | bytes 589832 | tf_op jit(solution)/shard_map/ppermute | solution.py:408
  10.2 13.1 %collective-permute-start.8 = (bf16[6,128,128]{2,1,0:T(8,128)(2,1)S(1)}, bf16[6,128,128]{2,1,0:T(8,128)(2,1)S(1)}, u32[]{:S(2)}, u32[]{:S(2)}) collective-permute-start(bf16[6,128,128]{2,1,0:T(8,128)(2,1)S(1)} %get-tuple-element.95), channel_id=1, source_target_pairs={{0,24},{8,16},{16,8},{24,0},{1,25},{9,17},{17,9},{25,1},{2,26},{10... | collective-permute-start | bytes 589832 | tf_op jit(solution)/shard_map/ppermute | solution.py:408
  10.3 7.0 %collective-permute-start.9 = (f32[34,4,128]{2,1,0:T(4,128)S(1)}, f32[34,4,128]{2,1,0:T(4,128)S(1)}, u32[]{:S(2)}, u32[]{:S(2)}) collective-permute-start(f32[34,4,128]{2,1,0:T(4,128)S(1)} %get-tuple-element.107), channel_id=1, source_target_pairs={{0,8},{8,0},{16,24},{24,16},{1,9},{9,1},{17,25},{25,17},{2,10},{10... | collective-permute-start | bytes 208904 | tf_op jit(solution)/shard_map/ppermute | solution.py:408
  12.1 8.1 %collective-permute-start.10 = (f32[34,4,128]{2,1,0:T(4,128)S(1)}, f32[34,4,128]{2,1,0:T(4,128)S(1)}, u32[]{:S(2)}, u32[]{:S(2)}) collective-permute-start(f32[34,4,128]{2,1,0:T(4,128)S(1)} %get-tuple-element.108), channel_id=1, source_target_pairs={{0,16},{8,24},{16,0},{24,8},{1,17},{9,25},{17,1},{25,9},{2,18},{10... | collective-permute-start | bytes 208904 | tf_op jit(solution)/shard_map/ppermute | solution.py:408
  17.3 6.0 %collective-permute-start.11 = (f32[34,4,128]{2,1,0:T(4,128)S(1)}, f32[34,4,128]{2,1,0:T(4,128)S(1)}, u32[]{:S(2)}, u32[]{:S(2)}) collective-permute-start(f32[34,4,128]{2,1,0:T(4,128)S(1)} %get-tuple-element.109), channel_id=1, source_target_pairs={{0,24},{8,16},{16,8},{24,0},{1,25},{9,17},{17,9},{25,1},{2,26},{10... | collective-permute-start | bytes 208904 | tf_op jit(solution)/shard_map/ppermute | solution.py:408
  25.3 7.1 %collective-permute-start.12 = (f32[144,128]{1,0:T(8,128)S(1)}, f32[144,128]{1,0:T(8,128)S(1)}, u32[]{:S(2)}, u32[]{:S(2)}) collective-permute-start(f32[144,128]{1,0:T(8,128)S(1)} %get-tuple-element.111.refs_0_), channel_id=1, source_target_pairs={{0,8},{8,0},{16,24},{24,16},{1,9},{9,1},{17,25},{25,17},{2,10},{10... | collective-permute-start | bytes 221192 | tf_op jit(solution)/shard_map/ppermute | solution.py:408
  26.9 5.9 %collective-permute-start.13 = (f32[144,128]{1,0:T(8,128)S(1)}, f32[144,128]{1,0:T(8,128)S(1)}, u32[]{:S(2)}, u32[]{:S(2)}) collective-permute-start(f32[144,128]{1,0:T(8,128)S(1)} %get-tuple-element.111.refs_0_), channel_id=1, source_target_pairs={{0,16},{8,24},{16,0},{24,8},{1,17},{9,25},{17,1},{25,9},{2,18},{10... | collective-permute-start | bytes 221192 | tf_op jit(solution)/shard_map/ppermute | solution.py:408
  29.0 5.3 %collective-permute-start.14 = (f32[144,128]{1,0:T(8,128)S(1)}, f32[144,128]{1,0:T(8,128)S(1)}, u32[]{:S(2)}, u32[]{:S(2)}) collective-permute-start(f32[144,128]{1,0:T(8,128)S(1)} %get-tuple-element.111.refs_0_), channel_id=1, source_target_pairs={{0,24},{8,16},{16,8},{24,0},{1,25},{9,17},{17,9},{25,1},{2,26},{10... | collective-permute-start | bytes 221192 | tf_op jit(solution)/shard_map/ppermute | solution.py:408
  29.1 16.5 %collective-permute-start.18 = (bf16[6,128,128]{2,1,0:T(8,128)(2,1)S(1)}, bf16[6,128,128]{2,1,0:T(8,128)(2,1)S(1)}, u32[]{:S(2)}, u32[]{:S(2)}) collective-permute-start(bf16[6,128,128]{2,1,0:T(8,128)(2,1)S(1)} %get-tuple-element.121), channel_id=1, source_target_pairs={{0,8},{8,0},{16,24},{24,16},{1,9},{9,1},{17,25},{25,17},{2,10},{10... | collective-permute-start | bytes 589832 | tf_op jit(solution)/shard_map/ppermute | solution.py:408
  30.4 15.2 %collective-permute-start.19 = (bf16[6,128,128]{2,1,0:T(8,128)(2,1)S(1)}, bf16[6,128,128]{2,1,0:T(8,128)(2,1)S(1)}, u32[]{:S(2)}, u32[]{:S(2)}) collective-permute-start(bf16[6,128,128]{2,1,0:T(8,128)(2,1)S(1)} %get-tuple-element.122), channel_id=1, source_target_pairs={{0,16},{8,24},{16,0},{24,8},{1,17},{9,25},{17,1},{25,9},{2,18},{10... | collective-permute-start | bytes 589832 | tf_op jit(solution)/shard_map/ppermute | solution.py:408
  32.5 13.2 %collective-permute-start.20 = (bf16[6,128,128]{2,1,0:T(8,128)(2,1)S(1)}, bf16[6,128,128]{2,1,0:T(8,128)(2,1)S(1)}, u32[]{:S(2)}, u32[]{:S(2)}) collective-permute-start(bf16[6,128,128]{2,1,0:T(8,128)(2,1)S(1)} %get-tuple-element.123), channel_id=1, source_target_pairs={{0,24},{8,16},{16,8},{24,0},{1,25},{9,17},{17,9},{25,1},{2,26},{10... | collective-permute-start | bytes 589832 | tf_op jit(solution)/shard_map/ppermute | solution.py:408
  34.8 5.7 %collective-permute-start.15 = (f32[144,128]{1,0:T(8,128)S(1)}, f32[144,128]{1,0:T(8,128)S(1)}, u32[]{:S(2)}, u32[]{:S(2)}) collective-permute-start(f32[144,128]{1,0:T(8,128)S(1)} %get-tuple-element.112.own_ref), channel_id=1, source_target_pairs={{0,1},{1,0},{2,3},{3,2},{4,5},{5,4},{6,7},{7,6},{8,9},{9,8},{10,11... | collective-permute-start | bytes 221192 | tf_op jit(solution)/shard_map/ppermute | solution.py:408
  40.8 4.6 %collective-permute-start.16 = (f32[144,128]{1,0:T(8,128)S(1)}, f32[144,128]{1,0:T(8,128)S(1)}, u32[]{:S(2)}, u32[]{:S(2)}) collective-permute-start(f32[144,128]{1,0:T(8,128)S(1)} %get-tuple-element.114.own_ref), channel_id=1, source_target_pairs={{0,2},{1,3},{2,0},{3,1},{4,6},{5,7},{6,4},{7,5},{8,10},{9,11},{10,... | collective-permute-start | bytes 221192 | tf_op jit(solution)/shard_map/ppermute | solution.py:408
  45.6 4.6 %collective-permute-start.17 = (f32[16,128]{1,0:T(8,128)S(1)}, f32[16,128]{1,0:T(8,128)S(1)}, u32[]{:S(2)}, u32[]{:S(2)}) collective-permute-start(f32[16,128]{1,0:T(8,128)S(1)} %get-tuple-element.117), channel_id=1, source_target_pairs={{0,4},{1,5},{2,6},{3,7},{4,0},{5,1},{6,2},{7,3},{8,12},{9,13},{10,... | collective-permute-start | bytes 24584 | tf_op jit(solution)/shard_map/ppermute | solution.py:408
  52.8 5.2 %collective-permute-start.21 = (f32[144,128]{1,0:T(8,128)S(1)}, f32[144,128]{1,0:T(8,128)S(1)}, u32[]{:S(2)}, u32[]{:S(2)}) collective-permute-start(f32[144,128]{1,0:T(8,128)S(1)} %get-tuple-element.129.refs_0_), channel_id=1, source_target_pairs={{0,8},{8,0},{16,24},{24,16},{1,9},{9,1},{17,25},{25,17},{2,10},{10... | collective-permute-start | bytes 221192 | tf_op jit(solution)/shard_map/ppermute | solution.py:408
  54.3 4.8 %collective-permute-start.22 = (f32[144,128]{1,0:T(8,128)S(1)}, f32[144,128]{1,0:T(8,128)S(1)}, u32[]{:S(2)}, u32[]{:S(2)}) collective-permute-start(f32[144,128]{1,0:T(8,128)S(1)} %get-tuple-element.129.refs_0_), channel_id=1, source_target_pairs={{0,16},{8,24},{16,0},{24,8},{1,17},{9,25},{17,1},{25,9},{2,18},{10... | collective-permute-start | bytes 221192 | tf_op jit(solution)/shard_map/ppermute | solution.py:408
  56.3 5.3 %collective-permute-start.23 = (f32[144,128]{1,0:T(8,128)S(1)}, f32[144,128]{1,0:T(8,128)S(1)}, u32[]{:S(2)}, u32[]{:S(2)}) collective-permute-start(f32[144,128]{1,0:T(8,128)S(1)} %get-tuple-element.129.refs_0_), channel_id=1, source_target_pairs={{0,24},{8,16},{16,8},{24,0},{1,25},{9,17},{17,9},{25,1},{2,26},{10... | collective-permute-start | bytes 221192 | tf_op jit(solution)/shard_map/ppermute | solution.py:408
  62.0 1.3 %collective-permute-start.24 = (f32[144,128]{1,0:T(8,128)S(1)}, f32[144,128]{1,0:T(8,128)S(1)}, u32[]{:S(2)}, u32[]{:S(2)}) collective-permute-start(f32[144,128]{1,0:T(8,128)S(1)} %get-tuple-element.130.own_ref), channel_id=1, source_target_pairs={{0,1},{1,0},{2,3},{3,2},{4,5},{5,4},{6,7},{7,6},{8,9},{9,8},{10,11... | collective-permute-start | bytes 221192 | tf_op jit(solution)/shard_map/ppermute | solution.py:408
  63.6 4.4 %collective-permute-start.25 = (f32[144,128]{1,0:T(8,128)S(1)}, f32[144,128]{1,0:T(8,128)S(1)}, u32[]{:S(2)}, u32[]{:S(2)}) collective-permute-start(f32[144,128]{1,0:T(8,128)S(1)} %get-tuple-element.132.own_ref), channel_id=1, source_target_pairs={{0,2},{1,3},{2,0},{3,1},{4,6},{5,7},{6,4},{7,5},{8,10},{9,11},{10,... | collective-permute-start | bytes 221192 | tf_op jit(solution)/shard_map/ppermute | solution.py:408
  68.2 4.6 %collective-permute-start.26 = (f32[16,128]{1,0:T(8,128)S(1)}, f32[16,128]{1,0:T(8,128)S(1)}, u32[]{:S(2)}, u32[]{:S(2)}) collective-permute-start(f32[16,128]{1,0:T(8,128)S(1)} %get-tuple-element.135), channel_id=1, source_target_pairs={{0,4},{1,5},{2,6},{3,7},{4,0},{5,1},{6,2},{7,3},{8,12},{9,13},{10,... | collective-permute-start | bytes 24584 | tf_op jit(solution)/shard_map/ppermute | solution.py:408
  73.7 4.3 %collective-permute-start.27 = (f32[32,4,128]{2,1,0:T(4,128)S(1)}, f32[32,4,128]{2,1,0:T(4,128)S(1)}, u32[]{:S(2)}, u32[]{:S(2)}) collective-permute-start(f32[32,4,128]{2,1,0:T(4,128)S(1)} %get-tuple-element.140), channel_id=1, source_target_pairs={{0,8},{8,0},{16,24},{24,16},{1,9},{9,1},{17,25},{25,17},{2,10},{10... | collective-permute-start | bytes 196616 | tf_op jit(solution)/shard_map/ppermute | solution.py:408
  74.4 4.3 %collective-permute-start.28 = (f32[32,4,128]{2,1,0:T(4,128)S(1)}, f32[32,4,128]{2,1,0:T(4,128)S(1)}, u32[]{:S(2)}, u32[]{:S(2)}) collective-permute-start(f32[32,4,128]{2,1,0:T(4,128)S(1)} %get-tuple-element.141), channel_id=1, source_target_pairs={{0,16},{8,24},{16,0},{24,8},{1,17},{9,25},{17,1},{25,9},{2,18},{10... | collective-permute-start | bytes 196616 | tf_op jit(solution)/shard_map/ppermute | solution.py:408
  74.4 5.2 %collective-permute-start.29 = (f32[32,4,128]{2,1,0:T(4,128)S(1)}, f32[32,4,128]{2,1,0:T(4,128)S(1)}, u32[]{:S(2)}, u32[]{:S(2)}) collective-permute-start(f32[32,4,128]{2,1,0:T(4,128)S(1)} %get-tuple-element.142), channel_id=1, source_target_pairs={{0,24},{8,16},{16,8},{24,0},{1,25},{9,17},{17,9},{25,1},{2,26},{10... | collective-permute-start | bytes 196616 | tf_op jit(solution)/shard_map/ppermute | solution.py:408

commit v4 on v3

--- a/solution.py
+++ b/solution.py
@@ -251,16 +251,8 @@
     total_ref[...] = joined(states)
 
 
-def gain_levels(charts):
-    found = [charts]
-    while len(charts) > 1:
-        charts = [times(charts[i], charts[i + 1]) for i in range(0, len(charts), 2)]
-        found.append(charts)
-    return found
-
-
 def backward_kernel(plan, regime_ref, *refs):
-    mats, (level_ref, picked_ref) = (refs[:-2], refs[-2:])
+    mats, (strand_ref, picked_ref) = (refs[:-2], refs[-2:])
     weights, states = ([], [])
     for b in range(plan.share):
         picked = picked_matrix(plan, regime_ref, mats, b)
@@ -270,11 +262,8 @@
     for b, t in plan.backward_steps():
         if t % plan.dwell < plan.dwell - 1:
             states[b] = times_rows(states[b], weights[b])
-    at = 0
-    for level in gain_levels(states[::-1]):
-        for chart in level:
-            level_ref[at] = chart
-            at += 1
+    for b in range(plan.share):
+        strand_ref[b] = states[plan.share - 1 - b]
 
 
 def forward_running_kernel(strand_ref, running_ref):
@@ -283,9 +272,9 @@
         running_ref[s] = chart
 
 
-def backward_running_kernel(level_ref, offset_ref, running_ref):
+def backward_running_kernel(strand_ref, offset_ref, running_ref):
     charts = [
-        jnp.concatenate([level_ref[s], offset_ref[s]], axis=0)
+        jnp.concatenate([strand_ref[s], offset_ref[s]], axis=0)
         for s in range(offset_ref.shape[0] - 1)
     ]
     for s, chart in enumerate(running(charts)):
@@ -315,29 +304,43 @@
     return jnp.logical_not(second) if reverse else second
 
 
-def pair_kernel(mask, reverse, last, own_ref, other_ref, before_ref, joined_ref, after_ref):
-    width = own_ref.shape[1]
+def pair_kernel(mask, reverse, own_ref, other_ref, before_ref, joined_ref, after_ref, *half_ref):
     own, other, before = (own_ref[...], other_ref[...], before_ref[...])
     second = is_second(mask, reverse)
-    earlier, later = (jnp.where(second, other, own), jnp.where(second, own, other))
-    if last:
-        joined_ref[...] = apply(earlier[width:], later)
-    else:
-        joined_ref[...] = compose(earlier, later)
+    joined = compose(jnp.where(second, other, own), jnp.where(second, own, other))
+    joined_ref[...] = joined
     after_ref[...] = jnp.where(second, compose(other, before), before)
-
-
-def entering(far_ref, before_ref, running_ref, reverse):
-    far = far_ref[...]
-    second = is_second(lax.axis_size("tm") // 2, reverse)
-    state = apply(jnp.where(second, far, jnp.zeros_like(far)), before_ref[...])
+    if half_ref:
+        rows = joined.shape[0] // 2
+        half_ref[0][...] = jnp.where(is_second(1, False), joined[rows:], joined[:rows])
+
+
+def entering(found, running_ref, stride, reverse):
+    before_ref, mine_ref, theirs_ref, half_ref, rest_ref = found
+    odd = is_second(1, False)
+    mine, theirs, half, rest = (mine_ref[...], theirs_ref[...], half_ref[...], rest_ref[...])
+    across = jnp.concatenate([jnp.where(odd, rest, half), jnp.where(odd, half, rest)], axis=0)
+    peers = [mine, jnp.where(odd, theirs, mine), jnp.where(odd, mine, theirs), across]
+    low, high = (is_second(stride, False), is_second(2 * stride, False))
+    quarter = low.astype(jnp.int32) + 2 * high.astype(jnp.int32)
+    width = mine.shape[1]
+    state = None
+    for at in (3, 2, 1) if reverse else (0, 1, 2):
+        chart = choose(quarter ^ at, peers)
+        ahead = quarter < at if reverse else quarter > at
+        if state is None:
+            state = jnp.where(ahead, chart[width:], jnp.zeros_like(chart[width:]))
+        else:
+            state = jnp.where(ahead, apply(state, chart), state)
+    state = apply(state, before_ref[...])
     return [state] + [apply(state, running_ref[s]) for s in range(running_ref.shape[0])]
 
 
-def filter_kernel(plan, regime_ref, before_ref, far_ref, running_ref, fpick_ref, *refs):
+def filter_kernel(plan, stride, regime_ref, *refs):
+    found, (running_ref, fpick_ref), refs = (refs[:5], refs[5:7], refs[7:])
     meas, refs = (refs[: plan.groups], refs[plan.groups :])
-    level_ref, bpick_ref, filtered_ref, pushed_ref, offset_ref, total_ref = refs
-    states = entering(far_ref, before_ref, running_ref, False)
+    strand_ref, bpick_ref, filtered_ref, pushed_ref, offset_ref, total_ref = refs
+    states = entering(found, running_ref, stride, False)
     gains = [plan.gain_row(regime_ref, meas, b) for b in range(plan.share)]
     weights = [doubled(fpick_ref[b]) for b in range(plan.share)]
     pushes = {}
@@ -355,22 +358,19 @@
     states = states[::-1]
     for b in range(plan.share):
         offset_ref[b] = states[b]
-    at = 0
+    mats = [strand_ref[b] for b in range(plan.share)]
     while len(states) > 1:
-        count = len(states)
-        states = [
-            times(states[i], level_ref[at + i + 1]) + states[i + 1] for i in range(0, count, 2)
-        ]
-        at += count
-    total_ref[0 : plan.width] = level_ref[at]
+        pairs = range(0, len(states), 2)
+        states = [times(states[i], mats[i + 1]) + states[i + 1] for i in pairs]
+        mats = [times(mats[i], mats[i + 1]) for i in pairs]
+    total_ref[0 : plan.width] = mats[0]
     total_ref[plan.width :] = states[0]
 
 
-def smooth_kernel(
-    plan, before_ref, far_ref, running_ref, picked_ref, filtered_ref, pushed_ref, *outs
-):
+def smooth_kernel(plan, stride, *refs):
+    found, (running_ref, picked_ref, filtered_ref, pushed_ref), outs = (refs[:5], refs[5:9], refs[9:])
     tracks = plan.tracks
-    states = entering(far_ref, before_ref, running_ref, True)[::-1]
+    states = entering(found, running_ref, stride, True)[::-1]
     weights = [doubled(picked_ref[b]) for b in range(plan.share)]
     for b, t in plan.backward_steps():
         value = filtered_ref[t] + states[b]
@@ -381,10 +381,16 @@
 
 
 def collect_kernel(plan, *refs):
-    parts, out_ref = (refs[: plan.groups], refs[plan.groups])
+    parts, out_ref, sem = (refs[: plan.groups], refs[plan.groups], refs[plan.groups + 1])
+    copies = []
     for j in range(plan.groups):
         first = pl.multiple_of((lax.axis_index("track") ^ j) * plan.span, plan.span)
-        out_ref[pl.ds(first, plan.span)] = parts[j][...]
+        rows = out_ref.at[pl.ds(first, plan.span)]
+        copies.append(pltpu.make_async_copy(parts[j], rows, sem.at[j]))
+    for copy in copies:
+        copy.start()
+    for copy in copies:
+        copy.wait()
 
 
 def body(observations, dynamics, smoother_gain, gains, regime):
@@ -395,6 +401,8 @@
     plan = Plan(groups, blocks // groups, length // blocks, owned, tracks, width)
     chart = shape((width + plan.rows, width))
     offset = shape((plan.rows, width))
+    half_chart = shape(((width + plan.rows) // 2, width))
+    top = spans // 4
     share = plan.share
     block_mats = lambda count: shape((count, width, width), BF16)
     unit = width * width * width
@@ -461,50 +469,56 @@
             20 * unit,
         )(*maps)
         stride = 1
-        while 2 * stride < spans:
-            last = 4 * stride >= spans
-            total, before = call(
-                functools.partial(pair_kernel, stride, reverse, last),
-                [offset if last else chart, chart],
+        while 4 * stride < spans:
+            last = 8 * stride >= spans
+            other = swap(total, stride, "tm")
+            total, before, *half = call(
+                functools.partial(pair_kernel, stride, reverse),
+                [chart, chart] + [half_chart] * last,
                 [VMEM] * 3,
                 20 * unit,
-            )(total, swap(total, stride, "tm"), before)
+            )(total, other, before)
             stride *= 2
-        total = total[-plan.rows :] if stride == 1 else total
-        return before, swap(total, stride, "tm")
-
-    late = [swap(value, j + 1, "track") for j, value in enumerate(late)]
-    levels = 2 * share - 1
-    level, bpick = call(
+        near = [(at, at ^ (stride << (at & 1))) for at in range(spans)]
+        mine = lax.ppermute(total, "tm", near)
+        half = swap(half[0], 3 * stride, "tm")
+        theirs = swap(mine, 1, "tm")
+        return before, mine, theirs, half, swap(half, 1, "tm")
+
+    for j, value in enumerate(late):
+        late[j] = swap(value, j + 1, "track")
+    bstrand, bpick = call(
         functools.partial(backward_kernel, plan),
-        [shape((levels, width, width)), block_mats(share)],
+        [shape((share, width, width)), block_mats(share)],
         [SMEM] + [VMEM] * (2 * groups - 1),
         300 * unit,
     )(regime, gown, *late, *further[peers:])
 
-    before, far = across(total, False)
+    found = across(total, False)
     runs = [shape((share - 1,) + chart.shape)]
     (frun,) = call(forward_running_kernel, runs, [VMEM], 60 * unit)(fstrand)
     filtered, pushed, offsets, total = call(
-        functools.partial(filter_kernel, plan),
+        functools.partial(filter_kernel, plan, top),
         [shape((plan.span, plan.rows, width))] * 2 + [shape((share,) + offset.shape), chart],
-        [SMEM] + [VMEM] * (6 + groups),
+        [SMEM] + [VMEM] * (9 + groups),
         100 * unit,
-    )(regime, before, far, frun, fpick, *meas, level, bpick)
-
-    before, far = across(total, True)
-    (brun,) = call(backward_running_kernel, runs, [VMEM] * 2, 60 * unit)(level, offsets)
+    )(regime, *found, frun, fpick, *meas, bstrand, bpick)
+
+    found = across(total, True)
+    (brun,) = call(backward_running_kernel, runs, [VMEM] * 2, 60 * unit)(bstrand, offsets)
     outs = call(
-        functools.partial(smooth_kernel, plan),
+        functools.partial(smooth_kernel, plan, top),
         [shape((plan.span, tracks, width))] * groups,
-        [VMEM] * 6,
+        [VMEM] * 9,
         50 * unit,
-    )(before, far, brun, bpick, filtered, pushed)
+    )(*found, brun, bpick, filtered, pushed)
     return call(
         functools.partial(collect_kernel, plan),
         [shape((length, tracks, width))],
         [VMEM] * groups,
         unit,
+        [sem((groups,))],
+        [HBM],
     )(*exchange(outs))[0]
 
 

time: 80.6 us -> 78.8 us (0.978)
  waiting for transfers between devices: 31.7 us -> 26.7 us
  starting transfers between devices: 31.5 us -> 34.8 us
    ppermute x24 -> x26, waiting for transfers between devices: 31.7 us -> 16.8 us  [swap(): return lax.ppermute(value, axis, pairs)]
    ppermute x0 -> x2, waiting for transfers between devices: none -> 9.83 us  [across(): mine = lax.ppermute(total, 'tm', near)]
    ppermute x24 -> x26, starting transfers between devices: 31.5 us -> 34.5 us  [swap(): return lax.ppermute(value, axis, pairs)]
    pallas_call x8 -> x6, Pallas kernels: 6.92 us -> 6.85 us  [the longest x1 3.19 us: body(): call(functools.partial(filter_kernel, plan, top), [shape((plan.span, plan...]
  transfers between devices with their start and end apart: 24 -> 28, of which waited for: 15 -> 13; matrix products, arithmetic and copies ran while one was open for 0% -> 0% of each run, Pallas kernels for 5% -> 4%
where the time goes in v4:
time: 78.8 us; the launch traced here: 78.5 us
  starting transfers between devices  34.8 us (44%)
  waiting for transfers between devices  26.7 us (34%)
  Pallas kernels  16.2 us (21%)
  between operations  0.81 us (1%)
    ppermute x26, starting transfers between devices, swap(): return lax.ppermute(value, axis, pairs)  34.5 us
    ppermute x26, waiting for transfers between devices, swap(): return lax.ppermute(value, axis, pairs)  16.8 us
    ppermute x2, waiting for transfers between devices, across(): mine = lax.ppermute(total, 'tm', near)  9.83 us
    pallas_call x1, Pallas kernels, body(): call(functools.partial(filter_kernel, plan, top), [shape((plan.span, plan...  3.19 us
    pallas_call x1, Pallas kernels, body(): call(functools.partial(forward_kernel, plan), [chart, shape((share,) + ch...  2 us
    pallas_call x1, Pallas kernels, body(): call(functools.partial(measured_kernel, plan), [shape((plan.span + plan.e...  1.74 us
    pallas_call x1, Pallas kernels, body(): call(functools.partial(second_gather_kernel, plan), [block_mats(share)] *...  1.62 us
  transfers between devices with their start and end apart: 28, of which 13 were waited for; matrix products, arithmetic and copies ran while one was open for 0% of the time, Pallas kernels for 4%

profile of v4, /device:TPU:0, one launch (start us, length us, event | category | flops | bytes accessed | tf_op | source)
XLA Modules:
  0.0 78.5 jit_solution(11443050587504727410)
XLA Ops:
  0.0 1.7 %shard_map.57 = (f32[34,4,128]{2,1,0:T(4,128)S(1)}, f32[34,4,128]{2,1,0:T(4,128)S(1)}, f32[34,4,128]{2,1,0:T(4,128)S(1)}, f32[34,4,128]{2,1,0:T(4,128)S(1)}, s32[1]{0:T(128)}) custom-call(s32[32]{0:T(128)} %regime_ref.11, bf16[64,128]{1,0:T(8,128)(2,1)} %gains_ref.1, f32[128,4,128]{2,1,0:T(4,128)} %obs_ref.1), custom_call_target="tpu_custom_call" | custom-call | flops 2097152 | bytes 32768 | tf_op jit(solution)/shard_map/pallas_call | solution.py:428
  2.4 1.6 %shard_map.56 = (bf16[6,128,128]{2,1,0:T(8,128)(2,1)S(1)}, bf16[6,128,128]{2,1,0:T(8,128)(2,1)S(1)}, bf16[6,128,128]{2,1,0:T(8,128)(2,1)S(1)}, bf16[2,128,128]{2...) custom-call(s32[32]{0:T(128)} %regime_ref.11, bf16[64,128,128]{2,1,0:T(8,128)(2,1)} %table_ref.1), custom_call_target="tpu_custom_call" | custom-call | flops 2097152 | bytes 32768 | tf_op jit(solution)/shard_map/pallas_call | solution.py:424
  4.0 1.6 %shard_map.55 = (bf16[8,128,128]{2,1,0:T(8,128)(2,1)S(1)}, bf16[8,128,128]{2,1,0:T(8,128)(2,1)S(1)}, bf16[6,128,128]{2,1,0:T(8,128)(2,1)S(1)}, bf16[6,128,128]{2...) custom-call(s32[32]{0:T(128)} %regime_ref.11, ...), custom_call_target="tpu_custom_call" | custom-call | flops 2097152 | bytes 32768 | tf_op jit(solution)/shard_map/pallas_call | solution.py:437
  5.6 3.0 %collective-permute-start.6 = (bf16[6,128,128]{2,1,0:T(8,128)(2,1)S(1)}, bf16[6,128,128]{2,1,0:T(8,128)(2,1)S(1)}, u32[]{:S(2)}, u32[]{:S(2)}) collective-permute-start(bf16[6,128,128]{2,1,0:T(8,128)(2,1)S(1)} %get-tuple-element.91), channel_id=1, source_target_pairs={{0,8},{8,0},{16,24},{24,16},{1,9},{9,1},{17,25},{25,17},{2,10},{10... | collective-permute-start | bytes 589832 | tf_op jit(solution)/shard_map/ppermute | solution.py:416
  8.6 1.6 %collective-permute-start.7 = (bf16[6,128,128]{2,1,0:T(8,128)(2,1)S(1)}, bf16[6,128,128]{2,1,0:T(8,128)(2,1)S(1)}, u32[]{:S(2)}, u32[]{:S(2)}) collective-permute-start(bf16[6,128,128]{2,1,0:T(8,128)(2,1)S(1)} %get-tuple-element.92), channel_id=1, source_target_pairs={{0,16},{8,24},{16,0},{24,8},{1,17},{9,25},{17,1},{25,9},{2,18},{10... | collective-permute-start | bytes 589832 | tf_op jit(solution)/shard_map/ppermute | solution.py:416
  10.3 1.8 %collective-permute-start.9 = (f32[34,4,128]{2,1,0:T(4,128)S(1)}, f32[34,4,128]{2,1,0:T(4,128)S(1)}, u32[]{:S(2)}, u32[]{:S(2)}) collective-permute-start(f32[34,4,128]{2,1,0:T(4,128)S(1)} %get-tuple-element.105), channel_id=1, source_target_pairs={{0,8},{8,0},{16,24},{24,16},{1,9},{9,1},{17,25},{25,17},{2,10},{10... | collective-permute-start | bytes 208904 | tf_op jit(solution)/shard_map/ppermute | solution.py:416
  12.1 1.6 %collective-permute-start.10 = (f32[34,4,128]{2,1,0:T(4,128)S(1)}, f32[34,4,128]{2,1,0:T(4,128)S(1)}, u32[]{:S(2)}, u32[]{:S(2)}) collective-permute-start(f32[34,4,128]{2,1,0:T(4,128)S(1)} %get-tuple-element.106), channel_id=1, source_target_pairs={{0,16},{8,24},{16,0},{24,8},{1,17},{9,25},{17,1},{25,9},{2,18},{10... | collective-permute-start | bytes 208904 | tf_op jit(solution)/shard_map/ppermute | solution.py:416
  13.7 3.6 %collective-permute-done.9.refs_8_ = f32[34,4,128]{2,1,0:T(4,128)S(1)} collective-permute-done((f32[34,4,128]{2,1,0:T(4,128)S(1)}, f32[34,4,128]{2,1,0:T(4,128)S(1)}, u32[]{:S(2)}, u32[]{:S(2)}) %collective-permute-start.9) | collective-permute-done | bytes 69664 | tf_op jit(solution)/shard_map/ppermute | solution.py:416
  17.3 3.0 %collective-permute-start.11 = (f32[34,4,128]{2,1,0:T(4,128)S(1)}, f32[34,4,128]{2,1,0:T(4,128)S(1)}, u32[]{:S(2)}, u32[]{:S(2)}) collective-permute-start(f32[34,4,128]{2,1,0:T(4,128)S(1)} %get-tuple-element.107), channel_id=1, source_target_pairs={{0,24},{8,16},{16,8},{24,0},{1,25},{9,17},{17,9},{25,1},{2,26},{10... | collective-permute-start | bytes 208904 | tf_op jit(solution)/shard_map/ppermute | solution.py:416
  20.3 3.0 %collective-permute-done.11.refs_10_ = f32[34,4,128]{2,1,0:T(4,128)S(1)} collective-permute-done((f32[34,4,128]{2,1,0:T(4,128)S(1)}, f32[34,4,128]{2,1,0:T(4,128)S(1)}, u32[]{:S(2)}, u32[]{:S(2)}) %collective-permute-start.11) | collective-permute-done | bytes 69664 | tf_op jit(solution)/shard_map/ppermute | solution.py:416
  23.3 2.0 %shard_map.58 = (f32[144,128]{1,0:T(8,128)S(1)}, f32[8,144,128]{2,1,0:T(8,128)S(1)}, bf16[8,128,128]{2,1,0:T(8,128)(2,1)S(1)}) custom-call(s32[32]{0:T(128)} %regime_ref.11, bf16[8,128,128]{2,1,0:T(8,128)(2,1)S(1)} %get-tuple-element.90.refs_0_, bf16[6,128,128]{2,1,0:T(8,128)(2,1)S(1)} %collective-permute-done.6.refs_1_, ...), custom_call_target="tpu_custom_call" | custom-call | flops 838860800 | bytes 13107200 | tf_op jit(solution)/shard_map/pallas_call | solution.py:451
  25.3 3.1 %collective-permute-start.14 = (f32[144,128]{1,0:T(8,128)S(1)}, f32[144,128]{1,0:T(8,128)S(1)}, u32[]{:S(2)}, u32[]{:S(2)}) collective-permute-start(f32[144,128]{1,0:T(8,128)S(1)} %get-tuple-element.109.refs_0_), channel_id=1, source_target_pairs={{0,24},{8,16},{16,8},{24,0},{1,25},{9,17},{17,9},{25,1},{2,26},{10... | collective-permute-start | bytes 221192 | tf_op jit(solution)/shard_map/ppermute | solution.py:416
  29.1 1.3 %collective-permute-start.20 = (bf16[6,128,128]{2,1,0:T(8,128)(2,1)S(1)}, bf16[6,128,128]{2,1,0:T(8,128)(2,1)S(1)}, u32[]{:S(2)}, u32[]{:S(2)}) collective-permute-start(bf16[6,128,128]{2,1,0:T(8,128)(2,1)S(1)} %get-tuple-element.118), channel_id=1, source_target_pairs={{0,8},{8,0},{16,24},{24,16},{1,9},{9,1},{17,25},{25,17},{2,10},{10... | collective-permute-start | bytes 589832 | tf_op jit(solution)/shard_map/ppermute | solution.py:416
  30.4 2.0 %collective-permute-start.21 = (bf16[6,128,128]{2,1,0:T(8,128)(2,1)S(1)}, bf16[6,128,128]{2,1,0:T(8,128)(2,1)S(1)}, u32[]{:S(2)}, u32[]{:S(2)}) collective-permute-start(bf16[6,128,128]{2,1,0:T(8,128)(2,1)S(1)} %get-tuple-element.119), channel_id=1, source_target_pairs={{0,16},{8,24},{16,0},{24,8},{1,17},{9,25},{17,1},{25,9},{2,18},{10... | collective-permute-start | bytes 589832 | tf_op jit(solution)/shard_map/ppermute | solution.py:416
  34.2 5.0 %collective-permute-start.15 = (f32[144,128]{1,0:T(8,128)S(1)}, f32[144,128]{1,0:T(8,128)S(1)}, u32[]{:S(2)}, u32[]{:S(2)}) collective-permute-start(f32[144,128]{1,0:T(8,128)S(1)} %get-tuple-element.110.own_ref), channel_id=1, source_target_pairs={{0,1},{1,0},{2,3},{3,2},{4,5},{5,4},{6,7},{7,6},{8,9},{9,8},{10,11... | collective-permute-start | bytes 221192 | tf_op jit(solution)/shard_map/ppermute | solution.py:416
  41.6 4.8 %collective-permute-done.16.refs_1_ = f32[144,128]{1,0:T(8,128)S(1)} collective-permute-done((f32[144,128]{1,0:T(8,128)S(1)}, f32[144,128]{1,0:T(8,128)S(1)}, u32[]{:S(2)}, u32[]{:S(2)}) %collective-permute-start.16) | collective-permute-done | bytes 73760 | tf_op jit(solution)/shard_map/ppermute | solution.py:483
  47.6 1.4 %shard_map.62 = (f32[8,128,128]{2,1,0:T(8,128)S(1)}, bf16[8,128,128]{2,1,0:T(8,128)(2,1)S(1)}) custom-call(s32[32]{0:T(128)} %regime_ref.11, bf16[8,128,128]{2,1,0:T(8,128)(2,1)S(1)} %get-tuple-element.117.refs_0_, bf16[6,128,128]{2,1,0:T(8,128)(2,1)S(1)} %collective-permute-done.20.refs_1_, bf16[6,128,128]{2,1,0:T(8,128)(2,1)S(1)} %collective-permute-done.21.refs_2_, ...), custom_call_target="tpu_custom_call" | custom-call | flops 629145600 | bytes 9830400 | tf_op jit(solution)/shard_map/pallas_call | solution.py:490
  49.1 3.2 %shard_map.63 = (f32[32,16,128]{2,1,0:T(8,128)S(1)}, f32[32,16,128]{2,1,0:T(8,128)S(1)}, f32[8,16,128]{2,1,0:T(8,128)S(1)}, f32[144,128]{1,0:T(8,128)S(1)}) custom-call(s32[32]{0:T(128)} %regime_ref.11, f32[144,128]{1,0:T(8,128)S(1)} %get-tuple-element.112.refs_0_, f32[144,128]{1,0:T(8,128)S(1)} %collective-permute-done.16.refs_1_, ...), custom_call_target="tpu_custom_call" | custom-call | flops 209715200 | bytes 3276800 | tf_op jit(solution)/shard_map/pallas_call | solution.py:500
  52.3 2.3 %collective-permute-start.25 = (f32[144,128]{1,0:T(8,128)S(1)}, f32[144,128]{1,0:T(8,128)S(1)}, u32[]{:S(2)}, u32[]{:S(2)}) collective-permute-start(f32[144,128]{1,0:T(8,128)S(1)} %get-tuple-element.126.refs_0_), channel_id=1, source_target_pairs={{0,24},{8,16},{16,8},{24,0},{1,25},{9,17},{17,9},{25,1},{2,26},{10... | collective-permute-start | bytes 221192 | tf_op jit(solution)/shard_map/ppermute | solution.py:416
  55.8 1.8 %collective-permute-done.25.refs_3_ = f32[144,128]{1,0:T(8,128)S(1)} collective-permute-done((f32[144,128]{1,0:T(8,128)S(1)}, f32[144,128]{1,0:T(8,128)S(1)}, u32[]{:S(2)}, u32[]{:S(2)}) %collective-permute-start.25) | collective-permute-done | bytes 73760 | tf_op jit(solution)/shard_map/ppermute | solution.py:416
  57.7 1.5 %collective-permute-done.24.refs_2_ = f32[144,128]{1,0:T(8,128)S(1)} collective-permute-done((f32[144,128]{1,0:T(8,128)S(1)}, f32[144,128]{1,0:T(8,128)S(1)}, u32[]{:S(2)}, u32[]{:S(2)}) %collective-permute-start.24) | collective-permute-done | bytes 73760 | tf_op jit(solution)/shard_map/ppermute | solution.py:416
  62.4 5.0 %collective-permute-done.27.refs_1_ = f32[144,128]{1,0:T(8,128)S(1)} collective-permute-done((f32[144,128]{1,0:T(8,128)S(1)}, f32[144,128]{1,0:T(8,128)S(1)}, u32[]{:S(2)}, u32[]{:S(2)}) %collective-permute-start.27) | collective-permute-done | bytes 73760 | tf_op jit(solution)/shard_map/ppermute | solution.py:483
  71.0 1.6 %collective-permute-start.32 = (f32[32,4,128]{2,1,0:T(4,128)S(1)}, f32[32,4,128]{2,1,0:T(4,128)S(1)}, u32[]{:S(2)}, u32[]{:S(2)}) collective-permute-start(f32[32,4,128]{2,1,0:T(4,128)S(1)} %get-tuple-element.137), channel_id=1, source_target_pairs={{0,16},{8,24},{16,0},{24,8},{1,17},{9,25},{17,1},{25,9},{2,18},{10... | collective-permute-start | bytes 196616 | tf_op jit(solution)/shard_map/ppermute | solution.py:416
  75.2 2.5 %collective-permute-done.33.refs_3_ = f32[32,4,128]{2,1,0:T(4,128)S(1)} collective-permute-done((f32[32,4,128]{2,1,0:T(4,128)S(1)}, f32[32,4,128]{2,1,0:T(4,128)S(1)}, u32[]{:S(2)}, u32[]{:S(2)}) %collective-permute-start.33) | collective-permute-done | bytes 65568 | tf_op jit(solution)/shard_map/ppermute | solution.py:416
  (47 shorter events, 17.6 us)
Async XLA Ops:
  5.6 17.7 %collective-permute-start.6 = (bf16[6,128,128]{2,1,0:T(8,128)(2,1)S(1)}, bf16[6,128,128]{2,1,0:T(8,128)(2,1)S(1)}, u32[]{:S(2)}, u32[]{:S(2)}) collective-permute-start(bf16[6,128,128]{2,1,0:T(8,128)(2,1)S(1)} %get-tuple-element.91), channel_id=1, source_target_pairs={{0,8},{8,0},{16,24},{24,16},{1,9},{9,1},{17,25},{25,17},{2,10},{10... | collective-permute-start | bytes 589832 | tf_op jit(solution)/shard_map/ppermute | solution.py:416
  8.6 14.7 %collective-permute-start.7 = (bf16[6,128,128]{2,1,0:T(8,128)(2,1)S(1)}, bf16[6,128,128]{2,1,0:T(8,128)(2,1)S(1)}, u32[]{:S(2)}, u32[]{:S(2)}) collective-permute-start(bf16[6,128,128]{2,1,0:T(8,128)(2,1)S(1)} %get-tuple-element.92), channel_id=1, source_target_pairs={{0,16},{8,24},{16,0},{24,8},{1,17},{9,25},{17,1},{25,9},{2,18},{10... | collective-permute-start | bytes 589832 | tf_op jit(solution)/shard_map/ppermute | solution.py:416
  10.2 13.1 %collective-permute-start.8 = (bf16[6,128,128]{2,1,0:T(8,128)(2,1)S(1)}, bf16[6,128,128]{2,1,0:T(8,128)(2,1)S(1)}, u32[]{:S(2)}, u32[]{:S(2)}) collective-permute-start(bf16[6,128,128]{2,1,0:T(8,128)(2,1)S(1)} %get-tuple-element.93), channel_id=1, source_target_pairs={{0,24},{8,16},{16,8},{24,0},{1,25},{9,17},{17,9},{25,1},{2,26},{10... | collective-permute-start | bytes 589832 | tf_op jit(solution)/shard_map/ppermute | solution.py:416
  10.3 7.0 %collective-permute-start.9 = (f32[34,4,128]{2,1,0:T(4,128)S(1)}, f32[34,4,128]{2,1,0:T(4,128)S(1)}, u32[]{:S(2)}, u32[]{:S(2)}) collective-permute-start(f32[34,4,128]{2,1,0:T(4,128)S(1)} %get-tuple-element.105), channel_id=1, source_target_pairs={{0,8},{8,0},{16,24},{24,16},{1,9},{9,1},{17,25},{25,17},{2,10},{10... | collective-permute-start | bytes 208904 | tf_op jit(solution)/shard_map/ppermute | solution.py:416
  12.1 8.1 %collective-permute-start.10 = (f32[34,4,128]{2,1,0:T(4,128)S(1)}, f32[34,4,128]{2,1,0:T(4,128)S(1)}, u32[]{:S(2)}, u32[]{:S(2)}) collective-permute-start(f32[34,4,128]{2,1,0:T(4,128)S(1)} %get-tuple-element.106), channel_id=1, source_target_pairs={{0,16},{8,24},{16,0},{24,8},{1,17},{9,25},{17,1},{25,9},{2,18},{10... | collective-permute-start | bytes 208904 | tf_op jit(solution)/shard_map/ppermute | solution.py:416
  17.3 6.0 %collective-permute-start.11 = (f32[34,4,128]{2,1,0:T(4,128)S(1)}, f32[34,4,128]{2,1,0:T(4,128)S(1)}, u32[]{:S(2)}, u32[]{:S(2)}) collective-permute-start(f32[34,4,128]{2,1,0:T(4,128)S(1)} %get-tuple-element.107), channel_id=1, source_target_pairs={{0,24},{8,16},{16,8},{24,0},{1,25},{9,17},{17,9},{25,1},{2,26},{10... | collective-permute-start | bytes 208904 | tf_op jit(solution)/shard_map/ppermute | solution.py:416
  25.3 7.1 %collective-permute-start.14 = (f32[144,128]{1,0:T(8,128)S(1)}, f32[144,128]{1,0:T(8,128)S(1)}, u32[]{:S(2)}, u32[]{:S(2)}) collective-permute-start(f32[144,128]{1,0:T(8,128)S(1)} %get-tuple-element.109.refs_0_), channel_id=1, source_target_pairs={{0,24},{8,16},{16,8},{24,0},{1,25},{9,17},{17,9},{25,1},{2,26},{10... | collective-permute-start | bytes 221192 | tf_op jit(solution)/shard_map/ppermute | solution.py:416
  28.4 5.3 %collective-permute-start.13 = (f32[144,128]{1,0:T(8,128)S(1)}, f32[144,128]{1,0:T(8,128)S(1)}, u32[]{:S(2)}, u32[]{:S(2)}) collective-permute-start(f32[144,128]{1,0:T(8,128)S(1)} %get-tuple-element.109.refs_0_), channel_id=1, source_target_pairs={{0,16},{8,24},{16,0},{24,8},{1,17},{9,25},{17,1},{25,9},{2,18},{10... | collective-permute-start | bytes 221192 | tf_op jit(solution)/shard_map/ppermute | solution.py:416
  28.4 5.3 %collective-permute-start.12 = (f32[144,128]{1,0:T(8,128)S(1)}, f32[144,128]{1,0:T(8,128)S(1)}, u32[]{:S(2)}, u32[]{:S(2)}) collective-permute-start(f32[144,128]{1,0:T(8,128)S(1)} %get-tuple-element.109.refs_0_), channel_id=1, source_target_pairs={{0,8},{8,0},{16,24},{24,16},{1,9},{9,1},{17,25},{25,17},{2,10},{10... | collective-permute-start | bytes 221192 | tf_op jit(solution)/shard_map/ppermute | solution.py:416
  29.1 18.5 %collective-permute-start.20 = (bf16[6,128,128]{2,1,0:T(8,128)(2,1)S(1)}, bf16[6,128,128]{2,1,0:T(8,128)(2,1)S(1)}, u32[]{:S(2)}, u32[]{:S(2)}) collective-permute-start(bf16[6,128,128]{2,1,0:T(8,128)(2,1)S(1)} %get-tuple-element.118), channel_id=1, source_target_pairs={{0,8},{8,0},{16,24},{24,16},{1,9},{9,1},{17,25},{25,17},{2,10},{10... | collective-permute-start | bytes 589832 | tf_op jit(solution)/shard_map/ppermute | solution.py:416
  30.4 17.2 %collective-permute-start.21 = (bf16[6,128,128]{2,1,0:T(8,128)(2,1)S(1)}, bf16[6,128,128]{2,1,0:T(8,128)(2,1)S(1)}, u32[]{:S(2)}, u32[]{:S(2)}) collective-permute-start(bf16[6,128,128]{2,1,0:T(8,128)(2,1)S(1)} %get-tuple-element.119), channel_id=1, source_target_pairs={{0,16},{8,24},{16,0},{24,8},{1,17},{9,25},{17,1},{25,9},{2,18},{10... | collective-permute-start | bytes 589832 | tf_op jit(solution)/shard_map/ppermute | solution.py:416
  32.5 15.2 %collective-permute-start.22 = (bf16[6,128,128]{2,1,0:T(8,128)(2,1)S(1)}, bf16[6,128,128]{2,1,0:T(8,128)(2,1)S(1)}, u32[]{:S(2)}, u32[]{:S(2)}) collective-permute-start(bf16[6,128,128]{2,1,0:T(8,128)(2,1)S(1)} %get-tuple-element.120), channel_id=1, source_target_pairs={{0,24},{8,16},{16,8},{24,0},{1,25},{9,17},{17,9},{25,1},{2,26},{10... | collective-permute-start | bytes 589832 | tf_op jit(solution)/shard_map/ppermute | solution.py:416
  34.2 5.9 %collective-permute-start.15 = (f32[144,128]{1,0:T(8,128)S(1)}, f32[144,128]{1,0:T(8,128)S(1)}, u32[]{:S(2)}, u32[]{:S(2)}) collective-permute-start(f32[144,128]{1,0:T(8,128)S(1)} %get-tuple-element.110.own_ref), channel_id=1, source_target_pairs={{0,1},{1,0},{2,3},{3,2},{4,5},{5,4},{6,7},{7,6},{8,9},{9,8},{10,11... | collective-permute-start | bytes 221192 | tf_op jit(solution)/shard_map/ppermute | solution.py:416
  40.4 6.0 %collective-permute-start.16 = (f32[144,128]{1,0:T(8,128)S(1)}, f32[144,128]{1,0:T(8,128)S(1)}, u32[]{:S(2)}, u32[]{:S(2)}) collective-permute-start(f32[144,128]{1,0:T(8,128)S(1)} %get-tuple-element.113), channel_id=1, source_target_pairs={{0,2},{1,5},{2,0},{3,7},{4,6},{5,1},{6,4},{7,3},{8,10},{9,13},{10,... | collective-permute-start | bytes 221192 | tf_op jit(solution)/shard_map/ppermute | solution.py:483
  40.5 6.6 %collective-permute-start.18 = (f32[72,128]{1,0:T(8,128)S(1)}, f32[72,128]{1,0:T(8,128)S(1)}, u32[]{:S(2)}, u32[]{:S(2)}) collective-permute-start(f32[72,128]{1,0:T(8,128)S(1)} %get-tuple-element.114), channel_id=1, source_target_pairs={{0,6},{1,7},{2,4},{3,5},{4,2},{5,3},{6,0},{7,1},{8,14},{9,15},{10,... | collective-permute-start | bytes 110600 | tf_op jit(solution)/shard_map/ppermute | solution.py:416
  46.4 2.7 %collective-permute-start.17 = (f32[144,128]{1,0:T(8,128)S(1)}, f32[144,128]{1,0:T(8,128)S(1)}, u32[]{:S(2)}, u32[]{:S(2)}) collective-permute-start(f32[144,128]{1,0:T(8,128)S(1)} %collective-permute-done.16.refs_1_), channel_id=1, source_target_pairs={{0,1},{1,0},{2,3},{3,2},{4,5},{5,4},{6,7},{7,6},{8,9},{9,8},{10,11... | collective-permute-start | bytes 221192 | tf_op jit(solution)/shard_map/ppermute | solution.py:416
  52.3 5.4 %collective-permute-start.25 = (f32[144,128]{1,0:T(8,128)S(1)}, f32[144,128]{1,0:T(8,128)S(1)}, u32[]{:S(2)}, u32[]{:S(2)}) collective-permute-start(f32[144,128]{1,0:T(8,128)S(1)} %get-tuple-element.126.refs_0_), channel_id=1, source_target_pairs={{0,24},{8,16},{16,8},{24,0},{1,25},{9,17},{17,9},{25,1},{2,26},{10... | collective-permute-start | bytes 221192 | tf_op jit(solution)/shard_map/ppermute | solution.py:416
  54.5 4.6 %collective-permute-start.24 = (f32[144,128]{1,0:T(8,128)S(1)}, f32[144,128]{1,0:T(8,128)S(1)}, u32[]{:S(2)}, u32[]{:S(2)}) collective-permute-start(f32[144,128]{1,0:T(8,128)S(1)} %get-tuple-element.126.refs_0_), channel_id=1, source_target_pairs={{0,16},{8,24},{16,0},{24,8},{1,17},{9,25},{17,1},{25,9},{2,18},{10... | collective-permute-start | bytes 221192 | tf_op jit(solution)/shard_map/ppermute | solution.py:416
  54.9 4.4 %collective-permute-start.23 = (f32[144,128]{1,0:T(8,128)S(1)}, f32[144,128]{1,0:T(8,128)S(1)}, u32[]{:S(2)}, u32[]{:S(2)}) collective-permute-start(f32[144,128]{1,0:T(8,128)S(1)} %get-tuple-element.126.refs_0_), channel_id=1, source_target_pairs={{0,8},{8,0},{16,24},{24,16},{1,9},{9,1},{17,25},{25,17},{2,10},{10... | collective-permute-start | bytes 221192 | tf_op jit(solution)/shard_map/ppermute | solution.py:416
  61.4 6.0 %collective-permute-start.27 = (f32[144,128]{1,0:T(8,128)S(1)}, f32[144,128]{1,0:T(8,128)S(1)}, u32[]{:S(2)}, u32[]{:S(2)}) collective-permute-start(f32[144,128]{1,0:T(8,128)S(1)} %get-tuple-element.130), channel_id=1, source_target_pairs={{0,2},{1,5},{2,0},{3,7},{4,6},{5,1},{6,4},{7,3},{8,10},{9,13},{10,... | collective-permute-start | bytes 221192 | tf_op jit(solution)/shard_map/ppermute | solution.py:483
  61.6 5.8 %collective-permute-start.29 = (f32[72,128]{1,0:T(8,128)S(1)}, f32[72,128]{1,0:T(8,128)S(1)}, u32[]{:S(2)}, u32[]{:S(2)}) collective-permute-start(f32[72,128]{1,0:T(8,128)S(1)} %get-tuple-element.131), channel_id=1, source_target_pairs={{0,6},{1,7},{2,4},{3,5},{4,2},{5,3},{6,0},{7,1},{8,14},{9,15},{10,... | collective-permute-start | bytes 110600 | tf_op jit(solution)/shard_map/ppermute | solution.py:416
  69.9 4.4 %collective-permute-start.31 = (f32[32,4,128]{2,1,0:T(4,128)S(1)}, f32[32,4,128]{2,1,0:T(4,128)S(1)}, u32[]{:S(2)}, u32[]{:S(2)}) collective-permute-start(f32[32,4,128]{2,1,0:T(4,128)S(1)} %get-tuple-element.136), channel_id=1, source_target_pairs={{0,8},{8,0},{16,24},{24,16},{1,9},{9,1},{17,25},{25,17},{2,10},{10... | collective-permute-start | bytes 196616 | tf_op jit(solution)/shard_map/ppermute | solution.py:416
  71.0 4.3 %collective-permute-start.32 = (f32[32,4,128]{2,1,0:T(4,128)S(1)}, f32[32,4,128]{2,1,0:T(4,128)S(1)}, u32[]{:S(2)}, u32[]{:S(2)}) collective-permute-start(f32[32,4,128]{2,1,0:T(4,128)S(1)} %get-tuple-element.137), channel_id=1, source_target_pairs={{0,16},{8,24},{16,0},{24,8},{1,17},{9,25},{17,1},{25,9},{2,18},{10... | collective-permute-start | bytes 196616 | tf_op jit(solution)/shard_map/ppermute | solution.py:416
  72.6 5.2 %collective-permute-start.33 = (f32[32,4,128]{2,1,0:T(4,128)S(1)}, f32[32,4,128]{2,1,0:T(4,128)S(1)}, u32[]{:S(2)}, u32[]{:S(2)}) collective-permute-start(f32[32,4,128]{2,1,0:T(4,128)S(1)} %get-tuple-element.138), channel_id=1, source_target_pairs={{0,24},{8,16},{16,8},{24,0},{1,25},{9,17},{17,9},{25,1},{2,26},{10... | collective-permute-start | bytes 196616 | tf_op jit(solution)/shard_map/ppermute | solution.py:416
  (4 other events, 6.1 us)
